TPU v7x, 128 devices: a whole 4x4x4 slice. The times are simulated.
128 devices in a mesh: lat: 16 (over x, z), wave: 8 (over y, core).
Axes of the slice: x: 4, y: 4, z: 4, core: 2. Of those that a mesh axis runs over, the one named last changes fastest.
Arguments:
- fourier: bfloat16 [2, 2000, 64, 256], P(None, 'lat', None, 'wave'), may hold values from -6 to 6
- table: bfloat16 [64, 2000, 4000], P('wave', 'lat'), may hold values from -0.125 to 0.125
- wavenums: int32 [64], P('wave'), may hold values from 0 to 3999, as said below
Outputs:
- spectra: float32 [4000, 64, 256], P('lat', 'wave')
Inputs may be any that keep to these rules, and one draw needn't show every extreme that they name: `wavenums`: the entries are distinct and include 0 and 3999; with G = 8 groups, entry g * 8 + k is the (k * G + g)-th smallest (counting from 0).
All inputs are finite; a program needn't handle non-finite values.
Results may differ from a plain program's by a relative error of at most 0.0003.
Values may be sent and summed in bfloat16 or wider, within the bound.
No kernel may reach another device: no remote copies, remote signals or barrier semaphores. Data moves between devices by JAX's collectives and lax.ppermute only.
A program may use at most 256 MiB of HBM per device.

v0:
```python
import functools

import jax
import jax.numpy as jnp
from jax import lax
from jax.experimental import pallas as pl
from jax.experimental.layout import Layout, with_layout_constraint
from jax.experimental.pallas import tpu as pltpu
from jax.sharding import PartitionSpec as P


ROWS = 256
LANES = 256
HALF = 128
TILE = 128
TILES = 3
TAIL = 16
SIDE = 4
PAIR = 2
GROUPS = 4
TOP = 32766.0
STEP = 64.0


def own_part(four_ref, slot, tiles, row, first, mval):
    tab = jnp.concatenate([tile[row] for tile in tiles], axis=1).astype(jnp.float32)
    shift = first & (TILE - 1)
    tab = pltpu.roll(tab, TILES * TILE - shift, 1)[:, :LANES]
    tab = jnp.concatenate([tab, jnp.zeros((HALF - tab.shape[0], LANES), tab.dtype)], axis=0)
    offset = lax.broadcasted_iota(jnp.int32, (1, LANES), 1) + first - mval
    keep = jnp.where(offset >= 0, 1.0, 0.0)
    sign = jnp.where((offset & 1) == 0, keep, -keep)
    tab = jnp.concatenate([(tab * keep).astype(jnp.bfloat16), (tab * sign).astype(jnp.bfloat16)], axis=0)
    north = four_ref[:, slot, 0].reshape(ROWS, HALF)
    south = four_ref[:, slot, 1].reshape(ROWS, HALF)
    return jnp.dot(north, tab[:HALF], preferred_element_type=jnp.float32) + jnp.dot(
        south, tab[HALF:], preferred_element_type=jnp.float32
    )


def decoded(codes, tail, row):
    at = lax.broadcasted_iota(jnp.int32, (TAIL, LANES), 0) == row
    code = jnp.sum(jnp.where(at, tail.astype(jnp.float32), 0.0), axis=0, keepdims=True)
    scale = jnp.exp2(code * (1.0 / STEP)) * (1.0 / TOP)
    return codes.astype(jnp.float32) * scale


def encode(value):
    most = jnp.maximum(jnp.max(jnp.abs(value), axis=0, keepdims=True), 1e-30)
    code = jnp.ceil(jnp.log2(most) * STEP) + 1.0
    inverse = jnp.exp2(code * (-1.0 / STEP)) * TOP
    return jnp.round(value * inverse).astype(jnp.int32).astype(jnp.int16), code


def rows_at(at):
    return pl.ds(at * ROWS if isinstance(at, int) else pl.multiple_of(at * ROWS, ROWS), ROWS)


def store_coded(out_ref, blocks, value, loop):
    row = lax.broadcasted_iota(jnp.int32, (TAIL, LANES), 0)

    def one(slot, tail):
        for b in range(blocks):
            at = slot * blocks + b
            codes, code = encode(value(slot, b))
            out_ref[rows_at(at)] = codes
            tail = jnp.where(row == at, code, tail)
        return tail

    tail = jnp.zeros((TAIL, LANES), jnp.float32)
    if loop:
        tail = lax.fori_loop(0, PAIR, one, tail)
    else:
        for slot in range(PAIR):
            tail = one(slot, tail)
    out_ref[PAIR * blocks * ROWS :] = tail.astype(jnp.int32).astype(jnp.int16)


def chunk_at(at, axis, ahead):
    return (at[axis] + ahead) & (SIDE - 1)


def block_at(at, axis, ahead, b):
    chunk = chunk_at(at, axis, ahead)
    other = at[1 - axis] if b is None else b
    return chunk * SIDE + other if axis == 0 else other * SIDE + chunk


def tile_specs(slots, rows, width, group, blocks):
    specs = []
    for block in blocks:
        for t in range(TILES):

            def index(i, at, block=block, t=t):
                return group, 0, block(at) * width // TILE + t

            specs.append(pl.BlockSpec((slots, rows, TILE), index))
    return specs


def first_kernel(at_ref, four_ref, *rest, axis, ahead, group, width, terms):
    out_ref = rest[-1]
    tiles, states = rest[: SIDE * TILES], rest[SIDE * TILES : SIDE * TILES + terms]

    def value(slot, b):
        first = block_at(at_ref, axis, ahead, b) * width
        mval = at_ref[2 + group * PAIR + slot]
        total = own_part(four_ref, slot, tiles[b * TILES : (b + 1) * TILES], slot, first, mval)
        at = slot * SIDE + b
        for state in states:
            total = total + decoded(rows_of(state, at), state[PAIR * SIDE * ROWS :], at)
        return total

    store_coded(out_ref, SIDE, value, True)


def rows_of(ref, at):
    return ref[rows_at(at)]


def summed(at_ref, four_ref, place, slot, mval, refs, axis, ahead, width):
    first = block_at(at_ref, axis, ahead, None) * width
    total = own_part(four_ref, place, refs[:TILES], slot, first, mval)
    refs = refs[TILES:]
    for _ in range(2):
        total = total + decoded(refs[slot][...], refs[PAIR][...], slot * SIDE + chunk_at(at_ref, axis, ahead))
        refs = refs[PAIR + 1 :]
    for state in refs:
        total = total + decoded(rows_of(state, slot), state[PAIR * ROWS :], slot)
    return total


def second_kernel(at_ref, four_ref, *rest, axis, aheads, width, terms):
    per = TILES + 2 * (PAIR + 1) + terms
    for pair, ahead in enumerate(aheads):
        refs = rest[pair * per : (pair + 1) * per]

        def value(slot, b):
            at = pair * PAIR + slot
            mval = at_ref[2 + (1 - axis) * 2 * PAIR + at]
            return summed(at_ref, four_ref, at, slot, mval, refs, axis, ahead, width)

        store_coded(rest[pair - 2], 1, value, False)


def last_kernel(at_ref, four_ref, *rest, width):
    out_ref = rest[-1]
    per = TILES + 2 * (PAIR + 1) + 2
    for group in range(GROUPS):
        refs = rest[group * per : (group + 1) * per]
        for slot in range(PAIR):
            k = group * PAIR + slot
            total = summed(at_ref, four_ref, k, slot, at_ref[2 + k], refs, 1 - group // 2, 0, width)
            out_ref[:, k, :] = total.T[:width]


def whole(array):
    return pl.BlockSpec(array.shape, lambda i, at: (0,) * array.ndim)


def four_of(slots, index):
    return pl.BlockSpec((8, slots, 2, 32, HALF), lambda i, at: (0, index, 0, 0, 0))


def second_operands(group, axis, ahead, tab, firsts, states, width):
    blocks = [functools.partial(block_at, axis=axis, ahead=ahead, b=None)]
    tab = tab[group // 2]
    specs = tile_specs(PAIR, tab.shape[1], width, group % 2, blocks)
    operands = [tab] * TILES
    for first in firsts:
        for slot in range(PAIR):
            specs.append(pl.BlockSpec((ROWS, LANES), lambda i, at, s=slot: (s * SIDE + chunk_at(at, axis, ahead), 0)))
        specs.append(pl.BlockSpec((TAIL, LANES), lambda i, at: (PAIR * SIDE * ROWS // TAIL, 0)))
        operands += [first] * (PAIR + 1)
    return specs + [whole(state) for state in states], operands + list(states)


def call(body, at, operands, in_specs, out_shapes, limit=10):
    outs = [jax.ShapeDtypeStruct(shape, dtype) for shape, dtype in out_shapes]
    return pl.pallas_call(
        body,
        grid_spec=pltpu.PrefetchScalarGridSpec(
            num_scalar_prefetch=1, grid=(1,), in_specs=in_specs, out_specs=[whole(out) for out in outs]
        ),
        out_shape=outs,
        compiler_params=pltpu.CompilerParams(vmem_limit_bytes=limit << 20),
    )(at, *operands)


def first_hop(group, ahead, at, four, tab, states, width):
    axis = group // 2
    tab = tab[axis]
    blocks = [functools.partial(block_at, axis=axis, ahead=ahead, b=b) for b in range(SIDE)]
    specs = [four_of(PAIR, group)] + tile_specs(PAIR, tab.shape[1], width, group % 2, blocks)
    specs += [whole(state) for state in states]
    operands = [four] + [tab] * (SIDE * TILES) + list(states)
    body = functools.partial(
        first_kernel, axis=axis, ahead=ahead, group=group, width=width, terms=len(states)
    )
    out = ((PAIR * SIDE * ROWS + TAIL, LANES), jnp.int16)
    return call(body, at, operands, specs, [out])[0]


def second_hop(start, aheads, at, four, tab, firsts, states, width):
    axis = 1 - start // 2
    specs, operands = [four_of(2 * PAIR, start // 2)], [four]
    for pair, ahead in enumerate(aheads):
        more, arrays = second_operands(start + pair, axis, ahead, tab, firsts[pair], states[pair], width)
        specs, operands = specs + more, operands + arrays
    body = functools.partial(second_kernel, axis=axis, aheads=aheads, width=width, terms=len(states[0]))
    return call(body, at, operands, specs, [((PAIR * ROWS + TAIL, LANES), jnp.int16)] * 2)


def last(at, four, tab, firsts, states, width):
    specs, operands = [whole(four)], [four]
    for group in range(GROUPS):
        more, arrays = second_operands(group, 1 - group // 2, 0, tab, firsts[group], states[group], width)
        specs, operands = specs + more, operands + arrays
    out = ((width, GROUPS * PAIR, ROWS), jnp.float32)
    return call(functools.partial(last_kernel, width=width), at, operands, specs, [out], 24)[0]


def ring(axis, sign):
    pairs = []
    for x in range(SIDE):
        for z in range(SIDE):
            to = ((x + sign) % SIDE, z) if axis == 0 else (x, (z + sign) % SIDE)
            pairs.append((x * SIDE + z, to[0] * SIDE + to[1]))
    return pairs


def per_device(fourier, table, wavenums):
    slots, rows, degrees = table.shape
    lat = lax.axis_size("lat")
    width = degrees // lat
    me = lax.axis_index("lat")

    split = fourier.transpose(2, 0, 3, 1)
    split = jnp.pad(split, ((0, 0), (0, 0), (0, 0), (0, HALF - rows)))
    split = split.reshape(8, slots, 2, split.shape[2], HALF)
    four = lax.all_to_all(split, "wave", split_axis=0, concat_axis=0, tiled=True)
    at = jnp.concatenate([jnp.stack([me // SIDE, me % SIDE]).astype(jnp.int32), wavenums])
    table = lax.optimization_barrier(with_layout_constraint(table, Layout((0, 1, 2))))
    table = (table[: 2 * PAIR], table[2 * PAIR :])

    def send(array, axis, sign):
        return lax.ppermute(array, "lat", ring(axis, sign))

    def first(group, ahead, states):
        return first_hop(group, ahead, at, four, table, states, width)

    def second(start, aheads, firsts, states):
        return second_hop(start, aheads, at, four, table, firsts, states, width)

    ways = [1 - 2 * (group % 2) for group in range(GROUPS)]
    every = range(GROUPS)
    far = [first(g, 2, []) for g in every]
    got_far = [send(far[g], g // 2, ways[g]) for g in every]
    near = [first(g, -ways[g], []) for g in every]
    got_near = [send(near[g], g // 2, -ways[g]) for g in every]
    both = [first(g, ways[g], [got_far[g]]) for g in every]
    got_both = [send(both[g], g // 2, ways[g]) for g in every]
    firsts = list(zip(got_near, got_both))

    halves = [(0, 1), (2, 3)]
    of = [(firsts[p], firsts[q]) for p, q in halves]
    far = [second(2 * h, (2, 2), of[h], ((), ())) for h in range(2)]
    got_far = [send(far[g // 2][g % 2], 1 - g // 2, ways[g]) for g in every]
    near = [second(2 * h, (-1, 1), of[h], ((), ())) for h in range(2)]
    got_near = [send(near[g // 2][g % 2], 1 - g // 2, -ways[g]) for g in every]
    both = [second(2 * h, (1, -1), of[h], ((got_far[p],), (got_far[q],))) for h, (p, q) in enumerate(halves)]
    got_both = [send(both[g // 2][g % 2], 1 - g // 2, ways[g]) for g in every]
    return last(at, four, table, firsts, list(zip(got_near, got_both)), width)


def solution(mesh):
    placed = (P(None, "lat", None, "wave"), P("wave", "lat", None), P("wave"))
    return jax.shard_map(
        per_device, mesh=mesh, in_specs=placed, out_specs=P("lat", "wave", None), check_vma=False
    )
```

profile of v0, /device:TPU:6, one launch (start us, length us, event | category | flops | bytes accessed | tf_op | source)
XLA Modules:
  0.0 164.7 jit_solution(9047452832912926938)
XLA Ops:
  0.0 1.4 copy.6
  1.4 1.3 pad.4.clone
  2.7 4.5 %all-to-all-start = ((bf16[8,8,2,32,128]{4,3,2,1,0:T(8,128)(2,1)}), bf16[8,8,2,32,128]{4,3,2,1,0:T(8,128)(2,1)S(1)}, u32[]{:S(2)}, u32[]{:S(2)}) async-start(bf16[8,8,2,32,128]{4,3,2,1,0:T(8,128)(2,1)} %bitcast.3), calls=%async_computation | async-start | bytes 2097152 | tf_op jit(solution)/shard_map/all_to_all | solution.py:241
  7.2 11.1 %copy.5 = bf16[8,125,4000]{2,1,0:T(8,128)(2,1)} copy(bf16[8,125,4000]{2,0,1:T(8,128)(2,1)} %param.4) | data formatting | bytes 16000000 | tf_op args[1]
  18.3 6.0 %fusion = (bf16[4,125,4000]{2,1,0:T(8,128)(2,1)}, bf16[4,125,4000]{2,1,0:T(8,128)(2,1)}) fusion(bf16[8,125,4000]{2,1,0:T(8,128)(2,1)} %copy.5), kind=kLoop, calls=%fused_computation.1 | loop fusion | bytes 16000000 | tf_op jit(solution)/shard_map/slice | solution.py:244
  24.3 2.2 %copy-done.1 = bf16[4,125,4000]{2,1,0:T(8,128)(2,1)S(1)} copy-done((bf16[4,125,4000]{2,1,0:T(8,128)(2,1)S(1)}, bf16[4,125,4000]{2,1,0:T(8,128)(2,1)}, u32[]{:S(2)}) %copy-start.1) | copy-done | bytes 4000024
  26.5 2.0 %shard_map.38 = s16[2064,256]{1,0:T(8,128)(2,1)S(1)} custom-call(s32[10]{0:T(128)S(1)} %pad_add_fusion.at_ref, bf16[8,8,2,32,128]{4,3,2,1,0:T(8,128)(2,1)S(1)} %all-to-all-done.four_ref, bf16[4,125,4000]{2,1,0:T(8,128)(2,1)S(1)} %copy-done.1, bf16[4,125,4000]{2,1,0:T(8,128)(2,1)S(1)} %copy-done.1, bf16[4,125,4000]{2,1,0:T(8,128)(2,1)S(1)} %copy-done.1, ...), custom_call_target="tpu_custom_call" | custom-call | tf_op jit(solution)/shard_map/pallas_call | solution.py:180
  29.1 2.0 %shard_map.41 = s16[2064,256]{1,0:T(8,128)(2,1)S(1)} custom-call(s32[10]{0:T(128)S(1)} %pad_add_fusion.at_ref, bf16[8,8,2,32,128]{4,3,2,1,0:T(8,128)(2,1)S(1)} %all-to-all-done.four_ref, bf16[4,125,4000]{2,1,0:T(8,128)(2,1)S(1)} %copy-done.1, bf16[4,125,4000]{2,1,0:T(8,128)(2,1)S(1)} %copy-done.1, bf16[4,125,4000]{2,1,0:T(8,128)(2,1)S(1)} %copy-done.1, ...), custom_call_target="tpu_custom_call" | custom-call | tf_op jit(solution)/shard_map/pallas_call | solution.py:180
  31.0 1.6 collective-permute-start.4
  32.7 2.0 %shard_map.47 = s16[2064,256]{1,0:T(8,128)(2,1)S(1)} custom-call(s32[10]{0:T(128)S(1)} %pad_add_fusion.at_ref, bf16[8,8,2,32,128]{4,3,2,1,0:T(8,128)(2,1)S(1)} %all-to-all-done.four_ref, bf16[4,125,4000]{2,1,0:T(8,128)(2,1)S(1)} %copy-done, bf16[4,125,4000]{2,1,0:T(8,128)(2,1)S(1)} %copy-done, bf16[4,125,4000]{2,1,0:T(8,128)(2,1)S(1)} %copy-done, ...), custom_call_target="tpu_custom_call" | custom-call | tf_op jit(solution)/shard_map/pallas_call | solution.py:180
  34.7 2.0 %collective-permute-start.13 = (s16[2064,256]{1,0:T(8,128)(2,1)S(1)}, s16[2064,256]{1,0:T(8,128)(2,1)S(1)}, u32[]{:S(2)}, u32[]{:S(2)}) collective-permute-start(s16[2064,256]{1,0:T(8,128)(2,1)S(1)} %shard_map.47), channel_id=1, source_target_pairs={{0,8},{8,16},{16,24},{24,0},{32,40},{40,48},{48,56},{56,32},{64,72... | collective-permute-start | bytes 3170312 | tf_op jit(solution)/shard_map/ppermute | solution.py:247
  36.6 2.0 %shard_map.50 = s16[2064,256]{1,0:T(8,128)(2,1)S(1)} custom-call(s32[10]{0:T(128)S(1)} %pad_add_fusion.at_ref, bf16[8,8,2,32,128]{4,3,2,1,0:T(8,128)(2,1)S(1)} %all-to-all-done.four_ref, bf16[4,125,4000]{2,1,0:T(8,128)(2,1)S(1)} %copy-done, bf16[4,125,4000]{2,1,0:T(8,128)(2,1)S(1)} %copy-done, bf16[4,125,4000]{2,1,0:T(8,128)(2,1)S(1)} %copy-done, ...), custom_call_target="tpu_custom_call" | custom-call | tf_op jit(solution)/shard_map/pallas_call | solution.py:180
  38.6 2.2 %collective-permute-start.16 = (s16[2064,256]{1,0:T(8,128)(2,1)S(1)}, s16[2064,256]{1,0:T(8,128)(2,1)S(1)}, u32[]{:S(2)}, u32[]{:S(2)}) collective-permute-start(s16[2064,256]{1,0:T(8,128)(2,1)S(1)} %shard_map.50), channel_id=1, source_target_pairs={{0,24},{8,0},{16,8},{24,16},{32,56},{40,32},{48,40},{56,48},{64,88... | collective-permute-start | bytes 3170312 | tf_op jit(solution)/shard_map/ppermute | solution.py:247
  40.8 2.0 %shard_map.37 = s16[2064,256]{1,0:T(8,128)(2,1)S(1)} custom-call(s32[10]{0:T(128)S(1)} %pad_add_fusion.at_ref, bf16[8,8,2,32,128]{4,3,2,1,0:T(8,128)(2,1)S(1)} %all-to-all-done.four_ref, bf16[4,125,4000]{2,1,0:T(8,128)(2,1)S(1)} %copy-done.1, bf16[4,125,4000]{2,1,0:T(8,128)(2,1)S(1)} %copy-done.1, bf16[4,125,4000]{2,1,0:T(8,128)(2,1)S(1)} %copy-done.1, ...), custom_call_target="tpu_custom_call" | custom-call | tf_op jit(solution)/shard_map/pallas_call | solution.py:180
  42.8 1.1 collective-permute-start
  43.9 2.0 %shard_map.40 = s16[2064,256]{1,0:T(8,128)(2,1)S(1)} custom-call(s32[10]{0:T(128)S(1)} %pad_add_fusion.at_ref, bf16[8,8,2,32,128]{4,3,2,1,0:T(8,128)(2,1)S(1)} %all-to-all-done.four_ref, bf16[4,125,4000]{2,1,0:T(8,128)(2,1)S(1)} %copy-done.1, bf16[4,125,4000]{2,1,0:T(8,128)(2,1)S(1)} %copy-done.1, bf16[4,125,4000]{2,1,0:T(8,128)(2,1)S(1)} %copy-done.1, ...), custom_call_target="tpu_custom_call" | custom-call | tf_op jit(solution)/shard_map/pallas_call | solution.py:180
  45.9 8.4 %collective-permute-done.1.rest_12_ = s16[2064,256]{1,0:T(8,128)(2,1)S(1)} collective-permute-done((s16[2064,256]{1,0:T(8,128)(2,1)S(1)}, s16[2064,256]{1,0:T(8,128)(2,1)S(1)}, u32[]{:S(2)}, u32[]{:S(2)}) %collective-permute-start.1) | collective-permute-done | bytes 1056800 | tf_op jit(solution)/shard_map/ppermute | solution.py:247
  54.3 1.7 %collective-permute-start.3 = (s16[2064,256]{1,0:T(8,128)(2,1)S(1)}, s16[2064,256]{1,0:T(8,128)(2,1)S(1)}, u32[]{:S(2)}, u32[]{:S(2)}) collective-permute-start(s16[2064,256]{1,0:T(8,128)(2,1)S(1)} %shard_map.40), channel_id=1, source_target_pairs={{0,32},{8,40},{16,48},{24,56},{32,64},{40,72},{48,80},{56,88},{64,... | collective-permute-start | bytes 3170312 | tf_op jit(solution)/shard_map/ppermute | solution.py:247
  56.0 2.1 %shard_map.39 = s16[2064,256]{1,0:T(8,128)(2,1)S(1)} custom-call(s32[10]{0:T(128)S(1)} %pad_add_fusion.at_ref, bf16[8,8,2,32,128]{4,3,2,1,0:T(8,128)(2,1)S(1)} %all-to-all-done.four_ref, bf16[4,125,4000]{2,1,0:T(8,128)(2,1)S(1)} %copy-done.1, bf16[4,125,4000]{2,1,0:T(8,128)(2,1)S(1)} %copy-done.1, bf16[4,125,4000]{2,1,0:T(8,128)(2,1)S(1)} %copy-done.1, ...), custom_call_target="tpu_custom_call" | custom-call | tf_op jit(solution)/shard_map/pallas_call | solution.py:180
  58.8 2.1 %shard_map.42 = s16[2064,256]{1,0:T(8,128)(2,1)S(1)} custom-call(s32[10]{0:T(128)S(1)} %pad_add_fusion.at_ref, bf16[8,8,2,32,128]{4,3,2,1,0:T(8,128)(2,1)S(1)} %all-to-all-done.four_ref, bf16[4,125,4000]{2,1,0:T(8,128)(2,1)S(1)} %copy-done.1, bf16[4,125,4000]{2,1,0:T(8,128)(2,1)S(1)} %copy-done.1, bf16[4,125,4000]{2,1,0:T(8,128)(2,1)S(1)} %copy-done.1, ...), custom_call_target="tpu_custom_call" | custom-call | tf_op jit(solution)/shard_map/pallas_call | solution.py:180
  60.9 1.3 collective-permute-done.13.rest_12_
  63.0 2.0 %shard_map.46 = s16[2064,256]{1,0:T(8,128)(2,1)S(1)} custom-call(s32[10]{0:T(128)S(1)} %pad_add_fusion.at_ref, bf16[8,8,2,32,128]{4,3,2,1,0:T(8,128)(2,1)S(1)} %all-to-all-done.four_ref, bf16[4,125,4000]{2,1,0:T(8,128)(2,1)S(1)} %copy-done, bf16[4,125,4000]{2,1,0:T(8,128)(2,1)S(1)} %copy-done, bf16[4,125,4000]{2,1,0:T(8,128)(2,1)S(1)} %copy-done, ...), custom_call_target="tpu_custom_call" | custom-call | tf_op jit(solution)/shard_map/pallas_call | solution.py:180
  65.0 3.8 %collective-permute-start.12 = (s16[2064,256]{1,0:T(8,128)(2,1)S(1)}, s16[2064,256]{1,0:T(8,128)(2,1)S(1)}, u32[]{:S(2)}, u32[]{:S(2)}) collective-permute-start(s16[2064,256]{1,0:T(8,128)(2,1)S(1)} %shard_map.46), channel_id=1, source_target_pairs={{0,24},{8,0},{16,8},{24,16},{32,56},{40,32},{48,40},{56,48},{64,88... | collective-permute-start | bytes 3170312 | tf_op jit(solution)/shard_map/ppermute | solution.py:247
  68.8 2.0 %shard_map.49 = s16[2064,256]{1,0:T(8,128)(2,1)S(1)} custom-call(s32[10]{0:T(128)S(1)} %pad_add_fusion.at_ref, bf16[8,8,2,32,128]{4,3,2,1,0:T(8,128)(2,1)S(1)} %all-to-all-done.four_ref, bf16[4,125,4000]{2,1,0:T(8,128)(2,1)S(1)} %copy-done, bf16[4,125,4000]{2,1,0:T(8,128)(2,1)S(1)} %copy-done, bf16[4,125,4000]{2,1,0:T(8,128)(2,1)S(1)} %copy-done, ...), custom_call_target="tpu_custom_call" | custom-call | tf_op jit(solution)/shard_map/pallas_call | solution.py:180
  70.8 2.1 %shard_map.48 = s16[2064,256]{1,0:T(8,128)(2,1)S(1)} custom-call(s32[10]{0:T(128)S(1)} %pad_add_fusion.at_ref, bf16[8,8,2,32,128]{4,3,2,1,0:T(8,128)(2,1)S(1)} %all-to-all-done.four_ref, bf16[4,125,4000]{2,1,0:T(8,128)(2,1)S(1)} %copy-done, bf16[4,125,4000]{2,1,0:T(8,128)(2,1)S(1)} %copy-done, bf16[4,125,4000]{2,1,0:T(8,128)(2,1)S(1)} %copy-done, ...), custom_call_target="tpu_custom_call" | custom-call | tf_op jit(solution)/shard_map/pallas_call | solution.py:180
  72.9 2.1 %shard_map.51 = s16[2064,256]{1,0:T(8,128)(2,1)S(1)} custom-call(s32[10]{0:T(128)S(1)} %pad_add_fusion.at_ref, bf16[8,8,2,32,128]{4,3,2,1,0:T(8,128)(2,1)S(1)} %all-to-all-done.four_ref, bf16[4,125,4000]{2,1,0:T(8,128)(2,1)S(1)} %copy-done, bf16[4,125,4000]{2,1,0:T(8,128)(2,1)S(1)} %copy-done, bf16[4,125,4000]{2,1,0:T(8,128)(2,1)S(1)} %copy-done, ...), custom_call_target="tpu_custom_call" | custom-call | tf_op jit(solution)/shard_map/pallas_call | solution.py:180
  75.0 6.2 %collective-permute-done.rest_3_.rest_4_.rest_5_ = s16[2064,256]{1,0:T(8,128)(2,1)S(1)} collective-permute-done((s16[2064,256]{1,0:T(8,128)(2,1)S(1)}, s16[2064,256]{1,0:T(8,128)(2,1)S(1)}, u32[]{:S(2)}, u32[]{:S(2)}) %collective-permute-start) | collective-permute-done | bytes 1056800 | tf_op jit(solution)/shard_map/ppermute | solution.py:247
  81.2 1.9 %collective-permute-start.15 = (s16[2064,256]{1,0:T(8,128)(2,1)S(1)}, s16[2064,256]{1,0:T(8,128)(2,1)S(1)}, u32[]{:S(2)}, u32[]{:S(2)}) collective-permute-start(s16[2064,256]{1,0:T(8,128)(2,1)S(1)} %shard_map.49), channel_id=1, source_target_pairs={{0,8},{8,16},{16,24},{24,0},{32,40},{40,48},{48,56},{56,32},{64,72... | collective-permute-start | bytes 3170312 | tf_op jit(solution)/shard_map/ppermute | solution.py:247
  83.1 1.9 %collective-permute-start.14 = (s16[2064,256]{1,0:T(8,128)(2,1)S(1)}, s16[2064,256]{1,0:T(8,128)(2,1)S(1)}, u32[]{:S(2)}, u32[]{:S(2)}) collective-permute-start(s16[2064,256]{1,0:T(8,128)(2,1)S(1)} %shard_map.48), channel_id=1, source_target_pairs={{0,8},{8,16},{16,24},{24,0},{32,40},{40,48},{48,56},{56,32},{64,72... | collective-permute-start | bytes 3170312 | tf_op jit(solution)/shard_map/ppermute | solution.py:247
  85.0 16.8 %collective-permute-done.2.rest_6_.rest_7_.rest_8_ = s16[2064,256]{1,0:T(8,128)(2,1)S(1)} collective-permute-done((s16[2064,256]{1,0:T(8,128)(2,1)S(1)}, s16[2064,256]{1,0:T(8,128)(2,1)S(1)}, u32[]{:S(2)}, u32[]{:S(2)}) %collective-permute-start.2) | collective-permute-done | bytes 1056800 | tf_op jit(solution)/shard_map/ppermute | solution.py:247
  101.9 4.0 %collective-permute-start.17 = (s16[2064,256]{1,0:T(8,128)(2,1)S(1)}, s16[2064,256]{1,0:T(8,128)(2,1)S(1)}, u32[]{:S(2)}, u32[]{:S(2)}) collective-permute-start(s16[2064,256]{1,0:T(8,128)(2,1)S(1)} %shard_map.51), channel_id=1, source_target_pairs={{0,24},{8,0},{16,8},{24,16},{32,56},{40,32},{48,40},{56,48},{64,88... | collective-permute-start | bytes 3170312 | tf_op jit(solution)/shard_map/ppermute | solution.py:247
  105.9 1.4 shard_map.44
  107.4 3.2 %collective-permute-start.8 = (s16[528,256]{1,0:T(8,128)(2,1)S(1)}, s16[528,256]{1,0:T(8,128)(2,1)S(1)}, u32[]{:S(2)}, u32[]{:S(2)}) collective-permute-start(s16[528,256]{1,0:T(8,128)(2,1)S(1)} %get-tuple-element.19), channel_id=1, source_target_pairs={{0,24},{8,0},{16,8},{24,16},{32,56},{40,32},{48,40},{56,48},{64,88... | collective-permute-start | bytes 811016 | tf_op jit(solution)/shard_map/ppermute | solution.py:247
  110.6 21.4 %collective-permute-done.14.rest_6_.rest_7_.rest_8_.rest_28_.rest_29_.rest_30_ = s16[2064,256]{1,0:T(8,128)(2,1)S(1)} collective-permute-done((s16[2064,256]{1,0:T(8,128)(2,1)S(1)}, s16[2064,256]{1,0:T(8,128)(2,1)S(1)}, u32[]{:S(2)}, u32[]{:S(2)}) %collective-permute-start.14) | collective-permute-done | bytes 1056800 | tf_op jit(solution)/shard_map/ppermute | solution.py:247
  132.0 1.4 shard_map.53
  134.0 1.5 collective-permute-start.20
  135.5 1.4 shard_map.43
  136.9 2.2 %collective-permute-start.6 = (s16[528,256]{1,0:T(8,128)(2,1)S(1)}, s16[528,256]{1,0:T(8,128)(2,1)S(1)}, u32[]{:S(2)}, u32[]{:S(2)}) collective-permute-start(s16[528,256]{1,0:T(8,128)(2,1)S(1)} %get-tuple-element.17), channel_id=1, source_target_pairs={{0,24},{8,0},{16,8},{24,16},{32,56},{40,32},{48,40},{56,48},{64,88... | collective-permute-start | bytes 811016 | tf_op jit(solution)/shard_map/ppermute | solution.py:247
  139.2 1.4 shard_map.52
  140.9 1.6 shard_map.45
  142.5 3.1 %collective-permute-start.22 = (s16[528,256]{1,0:T(8,128)(2,1)S(1)}, s16[528,256]{1,0:T(8,128)(2,1)S(1)}, u32[]{:S(2)}, u32[]{:S(2)}) collective-permute-start(s16[528,256]{1,0:T(8,128)(2,1)S(1)} %get-tuple-element.27), channel_id=1, source_target_pairs={{0,32},{8,40},{16,48},{24,56},{32,64},{40,72},{48,80},{56,88},{64,... | collective-permute-start | bytes 811016 | tf_op jit(solution)/shard_map/ppermute | solution.py:247
  145.7 1.6 shard_map.54
  147.3 3.3 %collective-permute-start.11 = (s16[528,256]{1,0:T(8,128)(2,1)S(1)}, s16[528,256]{1,0:T(8,128)(2,1)S(1)}, u32[]{:S(2)}, u32[]{:S(2)}) collective-permute-start(s16[528,256]{1,0:T(8,128)(2,1)S(1)} %get-tuple-element.22), channel_id=1, source_target_pairs={{0,24},{8,0},{16,8},{24,16},{32,56},{40,32},{48,40},{56,48},{64,88... | collective-permute-start | bytes 811016 | tf_op jit(solution)/shard_map/ppermute | solution.py:247
  150.6 2.0 %collective-permute-start.21 = (s16[528,256]{1,0:T(8,128)(2,1)S(1)}, s16[528,256]{1,0:T(8,128)(2,1)S(1)}, u32[]{:S(2)}, u32[]{:S(2)}) collective-permute-start(s16[528,256]{1,0:T(8,128)(2,1)S(1)} %get-tuple-element.26), channel_id=1, source_target_pairs={{0,32},{8,40},{16,48},{24,56},{32,64},{40,72},{48,80},{56,88},{64,... | collective-permute-start | bytes 811016 | tf_op jit(solution)/shard_map/ppermute | solution.py:247
  153.4 1.2 collective-permute-done.11.rest_21_
  154.6 2.5 %collective-permute-done.21.rest_32_ = s16[528,256]{1,0:T(8,128)(2,1)S(1)} collective-permute-done((s16[528,256]{1,0:T(8,128)(2,1)S(1)}, s16[528,256]{1,0:T(8,128)(2,1)S(1)}, u32[]{:S(2)}, u32[]{:S(2)}) %collective-permute-start.21) | collective-permute-done | bytes 270368 | tf_op jit(solution)/shard_map/ppermute | solution.py:247
  157.1 3.2 %collective-permute-done.23.rest_43_ = s16[528,256]{1,0:T(8,128)(2,1)S(1)} collective-permute-done((s16[528,256]{1,0:T(8,128)(2,1)S(1)}, s16[528,256]{1,0:T(8,128)(2,1)S(1)}, u32[]{:S(2)}, u32[]{:S(2)}) %collective-permute-start.23) | collective-permute-done | bytes 270368 | tf_op jit(solution)/shard_map/ppermute | solution.py:247
  160.3 4.4 %shard_map.55 = f32[250,8,256]{2,1,0:T(8,128)} custom-call(s32[10]{0:T(128)S(1)} %pad_add_fusion.at_ref, bf16[8,8,2,32,128]{4,3,2,1,0:T(8,128)(2,1)S(1)} %all-to-all-done.four_ref, bf16[4,125,4000]{2,1,0:T(8,128)(2,1)S(1)} %copy-done.2, bf16[4,125,4000]{2,1,0:T(8,128)(2,1)S(1)} %copy-done.2, bf16[4,125,4000]{2,1,0:T(8,128)(2,1)S(1)} %copy-done.2, ...), custom_call_target="tpu_custom_call" | custom-call | tf_op jit(solution)/shard_map/pallas_call | solution.py:180
  (34 shorter events, 3.9 us)
Async XLA Ops:
  2.7 21.7 %all-to-all-start = ((bf16[8,8,2,32,128]{4,3,2,1,0:T(8,128)(2,1)}), bf16[8,8,2,32,128]{4,3,2,1,0:T(8,128)(2,1)S(1)}, u32[]{:S(2)}, u32[]{:S(2)}) async-start(bf16[8,8,2,32,128]{4,3,2,1,0:T(8,128)(2,1)} %bitcast.3), calls=%async_computation | async-start | bytes 2097152 | tf_op jit(solution)/shard_map/all_to_all | solution.py:241
  7.1 11.1 %copy-start.3 = (s32[8]{0:T(128)S(1)}, s32[8]{0:T(128)}, u32[]{:S(2)}) copy-start(s32[8]{0:T(128)} %param.5) | copy-start | bytes 100
  24.3 2.2 %copy-start.1 = (bf16[4,125,4000]{2,1,0:T(8,128)(2,1)S(1)}, bf16[4,125,4000]{2,1,0:T(8,128)(2,1)}, u32[]{:S(2)}) copy-start(bf16[4,125,4000]{2,1,0:T(8,128)(2,1)} %get-tuple-element.30.rest_0_.rest_1_.rest_2_.rest_3_.rest_4_.rest_5_.rest_6_.rest_7_.rest_8_.rest_9_.rest_10_.rest_11_.rest_12_.rest_13_) | copy-start | bytes 12000004
  28.5 25.8 %collective-permute-start.1 = (s16[2064,256]{1,0:T(8,128)(2,1)S(1)}, s16[2064,256]{1,0:T(8,128)(2,1)S(1)}, u32[]{:S(2)}, u32[]{:S(2)}) collective-permute-start(s16[2064,256]{1,0:T(8,128)(2,1)S(1)} %shard_map.38), channel_id=1, source_target_pairs={{0,32},{8,40},{16,48},{24,56},{32,64},{40,72},{48,80},{56,88},{64,... | collective-permute-start | bytes 3170312 | tf_op jit(solution)/shard_map/ppermute | solution.py:247
  29.1 3.6 %copy-start = (bf16[4,125,4000]{2,1,0:T(8,128)(2,1)S(1)}, bf16[4,125,4000]{2,1,0:T(8,128)(2,1)}, u32[]{:S(2)}) copy-start(bf16[4,125,4000]{2,1,0:T(8,128)(2,1)} %get-tuple-element.29.rest_0_.rest_1_.rest_2_.rest_3_.rest_4_.rest_5_.rest_6_.rest_7_.rest_8_.rest_9_.rest_10_.rest_11_.rest_12_.rest_22_.rest_23_.rest_24_.rest_33_.rest_34_.rest_35_) | copy-start | bytes 12000004
  31.0 27.5 %collective-permute-start.4 = (s16[2064,256]{1,0:T(8,128)(2,1)S(1)}, s16[2064,256]{1,0:T(8,128)(2,1)S(1)}, u32[]{:S(2)}, u32[]{:S(2)}) collective-permute-start(s16[2064,256]{1,0:T(8,128)(2,1)S(1)} %shard_map.41), channel_id=1, source_target_pairs={{0,96},{8,104},{16,112},{24,120},{32,0},{40,8},{48,16},{56,24},{64... | collective-permute-start | bytes 3170312 | tf_op jit(solution)/shard_map/ppermute | solution.py:247
  34.7 27.5 %collective-permute-start.13 = (s16[2064,256]{1,0:T(8,128)(2,1)S(1)}, s16[2064,256]{1,0:T(8,128)(2,1)S(1)}, u32[]{:S(2)}, u32[]{:S(2)}) collective-permute-start(s16[2064,256]{1,0:T(8,128)(2,1)S(1)} %shard_map.47), channel_id=1, source_target_pairs={{0,8},{8,16},{16,24},{24,0},{32,40},{40,48},{48,56},{56,32},{64,72... | collective-permute-start | bytes 3170312 | tf_op jit(solution)/shard_map/ppermute | solution.py:247
  38.6 26.4 %collective-permute-start.16 = (s16[2064,256]{1,0:T(8,128)(2,1)S(1)}, s16[2064,256]{1,0:T(8,128)(2,1)S(1)}, u32[]{:S(2)}, u32[]{:S(2)}) collective-permute-start(s16[2064,256]{1,0:T(8,128)(2,1)S(1)} %shard_map.50), channel_id=1, source_target_pairs={{0,24},{8,0},{16,8},{24,16},{32,56},{40,32},{48,40},{56,48},{64,88... | collective-permute-start | bytes 3170312 | tf_op jit(solution)/shard_map/ppermute | solution.py:247
  42.8 38.3 %collective-permute-start = (s16[2064,256]{1,0:T(8,128)(2,1)S(1)}, s16[2064,256]{1,0:T(8,128)(2,1)S(1)}, u32[]{:S(2)}, u32[]{:S(2)}) collective-permute-start(s16[2064,256]{1,0:T(8,128)(2,1)S(1)} %shard_map.37), channel_id=1, source_target_pairs={{0,96},{8,104},{16,112},{24,120},{32,0},{40,8},{48,16},{56,24},{64... | collective-permute-start | bytes 3170312 | tf_op jit(solution)/shard_map/ppermute | solution.py:247
  54.3 28.8 %collective-permute-start.3 = (s16[2064,256]{1,0:T(8,128)(2,1)S(1)}, s16[2064,256]{1,0:T(8,128)(2,1)S(1)}, u32[]{:S(2)}, u32[]{:S(2)}) collective-permute-start(s16[2064,256]{1,0:T(8,128)(2,1)S(1)} %shard_map.40), channel_id=1, source_target_pairs={{0,32},{8,40},{16,48},{24,56},{32,64},{40,72},{48,80},{56,88},{64,... | collective-permute-start | bytes 3170312 | tf_op jit(solution)/shard_map/ppermute | solution.py:247
  58.5 43.3 %collective-permute-start.2 = (s16[2064,256]{1,0:T(8,128)(2,1)S(1)}, s16[2064,256]{1,0:T(8,128)(2,1)S(1)}, u32[]{:S(2)}, u32[]{:S(2)}) collective-permute-start(s16[2064,256]{1,0:T(8,128)(2,1)S(1)} %shard_map.39), channel_id=1, source_target_pairs={{0,32},{8,40},{16,48},{24,56},{32,64},{40,72},{48,80},{56,88},{64,... | collective-permute-start | bytes 3170312 | tf_op jit(solution)/shard_map/ppermute | solution.py:247
  62.2 43.7 %collective-permute-start.5 = (s16[2064,256]{1,0:T(8,128)(2,1)S(1)}, s16[2064,256]{1,0:T(8,128)(2,1)S(1)}, u32[]{:S(2)}, u32[]{:S(2)}) collective-permute-start(s16[2064,256]{1,0:T(8,128)(2,1)S(1)} %shard_map.42), channel_id=1, source_target_pairs={{0,96},{8,104},{16,112},{24,120},{32,0},{40,8},{48,16},{56,24},{64... | collective-permute-start | bytes 3170312 | tf_op jit(solution)/shard_map/ppermute | solution.py:247
  65.0 42.4 %collective-permute-start.12 = (s16[2064,256]{1,0:T(8,128)(2,1)S(1)}, s16[2064,256]{1,0:T(8,128)(2,1)S(1)}, u32[]{:S(2)}, u32[]{:S(2)}) collective-permute-start(s16[2064,256]{1,0:T(8,128)(2,1)S(1)} %shard_map.46), channel_id=1, source_target_pairs={{0,24},{8,0},{16,8},{24,16},{32,56},{40,32},{48,40},{56,48},{64,88... | collective-permute-start | bytes 3170312 | tf_op jit(solution)/shard_map/ppermute | solution.py:247
  81.2 29.4 %collective-permute-start.15 = (s16[2064,256]{1,0:T(8,128)(2,1)S(1)}, s16[2064,256]{1,0:T(8,128)(2,1)S(1)}, u32[]{:S(2)}, u32[]{:S(2)}) collective-permute-start(s16[2064,256]{1,0:T(8,128)(2,1)S(1)} %shard_map.49), channel_id=1, source_target_pairs={{0,8},{8,16},{16,24},{24,0},{32,40},{40,48},{48,56},{56,32},{64,72... | collective-permute-start | bytes 3170312 | tf_op jit(solution)/shard_map/ppermute | solution.py:247
  83.1 48.9 %collective-permute-start.14 = (s16[2064,256]{1,0:T(8,128)(2,1)S(1)}, s16[2064,256]{1,0:T(8,128)(2,1)S(1)}, u32[]{:S(2)}, u32[]{:S(2)}) collective-permute-start(s16[2064,256]{1,0:T(8,128)(2,1)S(1)} %shard_map.48), channel_id=1, source_target_pairs={{0,8},{8,16},{16,24},{24,0},{32,40},{40,48},{48,56},{56,32},{64,72... | collective-permute-start | bytes 3170312 | tf_op jit(solution)/shard_map/ppermute | solution.py:247
  101.9 30.2 %collective-permute-start.17 = (s16[2064,256]{1,0:T(8,128)(2,1)S(1)}, s16[2064,256]{1,0:T(8,128)(2,1)S(1)}, u32[]{:S(2)}, u32[]{:S(2)}) collective-permute-start(s16[2064,256]{1,0:T(8,128)(2,1)S(1)} %shard_map.51), channel_id=1, source_target_pairs={{0,24},{8,0},{16,8},{24,16},{32,56},{40,32},{48,40},{56,48},{64,88... | collective-permute-start | bytes 3170312 | tf_op jit(solution)/shard_map/ppermute | solution.py:247
  107.3 33.3 %collective-permute-start.7 = (s16[528,256]{1,0:T(8,128)(2,1)S(1)}, s16[528,256]{1,0:T(8,128)(2,1)S(1)}, u32[]{:S(2)}, u32[]{:S(2)}) collective-permute-start(s16[528,256]{1,0:T(8,128)(2,1)S(1)} %get-tuple-element.18), channel_id=1, source_target_pairs={{0,8},{8,16},{16,24},{24,0},{32,40},{40,48},{48,56},{56,32},{64,72... | collective-permute-start | bytes 811016 | tf_op jit(solution)/shard_map/ppermute | solution.py:247
  107.4 33.3 %collective-permute-start.8 = (s16[528,256]{1,0:T(8,128)(2,1)S(1)}, s16[528,256]{1,0:T(8,128)(2,1)S(1)}, u32[]{:S(2)}, u32[]{:S(2)}) collective-permute-start(s16[528,256]{1,0:T(8,128)(2,1)S(1)} %get-tuple-element.19), channel_id=1, source_target_pairs={{0,24},{8,0},{16,8},{24,16},{32,56},{40,32},{48,40},{56,48},{64,88... | collective-permute-start | bytes 811016 | tf_op jit(solution)/shard_map/ppermute | solution.py:247
  133.4 9.1 %collective-permute-start.19 = (s16[528,256]{1,0:T(8,128)(2,1)S(1)}, s16[528,256]{1,0:T(8,128)(2,1)S(1)}, u32[]{:S(2)}, u32[]{:S(2)}) collective-permute-start(s16[528,256]{1,0:T(8,128)(2,1)S(1)} %get-tuple-element.24), channel_id=1, source_target_pairs={{0,32},{8,40},{16,48},{24,56},{32,64},{40,72},{48,80},{56,88},{64,... | collective-permute-start | bytes 811016 | tf_op jit(solution)/shard_map/ppermute | solution.py:247
  134.0 11.7 %collective-permute-start.20 = (s16[528,256]{1,0:T(8,128)(2,1)S(1)}, s16[528,256]{1,0:T(8,128)(2,1)S(1)}, u32[]{:S(2)}, u32[]{:S(2)}) collective-permute-start(s16[528,256]{1,0:T(8,128)(2,1)S(1)} %get-tuple-element.25), channel_id=1, source_target_pairs={{0,96},{8,104},{16,112},{24,120},{32,0},{40,8},{48,16},{56,24},{64... | collective-permute-start | bytes 811016 | tf_op jit(solution)/shard_map/ppermute | solution.py:247
  136.9 10.4 %collective-permute-start.6 = (s16[528,256]{1,0:T(8,128)(2,1)S(1)}, s16[528,256]{1,0:T(8,128)(2,1)S(1)}, u32[]{:S(2)}, u32[]{:S(2)}) collective-permute-start(s16[528,256]{1,0:T(8,128)(2,1)S(1)} %get-tuple-element.17), channel_id=1, source_target_pairs={{0,24},{8,0},{16,8},{24,16},{32,56},{40,32},{48,40},{56,48},{64,88... | collective-permute-start | bytes 811016 | tf_op jit(solution)/shard_map/ppermute | solution.py:247
  140.6 10.0 %collective-permute-start.10 = (s16[528,256]{1,0:T(8,128)(2,1)S(1)}, s16[528,256]{1,0:T(8,128)(2,1)S(1)}, u32[]{:S(2)}, u32[]{:S(2)}) collective-permute-start(s16[528,256]{1,0:T(8,128)(2,1)S(1)} %get-tuple-element.21), channel_id=1, source_target_pairs={{0,8},{8,16},{16,24},{24,0},{32,40},{40,48},{48,56},{56,32},{64,72... | collective-permute-start | bytes 811016 | tf_op jit(solution)/shard_map/ppermute | solution.py:247
  140.7 11.9 %collective-permute-start.18 = (s16[528,256]{1,0:T(8,128)(2,1)S(1)}, s16[528,256]{1,0:T(8,128)(2,1)S(1)}, u32[]{:S(2)}, u32[]{:S(2)}) collective-permute-start(s16[528,256]{1,0:T(8,128)(2,1)S(1)} %get-tuple-element.23), channel_id=1, source_target_pairs={{0,96},{8,104},{16,112},{24,120},{32,0},{40,8},{48,16},{56,24},{64... | collective-permute-start | bytes 811016 | tf_op jit(solution)/shard_map/ppermute | solution.py:247
  142.5 10.1 %collective-permute-start.22 = (s16[528,256]{1,0:T(8,128)(2,1)S(1)}, s16[528,256]{1,0:T(8,128)(2,1)S(1)}, u32[]{:S(2)}, u32[]{:S(2)}) collective-permute-start(s16[528,256]{1,0:T(8,128)(2,1)S(1)} %get-tuple-element.27), channel_id=1, source_target_pairs={{0,32},{8,40},{16,48},{24,56},{32,64},{40,72},{48,80},{56,88},{64,... | collective-permute-start | bytes 811016 | tf_op jit(solution)/shard_map/ppermute | solution.py:247
  145.7 7.7 %collective-permute-start.9 = (s16[528,256]{1,0:T(8,128)(2,1)S(1)}, s16[528,256]{1,0:T(8,128)(2,1)S(1)}, u32[]{:S(2)}, u32[]{:S(2)}) collective-permute-start(s16[528,256]{1,0:T(8,128)(2,1)S(1)} %get-tuple-element.20), channel_id=1, source_target_pairs={{0,8},{8,16},{16,24},{24,0},{32,40},{40,48},{48,56},{56,32},{64,72... | collective-permute-start | bytes 811016 | tf_op jit(solution)/shard_map/ppermute | solution.py:247
  145.7 14.6 %copy-start.2 = (bf16[4,125,4000]{2,1,0:T(8,128)(2,1)S(1)}, bf16[4,125,4000]{2,1,0:T(8,128)(2,1)}, u32[]{:S(2)}) copy-start(bf16[4,125,4000]{2,1,0:T(8,128)(2,1)} %get-tuple-element.30.rest_0_.rest_1_.rest_2_.rest_3_.rest_4_.rest_5_.rest_6_.rest_7_.rest_8_.rest_9_.rest_10_.rest_11_.rest_12_.rest_13_) | copy-start | bytes 12000004
  147.3 7.3 %collective-permute-start.11 = (s16[528,256]{1,0:T(8,128)(2,1)S(1)}, s16[528,256]{1,0:T(8,128)(2,1)S(1)}, u32[]{:S(2)}, u32[]{:S(2)}) collective-permute-start(s16[528,256]{1,0:T(8,128)(2,1)S(1)} %get-tuple-element.22), channel_id=1, source_target_pairs={{0,24},{8,0},{16,8},{24,16},{32,56},{40,32},{48,40},{56,48},{64,88... | collective-permute-start | bytes 811016 | tf_op jit(solution)/shard_map/ppermute | solution.py:247
  150.6 6.5 %collective-permute-start.21 = (s16[528,256]{1,0:T(8,128)(2,1)S(1)}, s16[528,256]{1,0:T(8,128)(2,1)S(1)}, u32[]{:S(2)}, u32[]{:S(2)}) collective-permute-start(s16[528,256]{1,0:T(8,128)(2,1)S(1)} %get-tuple-element.26), channel_id=1, source_target_pairs={{0,32},{8,40},{16,48},{24,56},{32,64},{40,72},{48,80},{56,88},{64,... | collective-permute-start | bytes 811016 | tf_op jit(solution)/shard_map/ppermute | solution.py:247
  152.6 7.7 %collective-permute-start.23 = (s16[528,256]{1,0:T(8,128)(2,1)S(1)}, s16[528,256]{1,0:T(8,128)(2,1)S(1)}, u32[]{:S(2)}, u32[]{:S(2)}) collective-permute-start(s16[528,256]{1,0:T(8,128)(2,1)S(1)} %get-tuple-element.28), channel_id=1, source_target_pairs={{0,96},{8,104},{16,112},{24,120},{32,0},{40,8},{48,16},{56,24},{64... | collective-permute-start | bytes 811016 | tf_op jit(solution)/shard_map/ppermute | solution.py:247
where the time goes:
time: 165 us
  waiting for transfers between devices  62.3 us (38%)
  starting transfers between devices  42.8 us (26%)
  Pallas kernels  37.3 us (23%)
  local copies, waits for them, and re-layouts  22 us (13%)
    ppermute x24, waiting for transfers between devices, send(): return lax.ppermute(array, 'lat', ring(axis, sign))  62.3 us
    ppermute x24, starting transfers between devices, send(): return lax.ppermute(array, 'lat', ring(axis, sign))  38.3 us
    pallas_call x19, Pallas kernels, call(): pl.pallas_call(body, grid_spec=pltpu.PrefetchScalarGridSpec(num_scalar_pr...  37.3 us
    unnamed x10, local copies, waits for them, and re-layouts  14.7 us
    slice x1, local copies, waits for them, and re-layouts, per_device(): table = (table[:2 * PAIR], table[2 * PAIR:])  5.98 us
    all_to_all x1, starting transfers between devices, per_device(): lax.all_to_all(split, 'wave', split_axis=0, concat_axis=0, tiled=True)  4.47 us
  transfers between devices with their start and end apart: 25, of which 10 were waited for; matrix products, arithmetic and copies ran while one was open for 10% of the time, Pallas kernels for 19%

commit v1 on v0

--- a/solution.py
+++ b/solution.py
@@ -31,10 +31,14 @@
     keep = jnp.where(offset >= 0, 1.0, 0.0)
     sign = jnp.where((offset & 1) == 0, keep, -keep)
     tab = jnp.concatenate([(tab * keep).astype(jnp.bfloat16), (tab * sign).astype(jnp.bfloat16)], axis=0)
-    north = four_ref[:, slot, 0].reshape(ROWS, HALF)
-    south = four_ref[:, slot, 1].reshape(ROWS, HALF)
-    return jnp.dot(north, tab[:HALF], preferred_element_type=jnp.float32) + jnp.dot(
-        south, tab[HALF:], preferred_element_type=jnp.float32
+
+    def fields(hemisphere):
+        held = four_ref[:, slot, hemisphere]
+        held = held.reshape(ROWS, held.shape[-1])
+        return jnp.concatenate([held, jnp.zeros((ROWS, HALF - held.shape[1]), held.dtype)], axis=1)
+
+    return jnp.dot(fields(0), tab[:HALF], preferred_element_type=jnp.float32) + jnp.dot(
+        fields(1), tab[HALF:], preferred_element_type=jnp.float32
     )
 
 
@@ -98,7 +102,7 @@
     return specs
 
 
-def first_kernel(at_ref, four_ref, *rest, axis, ahead, group, width, terms):
+def first_kernel(at_ref, four_ref, *rest, axis, ahead, group, width, terms, looped):
     out_ref = rest[-1]
     tiles, states = rest[: SIDE * TILES], rest[SIDE * TILES : SIDE * TILES + terms]
 
@@ -111,7 +115,7 @@
             total = total + decoded(rows_of(state, at), state[PAIR * SIDE * ROWS :], at)
         return total
 
-    store_coded(out_ref, SIDE, value, True)
+    store_coded(out_ref, SIDE, value, looped)
 
 
 def rows_of(ref, at):
@@ -158,8 +162,8 @@
     return pl.BlockSpec(array.shape, lambda i, at: (0,) * array.ndim)
 
 
-def four_of(slots, index):
-    return pl.BlockSpec((8, slots, 2, 32, HALF), lambda i, at: (0, index, 0, 0, 0))
+def four_of(four, slots, index):
+    return pl.BlockSpec((8, slots, *four.shape[2:]), lambda i, at: (0, index, 0, 0, 0))
 
 
 def second_operands(group, axis, ahead, tab, firsts, states, width):
@@ -191,11 +195,11 @@
     axis = group // 2
     tab = tab[axis]
     blocks = [functools.partial(block_at, axis=axis, ahead=ahead, b=b) for b in range(SIDE)]
-    specs = [four_of(PAIR, group)] + tile_specs(PAIR, tab.shape[1], width, group % 2, blocks)
+    specs = [four_of(four, PAIR, group)] + tile_specs(PAIR, tab.shape[1], width, group % 2, blocks)
     specs += [whole(state) for state in states]
     operands = [four] + [tab] * (SIDE * TILES) + list(states)
     body = functools.partial(
-        first_kernel, axis=axis, ahead=ahead, group=group, width=width, terms=len(states)
+        first_kernel, axis=axis, ahead=ahead, group=group, width=width, terms=len(states), looped=ahead != 2
     )
     out = ((PAIR * SIDE * ROWS + TAIL, LANES), jnp.int16)
     return call(body, at, operands, specs, [out])[0]
@@ -203,7 +207,7 @@
 
 def second_hop(start, aheads, at, four, tab, firsts, states, width):
     axis = 1 - start // 2
-    specs, operands = [four_of(2 * PAIR, start // 2)], [four]
+    specs, operands = [four_of(four, 2 * PAIR, start // 2)], [four]
     for pair, ahead in enumerate(aheads):
         more, arrays = second_operands(start + pair, axis, ahead, tab, firsts[pair], states[pair], width)
         specs, operands = specs + more, operands + arrays
@@ -236,8 +240,7 @@
     me = lax.axis_index("lat")
 
     split = fourier.transpose(2, 0, 3, 1)
-    split = jnp.pad(split, ((0, 0), (0, 0), (0, 0), (0, HALF - rows)))
-    split = split.reshape(8, slots, 2, split.shape[2], HALF)
+    split = split.reshape(8, slots, 2, split.shape[2], rows)
     four = lax.all_to_all(split, "wave", split_axis=0, concat_axis=0, tiled=True)
     at = jnp.concatenate([jnp.stack([me // SIDE, me % SIDE]).astype(jnp.int32), wavenums])
     table = lax.optimization_barrier(with_layout_constraint(table, Layout((0, 1, 2))))

time: 165 us -> 164 us (level)
    transpose x0 -> x1, local copies, waits for them, and re-layouts: none -> 2.35 us  [per_device(): split = fourier.transpose(2, 0, 3, 1)]
    unnamed x10 -> x9, local copies, waits for them, and re-layouts: 14.7 us -> 13.3 us
  transfers between devices with their start and end apart: 25 -> 25, of which waited for: 10 -> 10; matrix products, arithmetic and copies ran while one was open for 10% -> 10% of each run, Pallas kernels for 19% -> 18%
where the time goes in v1:
time: 164 us
  waiting for transfers between devices  62.8 us (38%)
  starting transfers between devices  43.5 us (27%)
  Pallas kernels  35.8 us (22%)
  local copies, waits for them, and re-layouts  21.6 us (13%)
    ppermute x24, waiting for transfers between devices, send(): return lax.ppermute(array, 'lat', ring(axis, sign))  62.8 us
    ppermute x24, starting transfers between devices, send(): return lax.ppermute(array, 'lat', ring(axis, sign))  39 us
    pallas_call x19, Pallas kernels, call(): pl.pallas_call(body, grid_spec=pltpu.PrefetchScalarGridSpec(num_scalar_pr...  35.8 us
    unnamed x9, local copies, waits for them, and re-layouts  13.3 us
    slice x1, local copies, waits for them, and re-layouts, per_device(): table = (table[:2 * PAIR], table[2 * PAIR:])  5.98 us
    all_to_all x1, starting transfers between devices, per_device(): lax.all_to_all(split, 'wave', split_axis=0, concat_axis=0, tiled=True)  4.47 us
  transfers between devices with their start and end apart: 25, of which 10 were waited for; matrix products, arithmetic and copies ran while one was open for 10% of the time, Pallas kernels for 18%

profile of v1, /device:TPU:6, one launch (start us, length us, event | category | flops | bytes accessed | tf_op | source)
XLA Modules:
  0.0 164.0 jit_solution(805684293809533500)
XLA Ops:
  0.0 2.3 %copy.4 = bf16[64,2,32,125]{3,2,1,0:T(8,128)(2,1)} copy(bf16[64,2,32,125]{3,2,0,1:T(8,128)(2,1)} %bitcast.4) | data formatting | bytes 2048000 | tf_op jit(solution)/shard_map/transpose | solution.py:242
  2.3 4.5 %all-to-all-start = ((bf16[8,8,2,32,125]{4,3,2,1,0:T(8,128)(2,1)}), bf16[8,8,2,32,125]{4,3,2,1,0:T(8,128)(2,1)S(1)}, u32[]{:S(2)}, u32[]{:S(2)}) async-start(bf16[8,8,2,32,125]{4,3,2,1,0:T(8,128)(2,1)} %bitcast.3), calls=%async_computation | async-start | bytes 2097152 | tf_op jit(solution)/shard_map/all_to_all | solution.py:244
  6.8 11.1 %copy.5 = bf16[8,125,4000]{2,1,0:T(8,128)(2,1)} copy(bf16[8,125,4000]{2,0,1:T(8,128)(2,1)} %param.4) | data formatting | bytes 16000000 | tf_op args[1]
  18.0 6.0 %fusion = (bf16[4,125,4000]{2,1,0:T(8,128)(2,1)}, bf16[4,125,4000]{2,1,0:T(8,128)(2,1)}) fusion(bf16[8,125,4000]{2,1,0:T(8,128)(2,1)} %copy.5), kind=kLoop, calls=%fused_computation.1 | loop fusion | bytes 16000000 | tf_op jit(solution)/shard_map/slice | solution.py:247
  24.0 2.2 %copy-done.1 = bf16[4,125,4000]{2,1,0:T(8,128)(2,1)S(1)} copy-done((bf16[4,125,4000]{2,1,0:T(8,128)(2,1)S(1)}, bf16[4,125,4000]{2,1,0:T(8,128)(2,1)}, u32[]{:S(2)}) %copy-start.1) | copy-done | bytes 4000024
  26.2 1.6 shard_map.38
  28.3 1.6 shard_map.41
  30.0 1.6 collective-permute-start.4
  31.6 1.6 shard_map.47
  33.2 2.0 %collective-permute-start.13 = (s16[2064,256]{1,0:T(8,128)(2,1)S(1)}, s16[2064,256]{1,0:T(8,128)(2,1)S(1)}, u32[]{:S(2)}, u32[]{:S(2)}) collective-permute-start(s16[2064,256]{1,0:T(8,128)(2,1)S(1)} %shard_map.47), channel_id=1, source_target_pairs={{0,8},{8,16},{16,24},{24,0},{32,40},{40,48},{48,56},{56,32},{64,72... | collective-permute-start | bytes 3170312 | tf_op jit(solution)/shard_map/ppermute | solution.py:250
  35.2 1.6 shard_map.50
  36.8 2.2 %collective-permute-start.16 = (s16[2064,256]{1,0:T(8,128)(2,1)S(1)}, s16[2064,256]{1,0:T(8,128)(2,1)S(1)}, u32[]{:S(2)}, u32[]{:S(2)}) collective-permute-start(s16[2064,256]{1,0:T(8,128)(2,1)S(1)} %shard_map.50), channel_id=1, source_target_pairs={{0,24},{8,0},{16,8},{24,16},{32,56},{40,32},{48,40},{56,48},{64,88... | collective-permute-start | bytes 3170312 | tf_op jit(solution)/shard_map/ppermute | solution.py:250
  39.0 2.0 %shard_map.37 = s16[2064,256]{1,0:T(8,128)(2,1)S(1)} custom-call(s32[10]{0:T(128)S(1)} %pad_add_fusion.at_ref, bf16[8,8,2,32,125]{4,3,2,1,0:T(8,128)(2,1)S(1)} %all-to-all-done.four_ref, bf16[4,125,4000]{2,1,0:T(8,128)(2,1)S(1)} %copy-done.1, bf16[4,125,4000]{2,1,0:T(8,128)(2,1)S(1)} %copy-done.1, bf16[4,125,4000]{2,1,0:T(8,128)(2,1)S(1)} %copy-done.1, ...), custom_call_target="tpu_custom_call" | custom-call | tf_op jit(solution)/shard_map/pallas_call | solution.py:184
  41.0 1.1 collective-permute-start
  42.1 2.0 %shard_map.40 = s16[2064,256]{1,0:T(8,128)(2,1)S(1)} custom-call(s32[10]{0:T(128)S(1)} %pad_add_fusion.at_ref, bf16[8,8,2,32,125]{4,3,2,1,0:T(8,128)(2,1)S(1)} %all-to-all-done.four_ref, bf16[4,125,4000]{2,1,0:T(8,128)(2,1)S(1)} %copy-done.1, bf16[4,125,4000]{2,1,0:T(8,128)(2,1)S(1)} %copy-done.1, bf16[4,125,4000]{2,1,0:T(8,128)(2,1)S(1)} %copy-done.1, ...), custom_call_target="tpu_custom_call" | custom-call | tf_op jit(solution)/shard_map/pallas_call | solution.py:184
  44.0 9.6 %collective-permute-done.1.rest_12_ = s16[2064,256]{1,0:T(8,128)(2,1)S(1)} collective-permute-done((s16[2064,256]{1,0:T(8,128)(2,1)S(1)}, s16[2064,256]{1,0:T(8,128)(2,1)S(1)}, u32[]{:S(2)}, u32[]{:S(2)}) %collective-permute-start.1) | collective-permute-done | bytes 1056800 | tf_op jit(solution)/shard_map/ppermute | solution.py:250
  53.6 1.7 %collective-permute-start.3 = (s16[2064,256]{1,0:T(8,128)(2,1)S(1)}, s16[2064,256]{1,0:T(8,128)(2,1)S(1)}, u32[]{:S(2)}, u32[]{:S(2)}) collective-permute-start(s16[2064,256]{1,0:T(8,128)(2,1)S(1)} %shard_map.40), channel_id=1, source_target_pairs={{0,32},{8,40},{16,48},{24,56},{32,64},{40,72},{48,80},{56,88},{64,... | collective-permute-start | bytes 3170312 | tf_op jit(solution)/shard_map/ppermute | solution.py:250
  55.3 2.1 %shard_map.39 = s16[2064,256]{1,0:T(8,128)(2,1)S(1)} custom-call(s32[10]{0:T(128)S(1)} %pad_add_fusion.at_ref, bf16[8,8,2,32,125]{4,3,2,1,0:T(8,128)(2,1)S(1)} %all-to-all-done.four_ref, bf16[4,125,4000]{2,1,0:T(8,128)(2,1)S(1)} %copy-done.1, bf16[4,125,4000]{2,1,0:T(8,128)(2,1)S(1)} %copy-done.1, bf16[4,125,4000]{2,1,0:T(8,128)(2,1)S(1)} %copy-done.1, ...), custom_call_target="tpu_custom_call" | custom-call | tf_op jit(solution)/shard_map/pallas_call | solution.py:184
  57.7 2.1 %shard_map.42 = s16[2064,256]{1,0:T(8,128)(2,1)S(1)} custom-call(s32[10]{0:T(128)S(1)} %pad_add_fusion.at_ref, bf16[8,8,2,32,125]{4,3,2,1,0:T(8,128)(2,1)S(1)} %all-to-all-done.four_ref, bf16[4,125,4000]{2,1,0:T(8,128)(2,1)S(1)} %copy-done.1, bf16[4,125,4000]{2,1,0:T(8,128)(2,1)S(1)} %copy-done.1, bf16[4,125,4000]{2,1,0:T(8,128)(2,1)S(1)} %copy-done.1, ...), custom_call_target="tpu_custom_call" | custom-call | tf_op jit(solution)/shard_map/pallas_call | solution.py:184
  59.8 1.0 collective-permute-done.13.rest_12_
  61.6 2.0 %shard_map.46 = s16[2064,256]{1,0:T(8,128)(2,1)S(1)} custom-call(s32[10]{0:T(128)S(1)} %pad_add_fusion.at_ref, bf16[8,8,2,32,125]{4,3,2,1,0:T(8,128)(2,1)S(1)} %all-to-all-done.four_ref, bf16[4,125,4000]{2,1,0:T(8,128)(2,1)S(1)} %copy-done, bf16[4,125,4000]{2,1,0:T(8,128)(2,1)S(1)} %copy-done, bf16[4,125,4000]{2,1,0:T(8,128)(2,1)S(1)} %copy-done, ...), custom_call_target="tpu_custom_call" | custom-call | tf_op jit(solution)/shard_map/pallas_call | solution.py:184
  63.6 4.1 %collective-permute-start.12 = (s16[2064,256]{1,0:T(8,128)(2,1)S(1)}, s16[2064,256]{1,0:T(8,128)(2,1)S(1)}, u32[]{:S(2)}, u32[]{:S(2)}) collective-permute-start(s16[2064,256]{1,0:T(8,128)(2,1)S(1)} %shard_map.46), channel_id=1, source_target_pairs={{0,24},{8,0},{16,8},{24,16},{32,56},{40,32},{48,40},{56,48},{64,88... | collective-permute-start | bytes 3170312 | tf_op jit(solution)/shard_map/ppermute | solution.py:250
  67.7 2.0 %shard_map.49 = s16[2064,256]{1,0:T(8,128)(2,1)S(1)} custom-call(s32[10]{0:T(128)S(1)} %pad_add_fusion.at_ref, bf16[8,8,2,32,125]{4,3,2,1,0:T(8,128)(2,1)S(1)} %all-to-all-done.four_ref, bf16[4,125,4000]{2,1,0:T(8,128)(2,1)S(1)} %copy-done, bf16[4,125,4000]{2,1,0:T(8,128)(2,1)S(1)} %copy-done, bf16[4,125,4000]{2,1,0:T(8,128)(2,1)S(1)} %copy-done, ...), custom_call_target="tpu_custom_call" | custom-call | tf_op jit(solution)/shard_map/pallas_call | solution.py:184
  69.7 2.1 %shard_map.48 = s16[2064,256]{1,0:T(8,128)(2,1)S(1)} custom-call(s32[10]{0:T(128)S(1)} %pad_add_fusion.at_ref, bf16[8,8,2,32,125]{4,3,2,1,0:T(8,128)(2,1)S(1)} %all-to-all-done.four_ref, bf16[4,125,4000]{2,1,0:T(8,128)(2,1)S(1)} %copy-done, bf16[4,125,4000]{2,1,0:T(8,128)(2,1)S(1)} %copy-done, bf16[4,125,4000]{2,1,0:T(8,128)(2,1)S(1)} %copy-done, ...), custom_call_target="tpu_custom_call" | custom-call | tf_op jit(solution)/shard_map/pallas_call | solution.py:184
  71.8 2.1 %shard_map.51 = s16[2064,256]{1,0:T(8,128)(2,1)S(1)} custom-call(s32[10]{0:T(128)S(1)} %pad_add_fusion.at_ref, bf16[8,8,2,32,125]{4,3,2,1,0:T(8,128)(2,1)S(1)} %all-to-all-done.four_ref, bf16[4,125,4000]{2,1,0:T(8,128)(2,1)S(1)} %copy-done, bf16[4,125,4000]{2,1,0:T(8,128)(2,1)S(1)} %copy-done, bf16[4,125,4000]{2,1,0:T(8,128)(2,1)S(1)} %copy-done, ...), custom_call_target="tpu_custom_call" | custom-call | tf_op jit(solution)/shard_map/pallas_call | solution.py:184
  73.9 6.2 %collective-permute-done.rest_3_.rest_4_.rest_5_ = s16[2064,256]{1,0:T(8,128)(2,1)S(1)} collective-permute-done((s16[2064,256]{1,0:T(8,128)(2,1)S(1)}, s16[2064,256]{1,0:T(8,128)(2,1)S(1)}, u32[]{:S(2)}, u32[]{:S(2)}) %collective-permute-start) | collective-permute-done | bytes 1056800 | tf_op jit(solution)/shard_map/ppermute | solution.py:250
  80.1 1.9 %collective-permute-start.15 = (s16[2064,256]{1,0:T(8,128)(2,1)S(1)}, s16[2064,256]{1,0:T(8,128)(2,1)S(1)}, u32[]{:S(2)}, u32[]{:S(2)}) collective-permute-start(s16[2064,256]{1,0:T(8,128)(2,1)S(1)} %shard_map.49), channel_id=1, source_target_pairs={{0,8},{8,16},{16,24},{24,0},{32,40},{40,48},{48,56},{56,32},{64,72... | collective-permute-start | bytes 3170312 | tf_op jit(solution)/shard_map/ppermute | solution.py:250
  82.0 1.9 %collective-permute-start.14 = (s16[2064,256]{1,0:T(8,128)(2,1)S(1)}, s16[2064,256]{1,0:T(8,128)(2,1)S(1)}, u32[]{:S(2)}, u32[]{:S(2)}) collective-permute-start(s16[2064,256]{1,0:T(8,128)(2,1)S(1)} %shard_map.48), channel_id=1, source_target_pairs={{0,8},{8,16},{16,24},{24,0},{32,40},{40,48},{48,56},{56,32},{64,72... | collective-permute-start | bytes 3170312 | tf_op jit(solution)/shard_map/ppermute | solution.py:250
  83.9 17.2 %collective-permute-done.2.rest_6_.rest_7_.rest_8_ = s16[2064,256]{1,0:T(8,128)(2,1)S(1)} collective-permute-done((s16[2064,256]{1,0:T(8,128)(2,1)S(1)}, s16[2064,256]{1,0:T(8,128)(2,1)S(1)}, u32[]{:S(2)}, u32[]{:S(2)}) %collective-permute-start.2) | collective-permute-done | bytes 1056800 | tf_op jit(solution)/shard_map/ppermute | solution.py:250
  101.1 4.0 %collective-permute-start.17 = (s16[2064,256]{1,0:T(8,128)(2,1)S(1)}, s16[2064,256]{1,0:T(8,128)(2,1)S(1)}, u32[]{:S(2)}, u32[]{:S(2)}) collective-permute-start(s16[2064,256]{1,0:T(8,128)(2,1)S(1)} %shard_map.51), channel_id=1, source_target_pairs={{0,24},{8,0},{16,8},{24,16},{32,56},{40,32},{48,40},{56,48},{64,88... | collective-permute-start | bytes 3170312 | tf_op jit(solution)/shard_map/ppermute | solution.py:250
  105.2 1.4 shard_map.44
  106.7 3.2 %collective-permute-start.8 = (s16[528,256]{1,0:T(8,128)(2,1)S(1)}, s16[528,256]{1,0:T(8,128)(2,1)S(1)}, u32[]{:S(2)}, u32[]{:S(2)}) collective-permute-start(s16[528,256]{1,0:T(8,128)(2,1)S(1)} %get-tuple-element.19), channel_id=1, source_target_pairs={{0,24},{8,0},{16,8},{24,16},{32,56},{40,32},{48,40},{56,48},{64,88... | collective-permute-start | bytes 811016 | tf_op jit(solution)/shard_map/ppermute | solution.py:250
  109.9 21.1 %collective-permute-done.14.rest_6_.rest_7_.rest_8_.rest_28_.rest_29_.rest_30_ = s16[2064,256]{1,0:T(8,128)(2,1)S(1)} collective-permute-done((s16[2064,256]{1,0:T(8,128)(2,1)S(1)}, s16[2064,256]{1,0:T(8,128)(2,1)S(1)}, u32[]{:S(2)}, u32[]{:S(2)}) %collective-permute-start.14) | collective-permute-done | bytes 1056800 | tf_op jit(solution)/shard_map/ppermute | solution.py:250
  131.0 1.4 shard_map.53
  132.4 0.9 collective-permute-start.19
  133.3 1.2 collective-permute-start.20
  134.5 1.4 shard_map.43
  135.9 2.6 %collective-permute-start.6 = (s16[528,256]{1,0:T(8,128)(2,1)S(1)}, s16[528,256]{1,0:T(8,128)(2,1)S(1)}, u32[]{:S(2)}, u32[]{:S(2)}) collective-permute-start(s16[528,256]{1,0:T(8,128)(2,1)S(1)} %get-tuple-element.17), channel_id=1, source_target_pairs={{0,24},{8,0},{16,8},{24,16},{32,56},{40,32},{48,40},{56,48},{64,88... | collective-permute-start | bytes 811016 | tf_op jit(solution)/shard_map/ppermute | solution.py:250
  138.4 1.4 shard_map.52
  140.0 1.6 shard_map.45
  141.7 3.3 %collective-permute-start.22 = (s16[528,256]{1,0:T(8,128)(2,1)S(1)}, s16[528,256]{1,0:T(8,128)(2,1)S(1)}, u32[]{:S(2)}, u32[]{:S(2)}) collective-permute-start(s16[528,256]{1,0:T(8,128)(2,1)S(1)} %get-tuple-element.27), channel_id=1, source_target_pairs={{0,32},{8,40},{16,48},{24,56},{32,64},{40,72},{48,80},{56,88},{64,... | collective-permute-start | bytes 811016 | tf_op jit(solution)/shard_map/ppermute | solution.py:250
  145.0 1.6 shard_map.54
  146.6 3.3 %collective-permute-start.11 = (s16[528,256]{1,0:T(8,128)(2,1)S(1)}, s16[528,256]{1,0:T(8,128)(2,1)S(1)}, u32[]{:S(2)}, u32[]{:S(2)}) collective-permute-start(s16[528,256]{1,0:T(8,128)(2,1)S(1)} %get-tuple-element.22), channel_id=1, source_target_pairs={{0,24},{8,0},{16,8},{24,16},{32,56},{40,32},{48,40},{56,48},{64,88... | collective-permute-start | bytes 811016 | tf_op jit(solution)/shard_map/ppermute | solution.py:250
  149.9 2.0 %collective-permute-start.21 = (s16[528,256]{1,0:T(8,128)(2,1)S(1)}, s16[528,256]{1,0:T(8,128)(2,1)S(1)}, u32[]{:S(2)}, u32[]{:S(2)}) collective-permute-start(s16[528,256]{1,0:T(8,128)(2,1)S(1)} %get-tuple-element.26), channel_id=1, source_target_pairs={{0,32},{8,40},{16,48},{24,56},{32,64},{40,72},{48,80},{56,88},{64,... | collective-permute-start | bytes 811016 | tf_op jit(solution)/shard_map/ppermute | solution.py:250
  152.7 1.2 collective-permute-done.11.rest_21_
  153.9 2.5 %collective-permute-done.21.rest_32_ = s16[528,256]{1,0:T(8,128)(2,1)S(1)} collective-permute-done((s16[528,256]{1,0:T(8,128)(2,1)S(1)}, s16[528,256]{1,0:T(8,128)(2,1)S(1)}, u32[]{:S(2)}, u32[]{:S(2)}) %collective-permute-start.21) | collective-permute-done | bytes 270368 | tf_op jit(solution)/shard_map/ppermute | solution.py:250
  156.4 3.2 %collective-permute-done.23.rest_43_ = s16[528,256]{1,0:T(8,128)(2,1)S(1)} collective-permute-done((s16[528,256]{1,0:T(8,128)(2,1)S(1)}, s16[528,256]{1,0:T(8,128)(2,1)S(1)}, u32[]{:S(2)}, u32[]{:S(2)}) %collective-permute-start.23) | collective-permute-done | bytes 270368 | tf_op jit(solution)/shard_map/ppermute | solution.py:250
  159.6 4.4 %shard_map.55 = f32[250,8,256]{2,1,0:T(8,128)} custom-call(s32[10]{0:T(128)S(1)} %pad_add_fusion.at_ref, bf16[8,8,2,32,125]{4,3,2,1,0:T(8,128)(2,1)S(1)} %all-to-all-done.four_ref, bf16[4,125,4000]{2,1,0:T(8,128)(2,1)S(1)} %copy-done.2, bf16[4,125,4000]{2,1,0:T(8,128)(2,1)S(1)} %copy-done.2, bf16[4,125,4000]{2,1,0:T(8,128)(2,1)S(1)} %copy-done.2, ...), custom_call_target="tpu_custom_call" | custom-call | tf_op jit(solution)/shard_map/pallas_call | solution.py:184
  (33 shorter events, 2.9 us)
Async XLA Ops:
  2.3 21.7 %all-to-all-start = ((bf16[8,8,2,32,125]{4,3,2,1,0:T(8,128)(2,1)}), bf16[8,8,2,32,125]{4,3,2,1,0:T(8,128)(2,1)S(1)}, u32[]{:S(2)}, u32[]{:S(2)}) async-start(bf16[8,8,2,32,125]{4,3,2,1,0:T(8,128)(2,1)} %bitcast.3), calls=%async_computation | async-start | bytes 2097152 | tf_op jit(solution)/shard_map/all_to_all | solution.py:244
  6.8 11.1 %copy-start.3 = (s32[8]{0:T(128)S(1)}, s32[8]{0:T(128)}, u32[]{:S(2)}) copy-start(s32[8]{0:T(128)} %param.5) | copy-start | bytes 100
  24.0 2.2 %copy-start.1 = (bf16[4,125,4000]{2,1,0:T(8,128)(2,1)S(1)}, bf16[4,125,4000]{2,1,0:T(8,128)(2,1)}, u32[]{:S(2)}) copy-start(bf16[4,125,4000]{2,1,0:T(8,128)(2,1)} %get-tuple-element.30.rest_0_.rest_1_.rest_2_.rest_3_.rest_4_.rest_5_.rest_6_.rest_7_.rest_8_.rest_9_.rest_10_.rest_11_.rest_12_.rest_13_) | copy-start | bytes 12000004
  27.8 25.8 %collective-permute-start.1 = (s16[2064,256]{1,0:T(8,128)(2,1)S(1)}, s16[2064,256]{1,0:T(8,128)(2,1)S(1)}, u32[]{:S(2)}, u32[]{:S(2)}) collective-permute-start(s16[2064,256]{1,0:T(8,128)(2,1)S(1)} %shard_map.38), channel_id=1, source_target_pairs={{0,32},{8,40},{16,48},{24,56},{32,64},{40,72},{48,80},{56,88},{64,... | collective-permute-start | bytes 3170312 | tf_op jit(solution)/shard_map/ppermute | solution.py:250
  28.3 3.2 %copy-start = (bf16[4,125,4000]{2,1,0:T(8,128)(2,1)S(1)}, bf16[4,125,4000]{2,1,0:T(8,128)(2,1)}, u32[]{:S(2)}) copy-start(bf16[4,125,4000]{2,1,0:T(8,128)(2,1)} %get-tuple-element.29.rest_0_.rest_1_.rest_2_.rest_3_.rest_4_.rest_5_.rest_6_.rest_7_.rest_8_.rest_9_.rest_10_.rest_11_.rest_12_.rest_22_.rest_23_.rest_24_.rest_33_.rest_34_.rest_35_) | copy-start | bytes 12000004
  30.0 27.5 %collective-permute-start.4 = (s16[2064,256]{1,0:T(8,128)(2,1)S(1)}, s16[2064,256]{1,0:T(8,128)(2,1)S(1)}, u32[]{:S(2)}, u32[]{:S(2)}) collective-permute-start(s16[2064,256]{1,0:T(8,128)(2,1)S(1)} %shard_map.41), channel_id=1, source_target_pairs={{0,96},{8,104},{16,112},{24,120},{32,0},{40,8},{48,16},{56,24},{64... | collective-permute-start | bytes 3170312 | tf_op jit(solution)/shard_map/ppermute | solution.py:250
  33.2 27.6 %collective-permute-start.13 = (s16[2064,256]{1,0:T(8,128)(2,1)S(1)}, s16[2064,256]{1,0:T(8,128)(2,1)S(1)}, u32[]{:S(2)}, u32[]{:S(2)}) collective-permute-start(s16[2064,256]{1,0:T(8,128)(2,1)S(1)} %shard_map.47), channel_id=1, source_target_pairs={{0,8},{8,16},{16,24},{24,0},{32,40},{40,48},{48,56},{56,32},{64,72... | collective-permute-start | bytes 3170312 | tf_op jit(solution)/shard_map/ppermute | solution.py:250
  36.8 26.8 %collective-permute-start.16 = (s16[2064,256]{1,0:T(8,128)(2,1)S(1)}, s16[2064,256]{1,0:T(8,128)(2,1)S(1)}, u32[]{:S(2)}, u32[]{:S(2)}) collective-permute-start(s16[2064,256]{1,0:T(8,128)(2,1)S(1)} %shard_map.50), channel_id=1, source_target_pairs={{0,24},{8,0},{16,8},{24,16},{32,56},{40,32},{48,40},{56,48},{64,88... | collective-permute-start | bytes 3170312 | tf_op jit(solution)/shard_map/ppermute | solution.py:250
  41.0 39.1 %collective-permute-start = (s16[2064,256]{1,0:T(8,128)(2,1)S(1)}, s16[2064,256]{1,0:T(8,128)(2,1)S(1)}, u32[]{:S(2)}, u32[]{:S(2)}) collective-permute-start(s16[2064,256]{1,0:T(8,128)(2,1)S(1)} %shard_map.37), channel_id=1, source_target_pairs={{0,96},{8,104},{16,112},{24,120},{32,0},{40,8},{48,16},{56,24},{64... | collective-permute-start | bytes 3170312 | tf_op jit(solution)/shard_map/ppermute | solution.py:250
  53.6 28.4 %collective-permute-start.3 = (s16[2064,256]{1,0:T(8,128)(2,1)S(1)}, s16[2064,256]{1,0:T(8,128)(2,1)S(1)}, u32[]{:S(2)}, u32[]{:S(2)}) collective-permute-start(s16[2064,256]{1,0:T(8,128)(2,1)S(1)} %shard_map.40), channel_id=1, source_target_pairs={{0,32},{8,40},{16,48},{24,56},{32,64},{40,72},{48,80},{56,88},{64,... | collective-permute-start | bytes 3170312 | tf_op jit(solution)/shard_map/ppermute | solution.py:250
  57.4 43.7 %collective-permute-start.2 = (s16[2064,256]{1,0:T(8,128)(2,1)S(1)}, s16[2064,256]{1,0:T(8,128)(2,1)S(1)}, u32[]{:S(2)}, u32[]{:S(2)}) collective-permute-start(s16[2064,256]{1,0:T(8,128)(2,1)S(1)} %shard_map.39), channel_id=1, source_target_pairs={{0,32},{8,40},{16,48},{24,56},{32,64},{40,72},{48,80},{56,88},{64,... | collective-permute-start | bytes 3170312 | tf_op jit(solution)/shard_map/ppermute | solution.py:250
  60.8 44.4 %collective-permute-start.5 = (s16[2064,256]{1,0:T(8,128)(2,1)S(1)}, s16[2064,256]{1,0:T(8,128)(2,1)S(1)}, u32[]{:S(2)}, u32[]{:S(2)}) collective-permute-start(s16[2064,256]{1,0:T(8,128)(2,1)S(1)} %shard_map.42), channel_id=1, source_target_pairs={{0,96},{8,104},{16,112},{24,120},{32,0},{40,8},{48,16},{56,24},{64... | collective-permute-start | bytes 3170312 | tf_op jit(solution)/shard_map/ppermute | solution.py:250
  63.6 43.0 %collective-permute-start.12 = (s16[2064,256]{1,0:T(8,128)(2,1)S(1)}, s16[2064,256]{1,0:T(8,128)(2,1)S(1)}, u32[]{:S(2)}, u32[]{:S(2)}) collective-permute-start(s16[2064,256]{1,0:T(8,128)(2,1)S(1)} %shard_map.46), channel_id=1, source_target_pairs={{0,24},{8,0},{16,8},{24,16},{32,56},{40,32},{48,40},{56,48},{64,88... | collective-permute-start | bytes 3170312 | tf_op jit(solution)/shard_map/ppermute | solution.py:250
  80.1 29.8 %collective-permute-start.15 = (s16[2064,256]{1,0:T(8,128)(2,1)S(1)}, s16[2064,256]{1,0:T(8,128)(2,1)S(1)}, u32[]{:S(2)}, u32[]{:S(2)}) collective-permute-start(s16[2064,256]{1,0:T(8,128)(2,1)S(1)} %shard_map.49), channel_id=1, source_target_pairs={{0,8},{8,16},{16,24},{24,0},{32,40},{40,48},{48,56},{56,32},{64,72... | collective-permute-start | bytes 3170312 | tf_op jit(solution)/shard_map/ppermute | solution.py:250
  82.0 48.9 %collective-permute-start.14 = (s16[2064,256]{1,0:T(8,128)(2,1)S(1)}, s16[2064,256]{1,0:T(8,128)(2,1)S(1)}, u32[]{:S(2)}, u32[]{:S(2)}) collective-permute-start(s16[2064,256]{1,0:T(8,128)(2,1)S(1)} %shard_map.48), channel_id=1, source_target_pairs={{0,8},{8,16},{16,24},{24,0},{32,40},{40,48},{48,56},{56,32},{64,72... | collective-permute-start | bytes 3170312 | tf_op jit(solution)/shard_map/ppermute | solution.py:250
  101.1 29.8 %collective-permute-start.17 = (s16[2064,256]{1,0:T(8,128)(2,1)S(1)}, s16[2064,256]{1,0:T(8,128)(2,1)S(1)}, u32[]{:S(2)}, u32[]{:S(2)}) collective-permute-start(s16[2064,256]{1,0:T(8,128)(2,1)S(1)} %shard_map.51), channel_id=1, source_target_pairs={{0,24},{8,0},{16,8},{24,16},{32,56},{40,32},{48,40},{56,48},{64,88... | collective-permute-start | bytes 3170312 | tf_op jit(solution)/shard_map/ppermute | solution.py:250
  106.6 33.3 %collective-permute-start.7 = (s16[528,256]{1,0:T(8,128)(2,1)S(1)}, s16[528,256]{1,0:T(8,128)(2,1)S(1)}, u32[]{:S(2)}, u32[]{:S(2)}) collective-permute-start(s16[528,256]{1,0:T(8,128)(2,1)S(1)} %get-tuple-element.18), channel_id=1, source_target_pairs={{0,8},{8,16},{16,24},{24,0},{32,40},{40,48},{48,56},{56,32},{64,72... | collective-permute-start | bytes 811016 | tf_op jit(solution)/shard_map/ppermute | solution.py:250
  106.7 33.3 %collective-permute-start.8 = (s16[528,256]{1,0:T(8,128)(2,1)S(1)}, s16[528,256]{1,0:T(8,128)(2,1)S(1)}, u32[]{:S(2)}, u32[]{:S(2)}) collective-permute-start(s16[528,256]{1,0:T(8,128)(2,1)S(1)} %get-tuple-element.19), channel_id=1, source_target_pairs={{0,24},{8,0},{16,8},{24,16},{32,56},{40,32},{48,40},{56,48},{64,88... | collective-permute-start | bytes 811016 | tf_op jit(solution)/shard_map/ppermute | solution.py:250
  132.4 9.3 %collective-permute-start.19 = (s16[528,256]{1,0:T(8,128)(2,1)S(1)}, s16[528,256]{1,0:T(8,128)(2,1)S(1)}, u32[]{:S(2)}, u32[]{:S(2)}) collective-permute-start(s16[528,256]{1,0:T(8,128)(2,1)S(1)} %get-tuple-element.24), channel_id=1, source_target_pairs={{0,32},{8,40},{16,48},{24,56},{32,64},{40,72},{48,80},{56,88},{64,... | collective-permute-start | bytes 811016 | tf_op jit(solution)/shard_map/ppermute | solution.py:250
  133.3 11.7 %collective-permute-start.20 = (s16[528,256]{1,0:T(8,128)(2,1)S(1)}, s16[528,256]{1,0:T(8,128)(2,1)S(1)}, u32[]{:S(2)}, u32[]{:S(2)}) collective-permute-start(s16[528,256]{1,0:T(8,128)(2,1)S(1)} %get-tuple-element.25), channel_id=1, source_target_pairs={{0,96},{8,104},{16,112},{24,120},{32,0},{40,8},{48,16},{56,24},{64... | collective-permute-start | bytes 811016 | tf_op jit(solution)/shard_map/ppermute | solution.py:250
  135.9 10.7 %collective-permute-start.6 = (s16[528,256]{1,0:T(8,128)(2,1)S(1)}, s16[528,256]{1,0:T(8,128)(2,1)S(1)}, u32[]{:S(2)}, u32[]{:S(2)}) collective-permute-start(s16[528,256]{1,0:T(8,128)(2,1)S(1)} %get-tuple-element.17), channel_id=1, source_target_pairs={{0,24},{8,0},{16,8},{24,16},{32,56},{40,32},{48,40},{56,48},{64,88... | collective-permute-start | bytes 811016 | tf_op jit(solution)/shard_map/ppermute | solution.py:250
  139.9 10.0 %collective-permute-start.10 = (s16[528,256]{1,0:T(8,128)(2,1)S(1)}, s16[528,256]{1,0:T(8,128)(2,1)S(1)}, u32[]{:S(2)}, u32[]{:S(2)}) collective-permute-start(s16[528,256]{1,0:T(8,128)(2,1)S(1)} %get-tuple-element.21), channel_id=1, source_target_pairs={{0,8},{8,16},{16,24},{24,0},{32,40},{40,48},{48,56},{56,32},{64,72... | collective-permute-start | bytes 811016 | tf_op jit(solution)/shard_map/ppermute | solution.py:250
  140.0 12.0 %collective-permute-start.18 = (s16[528,256]{1,0:T(8,128)(2,1)S(1)}, s16[528,256]{1,0:T(8,128)(2,1)S(1)}, u32[]{:S(2)}, u32[]{:S(2)}) collective-permute-start(s16[528,256]{1,0:T(8,128)(2,1)S(1)} %get-tuple-element.23), channel_id=1, source_target_pairs={{0,96},{8,104},{16,112},{24,120},{32,0},{40,8},{48,16},{56,24},{64... | collective-permute-start | bytes 811016 | tf_op jit(solution)/shard_map/ppermute | solution.py:250
  141.7 10.3 %collective-permute-start.22 = (s16[528,256]{1,0:T(8,128)(2,1)S(1)}, s16[528,256]{1,0:T(8,128)(2,1)S(1)}, u32[]{:S(2)}, u32[]{:S(2)}) collective-permute-start(s16[528,256]{1,0:T(8,128)(2,1)S(1)} %get-tuple-element.27), channel_id=1, source_target_pairs={{0,32},{8,40},{16,48},{24,56},{32,64},{40,72},{48,80},{56,88},{64,... | collective-permute-start | bytes 811016 | tf_op jit(solution)/shard_map/ppermute | solution.py:250
  145.0 7.7 %collective-permute-start.9 = (s16[528,256]{1,0:T(8,128)(2,1)S(1)}, s16[528,256]{1,0:T(8,128)(2,1)S(1)}, u32[]{:S(2)}, u32[]{:S(2)}) collective-permute-start(s16[528,256]{1,0:T(8,128)(2,1)S(1)} %get-tuple-element.20), channel_id=1, source_target_pairs={{0,8},{8,16},{16,24},{24,0},{32,40},{40,48},{48,56},{56,32},{64,72... | collective-permute-start | bytes 811016 | tf_op jit(solution)/shard_map/ppermute | solution.py:250
  145.0 14.6 %copy-start.2 = (bf16[4,125,4000]{2,1,0:T(8,128)(2,1)S(1)}, bf16[4,125,4000]{2,1,0:T(8,128)(2,1)}, u32[]{:S(2)}) copy-start(bf16[4,125,4000]{2,1,0:T(8,128)(2,1)} %get-tuple-element.30.rest_0_.rest_1_.rest_2_.rest_3_.rest_4_.rest_5_.rest_6_.rest_7_.rest_8_.rest_9_.rest_10_.rest_11_.rest_12_.rest_13_) | copy-start | bytes 12000004
  146.6 7.3 %collective-permute-start.11 = (s16[528,256]{1,0:T(8,128)(2,1)S(1)}, s16[528,256]{1,0:T(8,128)(2,1)S(1)}, u32[]{:S(2)}, u32[]{:S(2)}) collective-permute-start(s16[528,256]{1,0:T(8,128)(2,1)S(1)} %get-tuple-element.22), channel_id=1, source_target_pairs={{0,24},{8,0},{16,8},{24,16},{32,56},{40,32},{48,40},{56,48},{64,88... | collective-permute-start | bytes 811016 | tf_op jit(solution)/shard_map/ppermute | solution.py:250
  149.9 6.5 %collective-permute-start.21 = (s16[528,256]{1,0:T(8,128)(2,1)S(1)}, s16[528,256]{1,0:T(8,128)(2,1)S(1)}, u32[]{:S(2)}, u32[]{:S(2)}) collective-permute-start(s16[528,256]{1,0:T(8,128)(2,1)S(1)} %get-tuple-element.26), channel_id=1, source_target_pairs={{0,32},{8,40},{16,48},{24,56},{32,64},{40,72},{48,80},{56,88},{64,... | collective-permute-start | bytes 811016 | tf_op jit(solution)/shard_map/ppermute | solution.py:250
  151.9 7.7 %collective-permute-start.23 = (s16[528,256]{1,0:T(8,128)(2,1)S(1)}, s16[528,256]{1,0:T(8,128)(2,1)S(1)}, u32[]{:S(2)}, u32[]{:S(2)}) collective-permute-start(s16[528,256]{1,0:T(8,128)(2,1)S(1)} %get-tuple-element.28), channel_id=1, source_target_pairs={{0,96},{8,104},{16,112},{24,120},{32,0},{40,8},{48,16},{56,24},{64... | collective-permute-start | bytes 811016 | tf_op jit(solution)/shard_map/ppermute | solution.py:250

commit v2 on v1

--- a/solution.py
+++ b/solution.py
@@ -147,14 +147,17 @@
         store_coded(rest[pair - 2], 1, value, False)
 
 
-def last_kernel(at_ref, four_ref, *rest, width):
+def last_kernel(at_ref, four_ref, *rest, start, width):
     out_ref = rest[-1]
     per = TILES + 2 * (PAIR + 1) + 2
-    for group in range(GROUPS):
-        refs = rest[group * per : (group + 1) * per]
+    if start:
+        out_ref[:, : start * PAIR] = rest[2 * per][...]
+    for pair in range(2):
+        refs = rest[pair * per : (pair + 1) * per]
         for slot in range(PAIR):
-            k = group * PAIR + slot
-            total = summed(at_ref, four_ref, k, slot, at_ref[2 + k], refs, 1 - group // 2, 0, width)
+            at = pair * PAIR + slot
+            k = start * PAIR + at
+            total = summed(at_ref, four_ref, at, slot, at_ref[2 + k], refs, 1 - start // 2, 0, width)
             out_ref[:, k, :] = total.T[:width]
 
 
@@ -215,13 +218,15 @@
     return call(body, at, operands, specs, [((PAIR * ROWS + TAIL, LANES), jnp.int16)] * 2)
 
 
-def last(at, four, tab, firsts, states, width):
-    specs, operands = [whole(four)], [four]
-    for group in range(GROUPS):
-        more, arrays = second_operands(group, 1 - group // 2, 0, tab, firsts[group], states[group], width)
+def last(start, at, four, tab, firsts, states, others, width):
+    specs, operands = [four_of(four, 2 * PAIR, start // 2)], [four]
+    for group in (start, start + 1):
+        more, arrays = second_operands(group, 1 - start // 2, 0, tab, firsts[group], states[group], width)
         specs, operands = specs + more, operands + arrays
-    out = ((width, GROUPS * PAIR, ROWS), jnp.float32)
-    return call(functools.partial(last_kernel, width=width), at, operands, specs, [out], 24)[0]
+    specs, operands = specs + [whole(other) for other in others], operands + others
+    out = ((width, (start + 2) * PAIR, ROWS), jnp.float32)
+    body = functools.partial(last_kernel, start=start, width=width)
+    return call(body, at, operands, specs, [out], 20)[0]
 
 
 def ring(axis, sign):
@@ -244,7 +249,9 @@
     four = lax.all_to_all(split, "wave", split_axis=0, concat_axis=0, tiled=True)
     at = jnp.concatenate([jnp.stack([me // SIDE, me % SIDE]).astype(jnp.int32), wavenums])
     table = lax.optimization_barrier(with_layout_constraint(table, Layout((0, 1, 2))))
-    table = (table[: 2 * PAIR], table[2 * PAIR :])
+    half = table[: 2 * PAIR]
+    table, half = lax.optimization_barrier((table, half))
+    table = (half, table[2 * PAIR :])
 
     def send(array, axis, sign):
         return lax.ppermute(array, "lat", ring(axis, sign))
@@ -273,7 +280,9 @@
     got_near = [send(near[g // 2][g % 2], 1 - g // 2, -ways[g]) for g in every]
     both = [second(2 * h, (1, -1), of[h], ((got_far[p],), (got_far[q],))) for h, (p, q) in enumerate(halves)]
     got_both = [send(both[g // 2][g % 2], 1 - g // 2, ways[g]) for g in every]
-    return last(at, four, table, firsts, list(zip(got_near, got_both)), width)
+    states = list(zip(got_near, got_both))
+    part = last(0, at, four, table, firsts, states, [], width)
+    return last(2, at, four, table, firsts, states, [part], width)
 
 
 def solution(mesh):

time: 164 us -> 163 us (level)
  the two profiles are of different devices: /device:TPU:6 before, /device:TPU:8 now
where the time goes in v2:
time: 163 us; the launch traced here: 162 us
  waiting for transfers between devices  60.3 us (37%)
  starting transfers between devices  44.1 us (27%)
  Pallas kernels  36.6 us (22%)
  local copies, waits for them, and re-layouts  20.9 us (13%)
    ppermute x24, waiting for transfers between devices, send(): return lax.ppermute(array, 'lat', ring(axis, sign))  60.3 us
    ppermute x24, starting transfers between devices, send(): return lax.ppermute(array, 'lat', ring(axis, sign))  39.2 us
    pallas_call x20, Pallas kernels, call(): pl.pallas_call(body, grid_spec=pltpu.PrefetchScalarGridSpec(num_scalar_pr...  36.6 us
    unnamed x11, local copies, waits for them, and re-layouts  13.6 us
    all_to_all x1, starting transfers between devices, per_device(): lax.all_to_all(split, 'wave', split_axis=0, concat_axis=0, tiled=True)  4.92 us
    slice x1, local copies, waits for them, and re-layouts, per_device(): half = table[:2 * PAIR]  4.69 us
  transfers between devices with their start and end apart: 25, of which 11 were waited for; matrix products, arithmetic and copies ran while one was open for 10% of the time, Pallas kernels for 20%

profile of v2, /device:TPU:8, one launch (start us, length us, event | category | flops | bytes accessed | tf_op | source)
XLA Modules:
  0.0 162.3 jit_solution(16650355458014127790)
XLA Ops:
  0.0 2.3 %copy.4 = bf16[64,2,32,125]{3,2,1,0:T(8,128)(2,1)} copy(bf16[64,2,32,125]{3,2,0,1:T(8,128)(2,1)} %bitcast.6) | data formatting | bytes 2048000 | tf_op jit(solution)/shard_map/transpose | solution.py:247
  2.3 4.9 %all-to-all-start = ((bf16[8,8,2,32,125]{4,3,2,1,0:T(8,128)(2,1)}), bf16[8,8,2,32,125]{4,3,2,1,0:T(8,128)(2,1)S(1)}, u32[]{:S(2)}, u32[]{:S(2)}) async-start(bf16[8,8,2,32,125]{4,3,2,1,0:T(8,128)(2,1)} %bitcast.3), calls=%async_computation | async-start | bytes 2097152 | tf_op jit(solution)/shard_map/all_to_all | solution.py:249
  7.3 11.1 %copy.5 = bf16[8,125,4000]{2,1,0:T(8,128)(2,1)} copy(bf16[8,125,4000]{2,0,1:T(8,128)(2,1)} %param.4) | data formatting | bytes 16000000 | tf_op args[1]
  18.4 4.7 %slice.8.rest_0_.rest_1_.rest_2_.rest_3_.rest_4_.rest_5_.rest_6_.rest_7_.rest_8_.rest_9_.rest_10_.rest_11_.rest_12_.rest_13_ = bf16[4,125,4000]{2,1,0:T(8,128)(2,1)} slice(bf16[8,125,4000]{2,1,0:T(8,128)(2,1)} %copy.5), slice={[0:4], [0:125], [0:4000]} | slice | bytes 8000000 | tf_op jit(solution)/shard_map/slice | solution.py:252
  23.1 2.2 %copy-done = bf16[4,125,4000]{2,1,0:T(8,128)(2,1)S(1)} copy-done((bf16[4,125,4000]{2,1,0:T(8,128)(2,1)S(1)}, bf16[4,125,4000]{2,1,0:T(8,128)(2,1)}, u32[]{:S(2)}) %copy-start) | copy-done | bytes 4000024
  25.3 1.6 shard_map.47
  27.0 1.6 collective-permute-start.13
  28.5 1.6 shard_map.50
  30.1 1.8 %collective-permute-start.16 = (s16[2064,256]{1,0:T(8,128)(2,1)S(1)}, s16[2064,256]{1,0:T(8,128)(2,1)S(1)}, u32[]{:S(2)}, u32[]{:S(2)}) collective-permute-start(s16[2064,256]{1,0:T(8,128)(2,1)S(1)} %shard_map.50), channel_id=1, source_target_pairs={{0,96},{8,104},{16,112},{24,120},{32,0},{40,8},{48,16},{56,24},{64... | collective-permute-start | bytes 3170312 | tf_op jit(solution)/shard_map/ppermute | solution.py:257
  32.2 1.6 shard_map.41
  33.8 4.1 %collective-permute-start.4 = (s16[2064,256]{1,0:T(8,128)(2,1)S(1)}, s16[2064,256]{1,0:T(8,128)(2,1)S(1)}, u32[]{:S(2)}, u32[]{:S(2)}) collective-permute-start(s16[2064,256]{1,0:T(8,128)(2,1)S(1)} %shard_map.41), channel_id=1, source_target_pairs={{0,24},{8,0},{16,8},{24,16},{32,56},{40,32},{48,40},{56,48},{64,88... | collective-permute-start | bytes 3170312 | tf_op jit(solution)/shard_map/ppermute | solution.py:257
  38.0 1.6 shard_map.38
  40.1 2.0 %shard_map.46 = s16[2064,256]{1,0:T(8,128)(2,1)S(1)} custom-call(s32[10]{0:T(128)S(1)} %pad_add_fusion.at_ref, bf16[8,8,2,32,125]{4,3,2,1,0:T(8,128)(2,1)S(1)} %all-to-all-done.four_ref, bf16[4,125,4000]{2,1,0:T(8,128)(2,1)S(1)} %copy-done.1, bf16[4,125,4000]{2,1,0:T(8,128)(2,1)S(1)} %copy-done.1, bf16[4,125,4000]{2,1,0:T(8,128)(2,1)S(1)} %copy-done.1, ...), custom_call_target="tpu_custom_call" | custom-call | tf_op jit(solution)/shard_map/pallas_call | solution.py:187
  42.1 1.6 collective-permute-start.12
  43.7 2.0 %shard_map.49 = s16[2064,256]{1,0:T(8,128)(2,1)S(1)} custom-call(s32[10]{0:T(128)S(1)} %pad_add_fusion.at_ref, bf16[8,8,2,32,125]{4,3,2,1,0:T(8,128)(2,1)S(1)} %all-to-all-done.four_ref, bf16[4,125,4000]{2,1,0:T(8,128)(2,1)S(1)} %copy-done.1, bf16[4,125,4000]{2,1,0:T(8,128)(2,1)S(1)} %copy-done.1, bf16[4,125,4000]{2,1,0:T(8,128)(2,1)S(1)} %copy-done.1, ...), custom_call_target="tpu_custom_call" | custom-call | tf_op jit(solution)/shard_map/pallas_call | solution.py:187
  45.7 7.9 %collective-permute-done.13.rest_12_ = s16[2064,256]{1,0:T(8,128)(2,1)S(1)} collective-permute-done((s16[2064,256]{1,0:T(8,128)(2,1)S(1)}, s16[2064,256]{1,0:T(8,128)(2,1)S(1)}, u32[]{:S(2)}, u32[]{:S(2)}) %collective-permute-start.13) | collective-permute-done | bytes 1056800 | tf_op jit(solution)/shard_map/ppermute | solution.py:257
  53.9 2.1 %shard_map.48 = s16[2064,256]{1,0:T(8,128)(2,1)S(1)} custom-call(s32[10]{0:T(128)S(1)} %pad_add_fusion.at_ref, bf16[8,8,2,32,125]{4,3,2,1,0:T(8,128)(2,1)S(1)} %all-to-all-done.four_ref, bf16[4,125,4000]{2,1,0:T(8,128)(2,1)S(1)} %copy-done.1, bf16[4,125,4000]{2,1,0:T(8,128)(2,1)S(1)} %copy-done.1, bf16[4,125,4000]{2,1,0:T(8,128)(2,1)S(1)} %copy-done.1, ...), custom_call_target="tpu_custom_call" | custom-call | tf_op jit(solution)/shard_map/pallas_call | solution.py:187
  56.4 1.5 collective-permute-start.14
  57.9 2.1 %shard_map.51 = s16[2064,256]{1,0:T(8,128)(2,1)S(1)} custom-call(s32[10]{0:T(128)S(1)} %pad_add_fusion.at_ref, bf16[8,8,2,32,125]{4,3,2,1,0:T(8,128)(2,1)S(1)} %all-to-all-done.four_ref, bf16[4,125,4000]{2,1,0:T(8,128)(2,1)S(1)} %copy-done.1, bf16[4,125,4000]{2,1,0:T(8,128)(2,1)S(1)} %copy-done.1, bf16[4,125,4000]{2,1,0:T(8,128)(2,1)S(1)} %copy-done.1, ...), custom_call_target="tpu_custom_call" | custom-call | tf_op jit(solution)/shard_map/pallas_call | solution.py:187
  60.3 1.6 collective-permute-start.17
  61.8 2.0 %shard_map.40 = s16[2064,256]{1,0:T(8,128)(2,1)S(1)} custom-call(s32[10]{0:T(128)S(1)} %pad_add_fusion.at_ref, bf16[8,8,2,32,125]{4,3,2,1,0:T(8,128)(2,1)S(1)} %all-to-all-done.four_ref, bf16[4,125,4000]{2,1,0:T(8,128)(2,1)S(1)} %slice.7.rest_0_.rest_1_.rest_2_.rest_3_.rest_4_.rest_5_.rest_6_.rest_7_.rest_8_.rest_9_.rest_10_.rest_11_.rest_12_.rest_13_, ...), custom_call_target="tpu_custom_call" | custom-call | tf_op jit(solution)/shard_map/pallas_call | solution.py:187
  63.8 1.7 %collective-permute-done.1.rest_12_ = s16[2064,256]{1,0:T(8,128)(2,1)S(1)} collective-permute-done((s16[2064,256]{1,0:T(8,128)(2,1)S(1)}, s16[2064,256]{1,0:T(8,128)(2,1)S(1)}, u32[]{:S(2)}, u32[]{:S(2)}) %collective-permute-start.1) | collective-permute-done | bytes 1056800 | tf_op jit(solution)/shard_map/ppermute | solution.py:257
  65.8 2.0 %shard_map.37 = s16[2064,256]{1,0:T(8,128)(2,1)S(1)} custom-call(s32[10]{0:T(128)S(1)} %pad_add_fusion.at_ref, bf16[8,8,2,32,125]{4,3,2,1,0:T(8,128)(2,1)S(1)} %all-to-all-done.four_ref, bf16[4,125,4000]{2,1,0:T(8,128)(2,1)S(1)} %slice.7.rest_0_.rest_1_.rest_2_.rest_3_.rest_4_.rest_5_.rest_6_.rest_7_.rest_8_.rest_9_.rest_10_.rest_11_.rest_12_.rest_13_, ...), custom_call_target="tpu_custom_call" | custom-call | tf_op jit(solution)/shard_map/pallas_call | solution.py:187
  67.7 2.1 %shard_map.42 = s16[2064,256]{1,0:T(8,128)(2,1)S(1)} custom-call(s32[10]{0:T(128)S(1)} %pad_add_fusion.at_ref, bf16[8,8,2,32,125]{4,3,2,1,0:T(8,128)(2,1)S(1)} %all-to-all-done.four_ref, bf16[4,125,4000]{2,1,0:T(8,128)(2,1)S(1)} %slice.7.rest_0_.rest_1_.rest_2_.rest_3_.rest_4_.rest_5_.rest_6_.rest_7_.rest_8_.rest_9_.rest_10_.rest_11_.rest_12_.rest_13_, ...), custom_call_target="tpu_custom_call" | custom-call | tf_op jit(solution)/shard_map/pallas_call | solution.py:187
  69.8 2.1 %shard_map.39 = s16[2064,256]{1,0:T(8,128)(2,1)S(1)} custom-call(s32[10]{0:T(128)S(1)} %pad_add_fusion.at_ref, bf16[8,8,2,32,125]{4,3,2,1,0:T(8,128)(2,1)S(1)} %all-to-all-done.four_ref, bf16[4,125,4000]{2,1,0:T(8,128)(2,1)S(1)} %slice.7.rest_0_.rest_1_.rest_2_.rest_3_.rest_4_.rest_5_.rest_6_.rest_7_.rest_8_.rest_9_.rest_10_.rest_11_.rest_12_.rest_13_, ...), custom_call_target="tpu_custom_call" | custom-call | tf_op jit(solution)/shard_map/pallas_call | solution.py:187
  71.9 7.2 %collective-permute-done.12.rest_3_.rest_4_.rest_5_ = s16[2064,256]{1,0:T(8,128)(2,1)S(1)} collective-permute-done((s16[2064,256]{1,0:T(8,128)(2,1)S(1)}, s16[2064,256]{1,0:T(8,128)(2,1)S(1)}, u32[]{:S(2)}, u32[]{:S(2)}) %collective-permute-start.12) | collective-permute-done | bytes 1056800 | tf_op jit(solution)/shard_map/ppermute | solution.py:257
  79.0 4.0 %collective-permute-start = (s16[2064,256]{1,0:T(8,128)(2,1)S(1)}, s16[2064,256]{1,0:T(8,128)(2,1)S(1)}, u32[]{:S(2)}, u32[]{:S(2)}) collective-permute-start(s16[2064,256]{1,0:T(8,128)(2,1)S(1)} %shard_map.37), channel_id=1, source_target_pairs={{0,24},{8,0},{16,8},{24,16},{32,56},{40,32},{48,40},{56,48},{64,88... | collective-permute-start | bytes 3170312 | tf_op jit(solution)/shard_map/ppermute | solution.py:257
  83.1 2.0 %collective-permute-start.5 = (s16[2064,256]{1,0:T(8,128)(2,1)S(1)}, s16[2064,256]{1,0:T(8,128)(2,1)S(1)}, u32[]{:S(2)}, u32[]{:S(2)}) collective-permute-start(s16[2064,256]{1,0:T(8,128)(2,1)S(1)} %shard_map.42), channel_id=1, source_target_pairs={{0,24},{8,0},{16,8},{24,16},{32,56},{40,32},{48,40},{56,48},{64,88... | collective-permute-start | bytes 3170312 | tf_op jit(solution)/shard_map/ppermute | solution.py:257
  85.0 16.9 %collective-permute-done.14.rest_6_.rest_7_.rest_8_ = s16[2064,256]{1,0:T(8,128)(2,1)S(1)} collective-permute-done((s16[2064,256]{1,0:T(8,128)(2,1)S(1)}, s16[2064,256]{1,0:T(8,128)(2,1)S(1)}, u32[]{:S(2)}, u32[]{:S(2)}) %collective-permute-start.14) | collective-permute-done | bytes 1056800 | tf_op jit(solution)/shard_map/ppermute | solution.py:257
  101.9 1.9 %collective-permute-start.2 = (s16[2064,256]{1,0:T(8,128)(2,1)S(1)}, s16[2064,256]{1,0:T(8,128)(2,1)S(1)}, u32[]{:S(2)}, u32[]{:S(2)}) collective-permute-start(s16[2064,256]{1,0:T(8,128)(2,1)S(1)} %shard_map.39), channel_id=1, source_target_pairs={{0,8},{8,16},{16,24},{24,0},{32,40},{40,48},{48,56},{56,32},{64,72... | collective-permute-start | bytes 3170312 | tf_op jit(solution)/shard_map/ppermute | solution.py:257
  103.9 1.4 shard_map.53
  105.3 2.0 %collective-permute-start.19 = (s16[528,256]{1,0:T(8,128)(2,1)S(1)}, s16[528,256]{1,0:T(8,128)(2,1)S(1)}, u32[]{:S(2)}, u32[]{:S(2)}) collective-permute-start(s16[528,256]{1,0:T(8,128)(2,1)S(1)} %get-tuple-element.28), channel_id=1, source_target_pairs={{0,8},{8,16},{16,24},{24,0},{32,40},{40,48},{48,56},{56,32},{64,72... | collective-permute-start | bytes 811016 | tf_op jit(solution)/shard_map/ppermute | solution.py:257
  107.3 1.3 collective-permute-start.20
  108.6 20.6 %collective-permute-done.5.rest_15_.rest_16_.rest_17_.rest_18_.rest_19_ = s16[2064,256]{1,0:T(8,128)(2,1)S(1)} collective-permute-done((s16[2064,256]{1,0:T(8,128)(2,1)S(1)}, s16[2064,256]{1,0:T(8,128)(2,1)S(1)}, u32[]{:S(2)}, u32[]{:S(2)}) %collective-permute-start.5) | collective-permute-done | bytes 1056800 | tf_op jit(solution)/shard_map/ppermute | solution.py:257
  130.2 1.4 shard_map.44
  132.4 2.7 %collective-permute-start.8 = (s16[528,256]{1,0:T(8,128)(2,1)S(1)}, s16[528,256]{1,0:T(8,128)(2,1)S(1)}, u32[]{:S(2)}, u32[]{:S(2)}) collective-permute-start(s16[528,256]{1,0:T(8,128)(2,1)S(1)} %get-tuple-element.22), channel_id=1, source_target_pairs={{0,96},{8,104},{16,112},{24,120},{32,0},{40,8},{48,16},{56,24},{64... | collective-permute-start | bytes 811016 | tf_op jit(solution)/shard_map/ppermute | solution.py:257
  135.1 1.4 shard_map.52
  136.5 2.8 %collective-permute-start.18 = (s16[528,256]{1,0:T(8,128)(2,1)S(1)}, s16[528,256]{1,0:T(8,128)(2,1)S(1)}, u32[]{:S(2)}, u32[]{:S(2)}) collective-permute-start(s16[528,256]{1,0:T(8,128)(2,1)S(1)} %get-tuple-element.27), channel_id=1, source_target_pairs={{0,24},{8,0},{16,8},{24,16},{32,56},{40,32},{48,40},{56,48},{64,88... | collective-permute-start | bytes 811016 | tf_op jit(solution)/shard_map/ppermute | solution.py:257
  139.4 1.6 shard_map.54
  141.0 1.4 shard_map.43
  142.8 3.0 %collective-permute-start.6 = (s16[528,256]{1,0:T(8,128)(2,1)S(1)}, s16[528,256]{1,0:T(8,128)(2,1)S(1)}, u32[]{:S(2)}, u32[]{:S(2)}) collective-permute-start(s16[528,256]{1,0:T(8,128)(2,1)S(1)} %get-tuple-element.20), channel_id=1, source_target_pairs={{0,96},{8,104},{16,112},{24,120},{32,0},{40,8},{48,16},{56,24},{64... | collective-permute-start | bytes 811016 | tf_op jit(solution)/shard_map/ppermute | solution.py:257
  145.8 1.6 shard_map.45
  147.4 3.3 %collective-permute-start.23 = (s16[528,256]{1,0:T(8,128)(2,1)S(1)}, s16[528,256]{1,0:T(8,128)(2,1)S(1)}, u32[]{:S(2)}, u32[]{:S(2)}) collective-permute-start(s16[528,256]{1,0:T(8,128)(2,1)S(1)} %get-tuple-element.32), channel_id=1, source_target_pairs={{0,24},{8,0},{16,8},{24,16},{32,56},{40,32},{48,40},{56,48},{64,88... | collective-permute-start | bytes 811016 | tf_op jit(solution)/shard_map/ppermute | solution.py:257
  151.2 1.5 collective-permute-start.9
  152.7 1.9 %collective-permute-done.23.rest_21_ = s16[528,256]{1,0:T(8,128)(2,1)S(1)} collective-permute-done((s16[528,256]{1,0:T(8,128)(2,1)S(1)}, s16[528,256]{1,0:T(8,128)(2,1)S(1)}, u32[]{:S(2)}, u32[]{:S(2)}) %collective-permute-start.23) | collective-permute-done | bytes 270368 | tf_op jit(solution)/shard_map/ppermute | solution.py:257
  154.7 1.9 %shard_map.55.rest_22_ = f32[250,4,256]{2,1,0:T(4,128)S(1)} custom-call(s32[10]{0:T(128)S(1)} %pad_add_fusion.at_ref, bf16[8,8,2,32,125]{4,3,2,1,0:T(8,128)(2,1)S(1)} %all-to-all-done.four_ref, bf16[4,125,4000]{2,1,0:T(8,128)(2,1)S(1)} %copy-done.1, bf16[4,125,4000]{2,1,0:T(8,128)(2,1)S(1)} %copy-done.1, bf16[4,125,4000]{2,1,0:T(8,128)(2,1)S(1)} %copy-done.1, ...), custom_call_target="tpu_custom_call" | custom-call | tf_op jit(solution)/shard_map/pallas_call | solution.py:187
  157.2 1.7 %collective-permute-done.9.rest_10_ = s16[528,256]{1,0:T(8,128)(2,1)S(1)} collective-permute-done((s16[528,256]{1,0:T(8,128)(2,1)S(1)}, s16[528,256]{1,0:T(8,128)(2,1)S(1)}, u32[]{:S(2)}, u32[]{:S(2)}) %collective-permute-start.9) | collective-permute-done | bytes 270368 | tf_op jit(solution)/shard_map/ppermute | solution.py:257
  158.9 3.4 %shard_map.56 = f32[250,8,256]{2,1,0:T(8,128)} custom-call(s32[10]{0:T(128)S(1)} %pad_add_fusion.at_ref, bf16[8,8,2,32,125]{4,3,2,1,0:T(8,128)(2,1)S(1)} %all-to-all-done.four_ref, bf16[4,125,4000]{2,1,0:T(8,128)(2,1)S(1)} %slice.7.rest_0_.rest_1_.rest_2_.rest_3_.rest_4_.rest_5_.rest_6_.rest_7_.rest_8_.rest_9_.rest_10_.rest_11_.rest_12_.rest_13_, ...), custom_call_target="tpu_custom_call" | custom-call | tf_op jit(solution)/shard_map/pallas_call | solution.py:187
  (38 shorter events, 5.6 us)
Async XLA Ops:
  2.3 20.8 %all-to-all-start = ((bf16[8,8,2,32,125]{4,3,2,1,0:T(8,128)(2,1)}), bf16[8,8,2,32,125]{4,3,2,1,0:T(8,128)(2,1)S(1)}, u32[]{:S(2)}, u32[]{:S(2)}) async-start(bf16[8,8,2,32,125]{4,3,2,1,0:T(8,128)(2,1)} %bitcast.3), calls=%async_computation | async-start | bytes 2097152 | tf_op jit(solution)/shard_map/all_to_all | solution.py:249
  18.4 4.7 %copy-start.2 = (s32[8]{0:T(128)S(1)}, s32[8]{0:T(128)}, u32[]{:S(2)}) copy-start(s32[8]{0:T(128)} %param.5) | copy-start | bytes 100
  23.1 2.2 %copy-start = (bf16[4,125,4000]{2,1,0:T(8,128)(2,1)S(1)}, bf16[4,125,4000]{2,1,0:T(8,128)(2,1)}, u32[]{:S(2)}) copy-start(bf16[4,125,4000]{2,1,0:T(8,128)(2,1)} %slice.8.rest_0_.rest_1_.rest_2_.rest_3_.rest_4_.rest_5_.rest_6_.rest_7_.rest_8_.rest_9_.rest_10_.rest_11_.rest_12_.rest_13_) | copy-start | bytes 12000004
  25.3 6.6 %slice-start = ((s8[8388608]{0:T(1024)(128)(4,1)}), s8[4194304]{0:T(1024)(128)(4,1)S(1)}, s32[]{:S(2)}) async-start(s8[8388608]{0:T(1024)(128)(4,1)} %bitcast.4), calls=%async_computation.1 | async-start | bytes 8388608
  26.9 5.0 %slice-start.1 = ((s8[8388608]{0:T(1024)(128)(4,1)}), s8[4194304]{0:T(1024)(128)(4,1)S(1)}, s32[]{:S(2)}) async-start(s8[8388608]{0:T(1024)(128)(4,1)} %bitcast.4), calls=%async_computation.2 | async-start | bytes 8388608
  27.0 26.6 %collective-permute-start.13 = (s16[2064,256]{1,0:T(8,128)(2,1)S(1)}, s16[2064,256]{1,0:T(8,128)(2,1)S(1)}, u32[]{:S(2)}, u32[]{:S(2)}) collective-permute-start(s16[2064,256]{1,0:T(8,128)(2,1)S(1)} %shard_map.47), channel_id=1, source_target_pairs={{0,32},{8,40},{16,48},{24,56},{32,64},{40,72},{48,80},{56,88},{64,... | collective-permute-start | bytes 3170312 | tf_op jit(solution)/shard_map/ppermute | solution.py:257
  30.1 26.3 %collective-permute-start.16 = (s16[2064,256]{1,0:T(8,128)(2,1)S(1)}, s16[2064,256]{1,0:T(8,128)(2,1)S(1)}, u32[]{:S(2)}, u32[]{:S(2)}) collective-permute-start(s16[2064,256]{1,0:T(8,128)(2,1)S(1)} %shard_map.50), channel_id=1, source_target_pairs={{0,96},{8,104},{16,112},{24,120},{32,0},{40,8},{48,16},{56,24},{64... | collective-permute-start | bytes 3170312 | tf_op jit(solution)/shard_map/ppermute | solution.py:257
  33.8 26.4 %collective-permute-start.4 = (s16[2064,256]{1,0:T(8,128)(2,1)S(1)}, s16[2064,256]{1,0:T(8,128)(2,1)S(1)}, u32[]{:S(2)}, u32[]{:S(2)}) collective-permute-start(s16[2064,256]{1,0:T(8,128)(2,1)S(1)} %shard_map.41), channel_id=1, source_target_pairs={{0,24},{8,0},{16,8},{24,16},{32,56},{40,32},{48,40},{56,48},{64,88... | collective-permute-start | bytes 3170312 | tf_op jit(solution)/shard_map/ppermute | solution.py:257
  38.0 2.2 %copy-start.1 = (bf16[4,125,4000]{2,1,0:T(8,128)(2,1)S(1)}, bf16[4,125,4000]{2,1,0:T(8,128)(2,1)}, u32[]{:S(2)}) copy-start(bf16[4,125,4000]{2,1,0:T(8,128)(2,1)} %slice.8.rest_0_.rest_1_.rest_2_.rest_3_.rest_4_.rest_5_.rest_6_.rest_7_.rest_8_.rest_9_.rest_10_.rest_11_.rest_12_.rest_13_) | copy-start | bytes 12000004
  39.6 26.0 %collective-permute-start.1 = (s16[2064,256]{1,0:T(8,128)(2,1)S(1)}, s16[2064,256]{1,0:T(8,128)(2,1)S(1)}, u32[]{:S(2)}, u32[]{:S(2)}) collective-permute-start(s16[2064,256]{1,0:T(8,128)(2,1)S(1)} %shard_map.38), channel_id=1, source_target_pairs={{0,8},{8,16},{16,24},{24,0},{32,40},{40,48},{48,56},{56,32},{64,72... | collective-permute-start | bytes 3170312 | tf_op jit(solution)/shard_map/ppermute | solution.py:257
  42.1 36.9 %collective-permute-start.12 = (s16[2064,256]{1,0:T(8,128)(2,1)S(1)}, s16[2064,256]{1,0:T(8,128)(2,1)S(1)}, u32[]{:S(2)}, u32[]{:S(2)}) collective-permute-start(s16[2064,256]{1,0:T(8,128)(2,1)S(1)} %shard_map.46), channel_id=1, source_target_pairs={{0,96},{8,104},{16,112},{24,120},{32,0},{40,8},{48,16},{56,24},{64... | collective-permute-start | bytes 3170312 | tf_op jit(solution)/shard_map/ppermute | solution.py:257
  53.6 29.5 %collective-permute-start.15 = (s16[2064,256]{1,0:T(8,128)(2,1)S(1)}, s16[2064,256]{1,0:T(8,128)(2,1)S(1)}, u32[]{:S(2)}, u32[]{:S(2)}) collective-permute-start(s16[2064,256]{1,0:T(8,128)(2,1)S(1)} %shard_map.49), channel_id=1, source_target_pairs={{0,32},{8,40},{16,48},{24,56},{32,64},{40,72},{48,80},{56,88},{64,... | collective-permute-start | bytes 3170312 | tf_op jit(solution)/shard_map/ppermute | solution.py:257
  56.4 45.5 %collective-permute-start.14 = (s16[2064,256]{1,0:T(8,128)(2,1)S(1)}, s16[2064,256]{1,0:T(8,128)(2,1)S(1)}, u32[]{:S(2)}, u32[]{:S(2)}) collective-permute-start(s16[2064,256]{1,0:T(8,128)(2,1)S(1)} %shard_map.48), channel_id=1, source_target_pairs={{0,32},{8,40},{16,48},{24,56},{32,64},{40,72},{48,80},{56,88},{64,... | collective-permute-start | bytes 3170312 | tf_op jit(solution)/shard_map/ppermute | solution.py:257
  60.3 43.6 %collective-permute-start.17 = (s16[2064,256]{1,0:T(8,128)(2,1)S(1)}, s16[2064,256]{1,0:T(8,128)(2,1)S(1)}, u32[]{:S(2)}, u32[]{:S(2)}) collective-permute-start(s16[2064,256]{1,0:T(8,128)(2,1)S(1)} %shard_map.51), channel_id=1, source_target_pairs={{0,96},{8,104},{16,112},{24,120},{32,0},{40,8},{48,16},{56,24},{64... | collective-permute-start | bytes 3170312 | tf_op jit(solution)/shard_map/ppermute | solution.py:257
  65.5 41.7 %collective-permute-start.3 = (s16[2064,256]{1,0:T(8,128)(2,1)S(1)}, s16[2064,256]{1,0:T(8,128)(2,1)S(1)}, u32[]{:S(2)}, u32[]{:S(2)}) collective-permute-start(s16[2064,256]{1,0:T(8,128)(2,1)S(1)} %shard_map.40), channel_id=1, source_target_pairs={{0,8},{8,16},{16,24},{24,0},{32,40},{40,48},{48,56},{56,32},{64,72... | collective-permute-start | bytes 3170312 | tf_op jit(solution)/shard_map/ppermute | solution.py:257
  79.0 29.5 %collective-permute-start = (s16[2064,256]{1,0:T(8,128)(2,1)S(1)}, s16[2064,256]{1,0:T(8,128)(2,1)S(1)}, u32[]{:S(2)}, u32[]{:S(2)}) collective-permute-start(s16[2064,256]{1,0:T(8,128)(2,1)S(1)} %shard_map.37), channel_id=1, source_target_pairs={{0,24},{8,0},{16,8},{24,16},{32,56},{40,32},{48,40},{56,48},{64,88... | collective-permute-start | bytes 3170312 | tf_op jit(solution)/shard_map/ppermute | solution.py:257
  83.1 46.1 %collective-permute-start.5 = (s16[2064,256]{1,0:T(8,128)(2,1)S(1)}, s16[2064,256]{1,0:T(8,128)(2,1)S(1)}, u32[]{:S(2)}, u32[]{:S(2)}) collective-permute-start(s16[2064,256]{1,0:T(8,128)(2,1)S(1)} %shard_map.42), channel_id=1, source_target_pairs={{0,24},{8,0},{16,8},{24,16},{32,56},{40,32},{48,40},{56,48},{64,88... | collective-permute-start | bytes 3170312 | tf_op jit(solution)/shard_map/ppermute | solution.py:257
  101.9 28.2 %collective-permute-start.2 = (s16[2064,256]{1,0:T(8,128)(2,1)S(1)}, s16[2064,256]{1,0:T(8,128)(2,1)S(1)}, u32[]{:S(2)}, u32[]{:S(2)}) collective-permute-start(s16[2064,256]{1,0:T(8,128)(2,1)S(1)} %shard_map.39), channel_id=1, source_target_pairs={{0,8},{8,16},{16,24},{24,0},{32,40},{40,48},{48,56},{56,32},{64,72... | collective-permute-start | bytes 3170312 | tf_op jit(solution)/shard_map/ppermute | solution.py:257
  105.3 34.1 %collective-permute-start.19 = (s16[528,256]{1,0:T(8,128)(2,1)S(1)}, s16[528,256]{1,0:T(8,128)(2,1)S(1)}, u32[]{:S(2)}, u32[]{:S(2)}) collective-permute-start(s16[528,256]{1,0:T(8,128)(2,1)S(1)} %get-tuple-element.28), channel_id=1, source_target_pairs={{0,8},{8,16},{16,24},{24,0},{32,40},{40,48},{48,56},{56,32},{64,72... | collective-permute-start | bytes 811016 | tf_op jit(solution)/shard_map/ppermute | solution.py:257
  107.3 32.1 %collective-permute-start.20 = (s16[528,256]{1,0:T(8,128)(2,1)S(1)}, s16[528,256]{1,0:T(8,128)(2,1)S(1)}, u32[]{:S(2)}, u32[]{:S(2)}) collective-permute-start(s16[528,256]{1,0:T(8,128)(2,1)S(1)} %get-tuple-element.29), channel_id=1, source_target_pairs={{0,24},{8,0},{16,8},{24,16},{32,56},{40,32},{48,40},{56,48},{64,88... | collective-permute-start | bytes 811016 | tf_op jit(solution)/shard_map/ppermute | solution.py:257
  131.6 10.9 %collective-permute-start.7 = (s16[528,256]{1,0:T(8,128)(2,1)S(1)}, s16[528,256]{1,0:T(8,128)(2,1)S(1)}, u32[]{:S(2)}, u32[]{:S(2)}) collective-permute-start(s16[528,256]{1,0:T(8,128)(2,1)S(1)} %get-tuple-element.21), channel_id=1, source_target_pairs={{0,32},{8,40},{16,48},{24,56},{32,64},{40,72},{48,80},{56,88},{64,... | collective-permute-start | bytes 811016 | tf_op jit(solution)/shard_map/ppermute | solution.py:257
  132.4 10.4 %collective-permute-start.8 = (s16[528,256]{1,0:T(8,128)(2,1)S(1)}, s16[528,256]{1,0:T(8,128)(2,1)S(1)}, u32[]{:S(2)}, u32[]{:S(2)}) collective-permute-start(s16[528,256]{1,0:T(8,128)(2,1)S(1)} %get-tuple-element.22), channel_id=1, source_target_pairs={{0,96},{8,104},{16,112},{24,120},{32,0},{40,8},{48,16},{56,24},{64... | collective-permute-start | bytes 811016 | tf_op jit(solution)/shard_map/ppermute | solution.py:257
  136.5 10.9 %collective-permute-start.18 = (s16[528,256]{1,0:T(8,128)(2,1)S(1)}, s16[528,256]{1,0:T(8,128)(2,1)S(1)}, u32[]{:S(2)}, u32[]{:S(2)}) collective-permute-start(s16[528,256]{1,0:T(8,128)(2,1)S(1)} %get-tuple-element.27), channel_id=1, source_target_pairs={{0,24},{8,0},{16,8},{24,16},{32,56},{40,32},{48,40},{56,48},{64,88... | collective-permute-start | bytes 811016 | tf_op jit(solution)/shard_map/ppermute | solution.py:257
  139.3 11.4 %collective-permute-start.22 = (s16[528,256]{1,0:T(8,128)(2,1)S(1)}, s16[528,256]{1,0:T(8,128)(2,1)S(1)}, u32[]{:S(2)}, u32[]{:S(2)}) collective-permute-start(s16[528,256]{1,0:T(8,128)(2,1)S(1)} %get-tuple-element.31), channel_id=1, source_target_pairs={{0,8},{8,16},{16,24},{24,0},{32,40},{40,48},{48,56},{56,32},{64,72... | collective-permute-start | bytes 811016 | tf_op jit(solution)/shard_map/ppermute | solution.py:257
  141.0 10.3 %collective-permute-start.21 = (s16[528,256]{1,0:T(8,128)(2,1)S(1)}, s16[528,256]{1,0:T(8,128)(2,1)S(1)}, u32[]{:S(2)}, u32[]{:S(2)}) collective-permute-start(s16[528,256]{1,0:T(8,128)(2,1)S(1)} %get-tuple-element.30), channel_id=1, source_target_pairs={{0,8},{8,16},{16,24},{24,0},{32,40},{40,48},{48,56},{56,32},{64,72... | collective-permute-start | bytes 811016 | tf_op jit(solution)/shard_map/ppermute | solution.py:257
  142.5 14.1 %collective-permute-start.10 = (s16[528,256]{1,0:T(8,128)(2,1)S(1)}, s16[528,256]{1,0:T(8,128)(2,1)S(1)}, u32[]{:S(2)}, u32[]{:S(2)}) collective-permute-start(s16[528,256]{1,0:T(8,128)(2,1)S(1)} %get-tuple-element.24), channel_id=1, source_target_pairs={{0,32},{8,40},{16,48},{24,56},{32,64},{40,72},{48,80},{56,88},{64,... | collective-permute-start | bytes 811016 | tf_op jit(solution)/shard_map/ppermute | solution.py:257
  142.8 13.7 %collective-permute-start.6 = (s16[528,256]{1,0:T(8,128)(2,1)S(1)}, s16[528,256]{1,0:T(8,128)(2,1)S(1)}, u32[]{:S(2)}, u32[]{:S(2)}) collective-permute-start(s16[528,256]{1,0:T(8,128)(2,1)S(1)} %get-tuple-element.20), channel_id=1, source_target_pairs={{0,96},{8,104},{16,112},{24,120},{32,0},{40,8},{48,16},{56,24},{64... | collective-permute-start | bytes 811016 | tf_op jit(solution)/shard_map/ppermute | solution.py:257
  147.4 7.3 %collective-permute-start.23 = (s16[528,256]{1,0:T(8,128)(2,1)S(1)}, s16[528,256]{1,0:T(8,128)(2,1)S(1)}, u32[]{:S(2)}, u32[]{:S(2)}) collective-permute-start(s16[528,256]{1,0:T(8,128)(2,1)S(1)} %get-tuple-element.32), channel_id=1, source_target_pairs={{0,24},{8,0},{16,8},{24,16},{32,56},{40,32},{48,40},{56,48},{64,88... | collective-permute-start | bytes 811016 | tf_op jit(solution)/shard_map/ppermute | solution.py:257
  150.7 6.5 %collective-permute-start.11 = (s16[528,256]{1,0:T(8,128)(2,1)S(1)}, s16[528,256]{1,0:T(8,128)(2,1)S(1)}, u32[]{:S(2)}, u32[]{:S(2)}) collective-permute-start(s16[528,256]{1,0:T(8,128)(2,1)S(1)} %get-tuple-element.25), channel_id=1, source_target_pairs={{0,96},{8,104},{16,112},{24,120},{32,0},{40,8},{48,16},{56,24},{64... | collective-permute-start | bytes 811016 | tf_op jit(solution)/shard_map/ppermute | solution.py:257
  151.2 7.7 %collective-permute-start.9 = (s16[528,256]{1,0:T(8,128)(2,1)S(1)}, s16[528,256]{1,0:T(8,128)(2,1)S(1)}, u32[]{:S(2)}, u32[]{:S(2)}) collective-permute-start(s16[528,256]{1,0:T(8,128)(2,1)S(1)} %get-tuple-element.23), channel_id=1, source_target_pairs={{0,32},{8,40},{16,48},{24,56},{32,64},{40,72},{48,80},{56,88},{64,... | collective-permute-start | bytes 811016 | tf_op jit(solution)/shard_map/ppermute | solution.py:257

commit v3 on v2

--- a/solution.py
+++ b/solution.py
@@ -134,17 +134,17 @@
     return total
 
 
-def second_kernel(at_ref, four_ref, *rest, axis, aheads, width, terms):
+def second_kernel(at_ref, four_ref, *rest, axis, jobs, width, terms):
     per = TILES + 2 * (PAIR + 1) + terms
-    for pair, ahead in enumerate(aheads):
-        refs = rest[pair * per : (pair + 1) * per]
+    for job, (pair, ahead) in enumerate(jobs):
+        refs = rest[job * per : (job + 1) * per]
 
         def value(slot, b):
             at = pair * PAIR + slot
             mval = at_ref[2 + (1 - axis) * 2 * PAIR + at]
             return summed(at_ref, four_ref, at, slot, mval, refs, axis, ahead, width)
 
-        store_coded(rest[pair - 2], 1, value, False)
+        store_coded(rest[job - len(jobs)], 1, value, False)
 
 
 def last_kernel(at_ref, four_ref, *rest, start, width):
@@ -208,14 +208,14 @@
     return call(body, at, operands, specs, [out])[0]
 
 
-def second_hop(start, aheads, at, four, tab, firsts, states, width):
+def second_hop(start, jobs, at, four, tab, firsts, states, width):
     axis = 1 - start // 2
     specs, operands = [four_of(four, 2 * PAIR, start // 2)], [four]
-    for pair, ahead in enumerate(aheads):
-        more, arrays = second_operands(start + pair, axis, ahead, tab, firsts[pair], states[pair], width)
+    for (pair, ahead), sums in zip(jobs, states):
+        more, arrays = second_operands(start + pair, axis, ahead, tab, firsts[pair], sums, width)
         specs, operands = specs + more, operands + arrays
-    body = functools.partial(second_kernel, axis=axis, aheads=aheads, width=width, terms=len(states[0]))
-    return call(body, at, operands, specs, [((PAIR * ROWS + TAIL, LANES), jnp.int16)] * 2)
+    body = functools.partial(second_kernel, axis=axis, jobs=jobs, width=width, terms=len(states[0]))
+    return call(body, at, operands, specs, [((PAIR * ROWS + TAIL, LANES), jnp.int16)] * len(jobs))
 
 
 def last(start, at, four, tab, firsts, states, others, width):
@@ -259,8 +259,8 @@
     def first(group, ahead, states):
         return first_hop(group, ahead, at, four, table, states, width)
 
-    def second(start, aheads, firsts, states):
-        return second_hop(start, aheads, at, four, table, firsts, states, width)
+    def second(start, jobs, firsts, states):
+        return second_hop(start, jobs, at, four, table, firsts, states, width)
 
     ways = [1 - 2 * (group % 2) for group in range(GROUPS)]
     every = range(GROUPS)
@@ -274,11 +274,11 @@
 
     halves = [(0, 1), (2, 3)]
     of = [(firsts[p], firsts[q]) for p, q in halves]
-    far = [second(2 * h, (2, 2), of[h], ((), ())) for h in range(2)]
-    got_far = [send(far[g // 2][g % 2], 1 - g // 2, ways[g]) for g in every]
-    near = [second(2 * h, (-1, 1), of[h], ((), ())) for h in range(2)]
-    got_near = [send(near[g // 2][g % 2], 1 - g // 2, -ways[g]) for g in every]
-    both = [second(2 * h, (1, -1), of[h], ((got_far[p],), (got_far[q],))) for h, (p, q) in enumerate(halves)]
+    jobs = ((0, 2), (1, 2), (0, -1), (1, 1))
+    alone = [second(2 * h, jobs, of[h], ((),) * 4) for h in range(2)]
+    got_far = [send(alone[g // 2][g % 2], 1 - g // 2, ways[g]) for g in every]
+    got_near = [send(alone[g // 2][2 + g % 2], 1 - g // 2, -ways[g]) for g in every]
+    both = [second(2 * h, ((0, 1), (1, -1)), of[h], ((got_far[p],), (got_far[q],))) for h, (p, q) in enumerate(halves)]
     got_both = [send(both[g // 2][g % 2], 1 - g // 2, ways[g]) for g in every]
     states = list(zip(got_near, got_both))
     part = last(0, at, four, table, firsts, states, [], width)

time: 163 us -> 163 us (level)
    pallas_call x20 -> x18, Pallas kernels: 36.6 us -> 35.5 us  [call(): pl.pallas_call(body, grid_spec=pltpu.PrefetchScalarGridSpec(num_scalar_pr...]
  transfers between devices with their start and end apart: 25 -> 25, of which waited for: 11 -> 12; matrix products, arithmetic and copies ran while one was open for 10% -> 10% of each run, Pallas kernels for 20% -> 19%
where the time goes in v3:
time: 163 us; the launch traced here: 162 us
  waiting for transfers between devices  61.5 us (38%)
  starting transfers between devices  44.1 us (27%)
  Pallas kernels  35.5 us (22%)
  local copies, waits for them, and re-layouts  21 us (13%)
    ppermute x24, waiting for transfers between devices, send(): return lax.ppermute(array, 'lat', ring(axis, sign))  61.5 us
    ppermute x24, starting transfers between devices, send(): return lax.ppermute(array, 'lat', ring(axis, sign))  39.1 us
    pallas_call x18, Pallas kernels, call(): pl.pallas_call(body, grid_spec=pltpu.PrefetchScalarGridSpec(num_scalar_pr...  35.5 us
    unnamed x11, local copies, waits for them, and re-layouts  13.6 us
    all_to_all x1, starting transfers between devices, per_device(): lax.all_to_all(split, 'wave', split_axis=0, concat_axis=0, tiled=True)  4.92 us
    slice x1, local copies, waits for them, and re-layouts, per_device(): half = table[:2 * PAIR]  4.7 us
  transfers between devices with their start and end apart: 25, of which 12 were waited for; matrix products, arithmetic and copies ran while one was open for 10% of the time, Pallas kernels for 19%

profile of v3, /device:TPU:8, one launch (start us, length us, event | category | flops | bytes accessed | tf_op | source)
XLA Modules:
  0.0 162.3 jit_solution(2027089158800587740)
XLA Ops:
  0.0 2.3 %copy.4 = bf16[64,2,32,125]{3,2,1,0:T(8,128)(2,1)} copy(bf16[64,2,32,125]{3,2,0,1:T(8,128)(2,1)} %bitcast.6) | data formatting | bytes 2048000 | tf_op jit(solution)/shard_map/transpose | solution.py:247
  2.3 4.9 %all-to-all-start = ((bf16[8,8,2,32,125]{4,3,2,1,0:T(8,128)(2,1)}), bf16[8,8,2,32,125]{4,3,2,1,0:T(8,128)(2,1)S(1)}, u32[]{:S(2)}, u32[]{:S(2)}) async-start(bf16[8,8,2,32,125]{4,3,2,1,0:T(8,128)(2,1)} %bitcast.3), calls=%async_computation | async-start | bytes 2097152 | tf_op jit(solution)/shard_map/all_to_all | solution.py:249
  7.3 11.1 %copy.5 = bf16[8,125,4000]{2,1,0:T(8,128)(2,1)} copy(bf16[8,125,4000]{2,0,1:T(8,128)(2,1)} %param.4) | data formatting | bytes 16000000 | tf_op args[1]
  18.4 4.7 %slice.8.rest_0_.rest_1_.rest_2_.rest_3_.rest_4_.rest_5_.rest_6_.rest_7_.rest_8_.rest_9_.rest_10_.rest_11_.rest_18_.rest_19_.rest_20_.rest_27_.rest_28_.rest_29_.rest_12_.rest_13_ = bf16[4,125,4000]{2,1,0:T(8,128)(2,1)} slice(bf16[8,125,4000]{2,1,0:T(8,128)(2,1)} %copy.5), slice={[0:4], [0:125], [0:4000]} | slice | bytes 8000000 | tf_op jit(solution)/shard_map/slice | solution.py:252
  23.2 2.2 %copy-done = bf16[4,125,4000]{2,1,0:T(8,128)(2,1)S(1)} copy-done((bf16[4,125,4000]{2,1,0:T(8,128)(2,1)S(1)}, bf16[4,125,4000]{2,1,0:T(8,128)(2,1)}, u32[]{:S(2)}) %copy-start) | copy-done | bytes 4000024
  25.4 1.6 shard_map.46
  27.0 1.6 collective-permute-start.13
  28.5 1.6 shard_map.49
  30.1 1.8 %collective-permute-start.16 = (s16[2064,256]{1,0:T(8,128)(2,1)S(1)}, s16[2064,256]{1,0:T(8,128)(2,1)S(1)}, u32[]{:S(2)}, u32[]{:S(2)}) collective-permute-start(s16[2064,256]{1,0:T(8,128)(2,1)S(1)} %shard_map.49), channel_id=1, source_target_pairs={{0,96},{8,104},{16,112},{24,120},{32,0},{40,8},{48,16},{56,24},{64... | collective-permute-start | bytes 3170312 | tf_op jit(solution)/shard_map/ppermute | solution.py:257
  32.2 1.6 shard_map.41
  33.9 4.1 %collective-permute-start.4 = (s16[2064,256]{1,0:T(8,128)(2,1)S(1)}, s16[2064,256]{1,0:T(8,128)(2,1)S(1)}, u32[]{:S(2)}, u32[]{:S(2)}) collective-permute-start(s16[2064,256]{1,0:T(8,128)(2,1)S(1)} %shard_map.41), channel_id=1, source_target_pairs={{0,24},{8,0},{16,8},{24,16},{32,56},{40,32},{48,40},{56,48},{64,88... | collective-permute-start | bytes 3170312 | tf_op jit(solution)/shard_map/ppermute | solution.py:257
  38.0 1.6 shard_map.38
  40.2 2.0 %shard_map.45 = s16[2064,256]{1,0:T(8,128)(2,1)S(1)} custom-call(s32[10]{0:T(128)S(1)} %pad_add_fusion.at_ref, bf16[8,8,2,32,125]{4,3,2,1,0:T(8,128)(2,1)S(1)} %all-to-all-done.four_ref, bf16[4,125,4000]{2,1,0:T(8,128)(2,1)S(1)} %copy-done.1, bf16[4,125,4000]{2,1,0:T(8,128)(2,1)S(1)} %copy-done.1, bf16[4,125,4000]{2,1,0:T(8,128)(2,1)S(1)} %copy-done.1, ...), custom_call_target="tpu_custom_call" | custom-call | tf_op jit(solution)/shard_map/pallas_call | solution.py:187
  42.2 1.6 %collective-permute-start.12 = (s16[2064,256]{1,0:T(8,128)(2,1)S(1)}, s16[2064,256]{1,0:T(8,128)(2,1)S(1)}, u32[]{:S(2)}, u32[]{:S(2)}) collective-permute-start(s16[2064,256]{1,0:T(8,128)(2,1)S(1)} %shard_map.45), channel_id=1, source_target_pairs={{0,96},{8,104},{16,112},{24,120},{32,0},{40,8},{48,16},{56,24},{64... | collective-permute-start | bytes 3170312 | tf_op jit(solution)/shard_map/ppermute | solution.py:257
  43.8 2.0 %shard_map.48 = s16[2064,256]{1,0:T(8,128)(2,1)S(1)} custom-call(s32[10]{0:T(128)S(1)} %pad_add_fusion.at_ref, bf16[8,8,2,32,125]{4,3,2,1,0:T(8,128)(2,1)S(1)} %all-to-all-done.four_ref, bf16[4,125,4000]{2,1,0:T(8,128)(2,1)S(1)} %copy-done.1, bf16[4,125,4000]{2,1,0:T(8,128)(2,1)S(1)} %copy-done.1, bf16[4,125,4000]{2,1,0:T(8,128)(2,1)S(1)} %copy-done.1, ...), custom_call_target="tpu_custom_call" | custom-call | tf_op jit(solution)/shard_map/pallas_call | solution.py:187
  45.8 7.9 %collective-permute-done.13.rest_12_ = s16[2064,256]{1,0:T(8,128)(2,1)S(1)} collective-permute-done((s16[2064,256]{1,0:T(8,128)(2,1)S(1)}, s16[2064,256]{1,0:T(8,128)(2,1)S(1)}, u32[]{:S(2)}, u32[]{:S(2)}) %collective-permute-start.13) | collective-permute-done | bytes 1056800 | tf_op jit(solution)/shard_map/ppermute | solution.py:257
  53.9 2.1 %shard_map.47 = s16[2064,256]{1,0:T(8,128)(2,1)S(1)} custom-call(s32[10]{0:T(128)S(1)} %pad_add_fusion.at_ref, bf16[8,8,2,32,125]{4,3,2,1,0:T(8,128)(2,1)S(1)} %all-to-all-done.four_ref, bf16[4,125,4000]{2,1,0:T(8,128)(2,1)S(1)} %copy-done.1, bf16[4,125,4000]{2,1,0:T(8,128)(2,1)S(1)} %copy-done.1, bf16[4,125,4000]{2,1,0:T(8,128)(2,1)S(1)} %copy-done.1, ...), custom_call_target="tpu_custom_call" | custom-call | tf_op jit(solution)/shard_map/pallas_call | solution.py:187
  56.4 1.5 collective-permute-start.14
  57.9 2.1 %shard_map.50 = s16[2064,256]{1,0:T(8,128)(2,1)S(1)} custom-call(s32[10]{0:T(128)S(1)} %pad_add_fusion.at_ref, bf16[8,8,2,32,125]{4,3,2,1,0:T(8,128)(2,1)S(1)} %all-to-all-done.four_ref, bf16[4,125,4000]{2,1,0:T(8,128)(2,1)S(1)} %copy-done.1, bf16[4,125,4000]{2,1,0:T(8,128)(2,1)S(1)} %copy-done.1, bf16[4,125,4000]{2,1,0:T(8,128)(2,1)S(1)} %copy-done.1, ...), custom_call_target="tpu_custom_call" | custom-call | tf_op jit(solution)/shard_map/pallas_call | solution.py:187
  60.3 1.6 collective-permute-start.17
  61.8 2.0 %shard_map.40 = s16[2064,256]{1,0:T(8,128)(2,1)S(1)} custom-call(s32[10]{0:T(128)S(1)} %pad_add_fusion.at_ref, bf16[8,8,2,32,125]{4,3,2,1,0:T(8,128)(2,1)S(1)} %all-to-all-done.four_ref, ...), custom_call_target="tpu_custom_call" | custom-call | tf_op jit(solution)/shard_map/pallas_call | solution.py:187
  63.8 1.7 %collective-permute-done.1.rest_12_ = s16[2064,256]{1,0:T(8,128)(2,1)S(1)} collective-permute-done((s16[2064,256]{1,0:T(8,128)(2,1)S(1)}, s16[2064,256]{1,0:T(8,128)(2,1)S(1)}, u32[]{:S(2)}, u32[]{:S(2)}) %collective-permute-start.1) | collective-permute-done | bytes 1056800 | tf_op jit(solution)/shard_map/ppermute | solution.py:257
  65.8 2.0 %shard_map.37 = s16[2064,256]{1,0:T(8,128)(2,1)S(1)} custom-call(s32[10]{0:T(128)S(1)} %pad_add_fusion.at_ref, bf16[8,8,2,32,125]{4,3,2,1,0:T(8,128)(2,1)S(1)} %all-to-all-done.four_ref, ...), custom_call_target="tpu_custom_call" | custom-call | tf_op jit(solution)/shard_map/pallas_call | solution.py:187
  67.8 2.1 %shard_map.42 = s16[2064,256]{1,0:T(8,128)(2,1)S(1)} custom-call(s32[10]{0:T(128)S(1)} %pad_add_fusion.at_ref, bf16[8,8,2,32,125]{4,3,2,1,0:T(8,128)(2,1)S(1)} %all-to-all-done.four_ref, ...), custom_call_target="tpu_custom_call" | custom-call | tf_op jit(solution)/shard_map/pallas_call | solution.py:187
  69.8 2.1 %shard_map.39 = s16[2064,256]{1,0:T(8,128)(2,1)S(1)} custom-call(s32[10]{0:T(128)S(1)} %pad_add_fusion.at_ref, bf16[8,8,2,32,125]{4,3,2,1,0:T(8,128)(2,1)S(1)} %all-to-all-done.four_ref, ...), custom_call_target="tpu_custom_call" | custom-call | tf_op jit(solution)/shard_map/pallas_call | solution.py:187
  71.9 7.2 %collective-permute-done.12.rest_3_.rest_4_.rest_5_.rest_21_.rest_22_.rest_23_ = s16[2064,256]{1,0:T(8,128)(2,1)S(1)} collective-permute-done((s16[2064,256]{1,0:T(8,128)(2,1)S(1)}, s16[2064,256]{1,0:T(8,128)(2,1)S(1)}, u32[]{:S(2)}, u32[]{:S(2)}) %collective-permute-start.12) | collective-permute-done | bytes 1056800 | tf_op jit(solution)/shard_map/ppermute | solution.py:257
  79.1 4.0 %collective-permute-start = (s16[2064,256]{1,0:T(8,128)(2,1)S(1)}, s16[2064,256]{1,0:T(8,128)(2,1)S(1)}, u32[]{:S(2)}, u32[]{:S(2)}) collective-permute-start(s16[2064,256]{1,0:T(8,128)(2,1)S(1)} %shard_map.37), channel_id=1, source_target_pairs={{0,24},{8,0},{16,8},{24,16},{32,56},{40,32},{48,40},{56,48},{64,88... | collective-permute-start | bytes 3170312 | tf_op jit(solution)/shard_map/ppermute | solution.py:257
  83.1 2.0 %collective-permute-start.5 = (s16[2064,256]{1,0:T(8,128)(2,1)S(1)}, s16[2064,256]{1,0:T(8,128)(2,1)S(1)}, u32[]{:S(2)}, u32[]{:S(2)}) collective-permute-start(s16[2064,256]{1,0:T(8,128)(2,1)S(1)} %shard_map.42), channel_id=1, source_target_pairs={{0,24},{8,0},{16,8},{24,16},{32,56},{40,32},{48,40},{56,48},{64,88... | collective-permute-start | bytes 3170312 | tf_op jit(solution)/shard_map/ppermute | solution.py:257
  85.1 16.9 %collective-permute-done.14.rest_6_.rest_7_.rest_8_.rest_24_.rest_25_.rest_26_ = s16[2064,256]{1,0:T(8,128)(2,1)S(1)} collective-permute-done((s16[2064,256]{1,0:T(8,128)(2,1)S(1)}, s16[2064,256]{1,0:T(8,128)(2,1)S(1)}, u32[]{:S(2)}, u32[]{:S(2)}) %collective-permute-start.14) | collective-permute-done | bytes 1056800 | tf_op jit(solution)/shard_map/ppermute | solution.py:257
  102.0 1.9 %collective-permute-start.2 = (s16[2064,256]{1,0:T(8,128)(2,1)S(1)}, s16[2064,256]{1,0:T(8,128)(2,1)S(1)}, u32[]{:S(2)}, u32[]{:S(2)}) collective-permute-start(s16[2064,256]{1,0:T(8,128)(2,1)S(1)} %shard_map.39), channel_id=1, source_target_pairs={{0,8},{8,16},{16,24},{24,0},{32,40},{40,48},{48,56},{56,32},{64,72... | collective-permute-start | bytes 3170312 | tf_op jit(solution)/shard_map/ppermute | solution.py:257
  103.9 2.2 %shard_map.51 = (s16[528,256]{1,0:T(8,128)(2,1)S(1)}, s16[528,256]{1,0:T(8,128)(2,1)S(1)}, s16[528,256]{1,0:T(8,128)(2,1)S(1)}, s16[528,256]{1,0:T(8,128)(2,1)S(1)}) custom-call(s32[10]{0:T(128)S(1)} %pad_add_fusion.at_ref, bf16[8,8,2,32,125]{4,3,2,1,0:T(8,128)(2,1)S(1)} %all-to-all-done.four_ref, bf16[4,125,4000]{2,1,0:T(8,128)(2,1)S(1)} %copy-done.1, ...), custom_call_target="tpu_custom_call" | custom-call | tf_op jit(solution)/shard_map/pallas_call | solution.py:187
  106.1 2.0 %collective-permute-start.19 = (s16[528,256]{1,0:T(8,128)(2,1)S(1)}, s16[528,256]{1,0:T(8,128)(2,1)S(1)}, u32[]{:S(2)}, u32[]{:S(2)}) collective-permute-start(s16[528,256]{1,0:T(8,128)(2,1)S(1)} %get-tuple-element.28), channel_id=1, source_target_pairs={{0,8},{8,16},{16,24},{24,0},{32,40},{40,48},{48,56},{56,32},{64,72... | collective-permute-start | bytes 811016 | tf_op jit(solution)/shard_map/ppermute | solution.py:257
  108.1 1.3 collective-permute-start.20
  109.4 19.8 %collective-permute-done.5.rest_15_.rest_16_.rest_17_.rest_33_.rest_34_.rest_35_.rest_18_.rest_19_ = s16[2064,256]{1,0:T(8,128)(2,1)S(1)} collective-permute-done((s16[2064,256]{1,0:T(8,128)(2,1)S(1)}, s16[2064,256]{1,0:T(8,128)(2,1)S(1)}, u32[]{:S(2)}, u32[]{:S(2)}) %collective-permute-start.5) | collective-permute-done | bytes 1056800 | tf_op jit(solution)/shard_map/ppermute | solution.py:257
  129.2 0.9 collective-permute-done.2.rest_6_.rest_7_.rest_8_.rest_24_.rest_25_.rest_26_
  130.2 2.2 %shard_map.43 = (s16[528,256]{1,0:T(8,128)(2,1)S(1)}, s16[528,256]{1,0:T(8,128)(2,1)S(1)}, s16[528,256]{1,0:T(8,128)(2,1)S(1)}, s16[528,256]{1,0:T(8,128)(2,1)S(1)}) custom-call(s32[10]{0:T(128)S(1)} %pad_add_fusion.at_ref, bf16[8,8,2,32,125]{4,3,2,1,0:T(8,128)(2,1)S(1)} %all-to-all-done.four_ref, ...), custom_call_target="tpu_custom_call" | custom-call | tf_op jit(solution)/shard_map/pallas_call | solution.py:187
  133.0 2.7 %collective-permute-start.8 = (s16[528,256]{1,0:T(8,128)(2,1)S(1)}, s16[528,256]{1,0:T(8,128)(2,1)S(1)}, u32[]{:S(2)}, u32[]{:S(2)}) collective-permute-start(s16[528,256]{1,0:T(8,128)(2,1)S(1)} %get-tuple-element.22), channel_id=1, source_target_pairs={{0,96},{8,104},{16,112},{24,120},{32,0},{40,8},{48,16},{56,24},{64... | collective-permute-start | bytes 811016 | tf_op jit(solution)/shard_map/ppermute | solution.py:257
  135.7 2.8 %collective-permute-start.18 = (s16[528,256]{1,0:T(8,128)(2,1)S(1)}, s16[528,256]{1,0:T(8,128)(2,1)S(1)}, u32[]{:S(2)}, u32[]{:S(2)}) collective-permute-start(s16[528,256]{1,0:T(8,128)(2,1)S(1)} %get-tuple-element.27), channel_id=1, source_target_pairs={{0,24},{8,0},{16,8},{24,16},{32,56},{40,32},{48,40},{56,48},{64,88... | collective-permute-start | bytes 811016 | tf_op jit(solution)/shard_map/ppermute | solution.py:257
  138.5 1.6 shard_map.52
  140.2 1.8 %collective-permute-done.7.rest_9_ = s16[528,256]{1,0:T(8,128)(2,1)S(1)} collective-permute-done((s16[528,256]{1,0:T(8,128)(2,1)S(1)}, s16[528,256]{1,0:T(8,128)(2,1)S(1)}, u32[]{:S(2)}, u32[]{:S(2)}) %collective-permute-start.7) | collective-permute-done | bytes 270368 | tf_op jit(solution)/shard_map/ppermute | solution.py:257
  141.9 3.5 %collective-permute-start.6 = (s16[528,256]{1,0:T(8,128)(2,1)S(1)}, s16[528,256]{1,0:T(8,128)(2,1)S(1)}, u32[]{:S(2)}, u32[]{:S(2)}) collective-permute-start(s16[528,256]{1,0:T(8,128)(2,1)S(1)} %get-tuple-element.20), channel_id=1, source_target_pairs={{0,96},{8,104},{16,112},{24,120},{32,0},{40,8},{48,16},{56,24},{64... | collective-permute-start | bytes 811016 | tf_op jit(solution)/shard_map/ppermute | solution.py:257
  145.5 1.6 shard_map.44
  147.1 3.3 %collective-permute-start.23 = (s16[528,256]{1,0:T(8,128)(2,1)S(1)}, s16[528,256]{1,0:T(8,128)(2,1)S(1)}, u32[]{:S(2)}, u32[]{:S(2)}) collective-permute-start(s16[528,256]{1,0:T(8,128)(2,1)S(1)} %get-tuple-element.32), channel_id=1, source_target_pairs={{0,24},{8,0},{16,8},{24,16},{32,56},{40,32},{48,40},{56,48},{64,88... | collective-permute-start | bytes 811016 | tf_op jit(solution)/shard_map/ppermute | solution.py:257
  151.3 1.2 collective-permute-start.9
  152.4 1.9 %collective-permute-done.23.rest_21_ = s16[528,256]{1,0:T(8,128)(2,1)S(1)} collective-permute-done((s16[528,256]{1,0:T(8,128)(2,1)S(1)}, s16[528,256]{1,0:T(8,128)(2,1)S(1)}, u32[]{:S(2)}, u32[]{:S(2)}) %collective-permute-start.23) | collective-permute-done | bytes 270368 | tf_op jit(solution)/shard_map/ppermute | solution.py:257
  154.4 1.9 %shard_map.53.rest_22_ = f32[250,4,256]{2,1,0:T(4,128)S(1)} custom-call(s32[10]{0:T(128)S(1)} %pad_add_fusion.at_ref, bf16[8,8,2,32,125]{4,3,2,1,0:T(8,128)(2,1)S(1)} %all-to-all-done.four_ref, bf16[4,125,4000]{2,1,0:T(8,128)(2,1)S(1)} %copy-done.1, bf16[4,125,4000]{2,1,0:T(8,128)(2,1)S(1)} %copy-done.1, bf16[4,125,4000]{2,1,0:T(8,128)(2,1)S(1)} %copy-done.1, ...), custom_call_target="tpu_custom_call" | custom-call | tf_op jit(solution)/shard_map/pallas_call | solution.py:187
  156.9 2.1 %collective-permute-done.9.rest_10_ = s16[528,256]{1,0:T(8,128)(2,1)S(1)} collective-permute-done((s16[528,256]{1,0:T(8,128)(2,1)S(1)}, s16[528,256]{1,0:T(8,128)(2,1)S(1)}, u32[]{:S(2)}, u32[]{:S(2)}) %collective-permute-start.9) | collective-permute-done | bytes 270368 | tf_op jit(solution)/shard_map/ppermute | solution.py:257
  158.9 3.4 %shard_map.54 = f32[250,8,256]{2,1,0:T(8,128)} custom-call(s32[10]{0:T(128)S(1)} %pad_add_fusion.at_ref, bf16[8,8,2,32,125]{4,3,2,1,0:T(8,128)(2,1)S(1)} %all-to-all-done.four_ref, ...), custom_call_target="tpu_custom_call" | custom-call | tf_op jit(solution)/shard_map/pallas_call | solution.py:187
  (36 shorter events, 4.4 us)
Async XLA Ops:
  2.3 20.8 %all-to-all-start = ((bf16[8,8,2,32,125]{4,3,2,1,0:T(8,128)(2,1)}), bf16[8,8,2,32,125]{4,3,2,1,0:T(8,128)(2,1)S(1)}, u32[]{:S(2)}, u32[]{:S(2)}) async-start(bf16[8,8,2,32,125]{4,3,2,1,0:T(8,128)(2,1)} %bitcast.3), calls=%async_computation | async-start | bytes 2097152 | tf_op jit(solution)/shard_map/all_to_all | solution.py:249
  18.4 4.7 %copy-start.2 = (s32[8]{0:T(128)S(1)}, s32[8]{0:T(128)}, u32[]{:S(2)}) copy-start(s32[8]{0:T(128)} %param.5) | copy-start | bytes 100
  23.2 2.2 %copy-start = (bf16[4,125,4000]{2,1,0:T(8,128)(2,1)S(1)}, bf16[4,125,4000]{2,1,0:T(8,128)(2,1)}, u32[]{:S(2)}) copy-start(bf16[4,125,4000]{2,1,0:T(8,128)(2,1)} %slice.8.rest_0_.rest_1_.rest_2_.rest_3_.rest_4_.rest_5_.rest_6_.rest_7_.rest_8_.rest_9_.rest_10_.rest_11_.rest_18_.rest_19_.rest_20_.rest_27_.rest_28_.rest_29_.rest_12_.rest_13_) | copy-start | bytes 12000004
  25.3 6.6 %slice-start = ((s8[8388608]{0:T(1024)(128)(4,1)}), s8[4194304]{0:T(1024)(128)(4,1)S(1)}, s32[]{:S(2)}) async-start(s8[8388608]{0:T(1024)(128)(4,1)} %bitcast.4), calls=%async_computation.1 | async-start | bytes 8388608
  27.0 5.0 %slice-start.1 = ((s8[8388608]{0:T(1024)(128)(4,1)}), s8[4194304]{0:T(1024)(128)(4,1)S(1)}, s32[]{:S(2)}) async-start(s8[8388608]{0:T(1024)(128)(4,1)} %bitcast.4), calls=%async_computation.2 | async-start | bytes 8388608
  27.0 26.6 %collective-permute-start.13 = (s16[2064,256]{1,0:T(8,128)(2,1)S(1)}, s16[2064,256]{1,0:T(8,128)(2,1)S(1)}, u32[]{:S(2)}, u32[]{:S(2)}) collective-permute-start(s16[2064,256]{1,0:T(8,128)(2,1)S(1)} %shard_map.46), channel_id=1, source_target_pairs={{0,32},{8,40},{16,48},{24,56},{32,64},{40,72},{48,80},{56,88},{64,... | collective-permute-start | bytes 3170312 | tf_op jit(solution)/shard_map/ppermute | solution.py:257
  30.1 26.3 %collective-permute-start.16 = (s16[2064,256]{1,0:T(8,128)(2,1)S(1)}, s16[2064,256]{1,0:T(8,128)(2,1)S(1)}, u32[]{:S(2)}, u32[]{:S(2)}) collective-permute-start(s16[2064,256]{1,0:T(8,128)(2,1)S(1)} %shard_map.49), channel_id=1, source_target_pairs={{0,96},{8,104},{16,112},{24,120},{32,0},{40,8},{48,16},{56,24},{64... | collective-permute-start | bytes 3170312 | tf_op jit(solution)/shard_map/ppermute | solution.py:257
  33.9 26.4 %collective-permute-start.4 = (s16[2064,256]{1,0:T(8,128)(2,1)S(1)}, s16[2064,256]{1,0:T(8,128)(2,1)S(1)}, u32[]{:S(2)}, u32[]{:S(2)}) collective-permute-start(s16[2064,256]{1,0:T(8,128)(2,1)S(1)} %shard_map.41), channel_id=1, source_target_pairs={{0,24},{8,0},{16,8},{24,16},{32,56},{40,32},{48,40},{56,48},{64,88... | collective-permute-start | bytes 3170312 | tf_op jit(solution)/shard_map/ppermute | solution.py:257
  38.0 2.2 %copy-start.1 = (bf16[4,125,4000]{2,1,0:T(8,128)(2,1)S(1)}, bf16[4,125,4000]{2,1,0:T(8,128)(2,1)}, u32[]{:S(2)}) copy-start(bf16[4,125,4000]{2,1,0:T(8,128)(2,1)} %slice.8.rest_0_.rest_1_.rest_2_.rest_3_.rest_4_.rest_5_.rest_6_.rest_7_.rest_8_.rest_9_.rest_10_.rest_11_.rest_18_.rest_19_.rest_20_.rest_27_.rest_28_.rest_29_.rest_12_.rest_13_) | copy-start | bytes 12000004
  39.6 26.0 %collective-permute-start.1 = (s16[2064,256]{1,0:T(8,128)(2,1)S(1)}, s16[2064,256]{1,0:T(8,128)(2,1)S(1)}, u32[]{:S(2)}, u32[]{:S(2)}) collective-permute-start(s16[2064,256]{1,0:T(8,128)(2,1)S(1)} %shard_map.38), channel_id=1, source_target_pairs={{0,8},{8,16},{16,24},{24,0},{32,40},{40,48},{48,56},{56,32},{64,72... | collective-permute-start | bytes 3170312 | tf_op jit(solution)/shard_map/ppermute | solution.py:257
  42.2 36.9 %collective-permute-start.12 = (s16[2064,256]{1,0:T(8,128)(2,1)S(1)}, s16[2064,256]{1,0:T(8,128)(2,1)S(1)}, u32[]{:S(2)}, u32[]{:S(2)}) collective-permute-start(s16[2064,256]{1,0:T(8,128)(2,1)S(1)} %shard_map.45), channel_id=1, source_target_pairs={{0,96},{8,104},{16,112},{24,120},{32,0},{40,8},{48,16},{56,24},{64... | collective-permute-start | bytes 3170312 | tf_op jit(solution)/shard_map/ppermute | solution.py:257
  53.6 29.5 %collective-permute-start.15 = (s16[2064,256]{1,0:T(8,128)(2,1)S(1)}, s16[2064,256]{1,0:T(8,128)(2,1)S(1)}, u32[]{:S(2)}, u32[]{:S(2)}) collective-permute-start(s16[2064,256]{1,0:T(8,128)(2,1)S(1)} %shard_map.48), channel_id=1, source_target_pairs={{0,32},{8,40},{16,48},{24,56},{32,64},{40,72},{48,80},{56,88},{64,... | collective-permute-start | bytes 3170312 | tf_op jit(solution)/shard_map/ppermute | solution.py:257
  56.4 45.5 %collective-permute-start.14 = (s16[2064,256]{1,0:T(8,128)(2,1)S(1)}, s16[2064,256]{1,0:T(8,128)(2,1)S(1)}, u32[]{:S(2)}, u32[]{:S(2)}) collective-permute-start(s16[2064,256]{1,0:T(8,128)(2,1)S(1)} %shard_map.47), channel_id=1, source_target_pairs={{0,32},{8,40},{16,48},{24,56},{32,64},{40,72},{48,80},{56,88},{64,... | collective-permute-start | bytes 3170312 | tf_op jit(solution)/shard_map/ppermute | solution.py:257
  60.3 43.6 %collective-permute-start.17 = (s16[2064,256]{1,0:T(8,128)(2,1)S(1)}, s16[2064,256]{1,0:T(8,128)(2,1)S(1)}, u32[]{:S(2)}, u32[]{:S(2)}) collective-permute-start(s16[2064,256]{1,0:T(8,128)(2,1)S(1)} %shard_map.50), channel_id=1, source_target_pairs={{0,96},{8,104},{16,112},{24,120},{32,0},{40,8},{48,16},{56,24},{64... | collective-permute-start | bytes 3170312 | tf_op jit(solution)/shard_map/ppermute | solution.py:257
  65.5 42.6 %collective-permute-start.3 = (s16[2064,256]{1,0:T(8,128)(2,1)S(1)}, s16[2064,256]{1,0:T(8,128)(2,1)S(1)}, u32[]{:S(2)}, u32[]{:S(2)}) collective-permute-start(s16[2064,256]{1,0:T(8,128)(2,1)S(1)} %shard_map.40), channel_id=1, source_target_pairs={{0,8},{8,16},{16,24},{24,0},{32,40},{40,48},{48,56},{56,32},{64,72... | collective-permute-start | bytes 3170312 | tf_op jit(solution)/shard_map/ppermute | solution.py:257
  79.1 30.4 %collective-permute-start = (s16[2064,256]{1,0:T(8,128)(2,1)S(1)}, s16[2064,256]{1,0:T(8,128)(2,1)S(1)}, u32[]{:S(2)}, u32[]{:S(2)}) collective-permute-start(s16[2064,256]{1,0:T(8,128)(2,1)S(1)} %shard_map.37), channel_id=1, source_target_pairs={{0,24},{8,0},{16,8},{24,16},{32,56},{40,32},{48,40},{56,48},{64,88... | collective-permute-start | bytes 3170312 | tf_op jit(solution)/shard_map/ppermute | solution.py:257
  83.1 46.1 %collective-permute-start.5 = (s16[2064,256]{1,0:T(8,128)(2,1)S(1)}, s16[2064,256]{1,0:T(8,128)(2,1)S(1)}, u32[]{:S(2)}, u32[]{:S(2)}) collective-permute-start(s16[2064,256]{1,0:T(8,128)(2,1)S(1)} %shard_map.42), channel_id=1, source_target_pairs={{0,24},{8,0},{16,8},{24,16},{32,56},{40,32},{48,40},{56,48},{64,88... | collective-permute-start | bytes 3170312 | tf_op jit(solution)/shard_map/ppermute | solution.py:257
  102.0 28.2 %collective-permute-start.2 = (s16[2064,256]{1,0:T(8,128)(2,1)S(1)}, s16[2064,256]{1,0:T(8,128)(2,1)S(1)}, u32[]{:S(2)}, u32[]{:S(2)}) collective-permute-start(s16[2064,256]{1,0:T(8,128)(2,1)S(1)} %shard_map.39), channel_id=1, source_target_pairs={{0,8},{8,16},{16,24},{24,0},{32,40},{40,48},{48,56},{56,32},{64,72... | collective-permute-start | bytes 3170312 | tf_op jit(solution)/shard_map/ppermute | solution.py:257
  106.1 32.4 %collective-permute-start.19 = (s16[528,256]{1,0:T(8,128)(2,1)S(1)}, s16[528,256]{1,0:T(8,128)(2,1)S(1)}, u32[]{:S(2)}, u32[]{:S(2)}) collective-permute-start(s16[528,256]{1,0:T(8,128)(2,1)S(1)} %get-tuple-element.28), channel_id=1, source_target_pairs={{0,8},{8,16},{16,24},{24,0},{32,40},{40,48},{48,56},{56,32},{64,72... | collective-permute-start | bytes 811016 | tf_op jit(solution)/shard_map/ppermute | solution.py:257
  108.1 30.4 %collective-permute-start.20 = (s16[528,256]{1,0:T(8,128)(2,1)S(1)}, s16[528,256]{1,0:T(8,128)(2,1)S(1)}, u32[]{:S(2)}, u32[]{:S(2)}) collective-permute-start(s16[528,256]{1,0:T(8,128)(2,1)S(1)} %get-tuple-element.29), channel_id=1, source_target_pairs={{0,24},{8,0},{16,8},{24,16},{32,56},{40,32},{48,40},{56,48},{64,88... | collective-permute-start | bytes 811016 | tf_op jit(solution)/shard_map/ppermute | solution.py:257
  132.4 9.5 %collective-permute-start.7 = (s16[528,256]{1,0:T(8,128)(2,1)S(1)}, s16[528,256]{1,0:T(8,128)(2,1)S(1)}, u32[]{:S(2)}, u32[]{:S(2)}) collective-permute-start(s16[528,256]{1,0:T(8,128)(2,1)S(1)} %get-tuple-element.21), channel_id=1, source_target_pairs={{0,32},{8,40},{16,48},{24,56},{32,64},{40,72},{48,80},{56,88},{64,... | collective-permute-start | bytes 811016 | tf_op jit(solution)/shard_map/ppermute | solution.py:257
  133.0 8.9 %collective-permute-start.8 = (s16[528,256]{1,0:T(8,128)(2,1)S(1)}, s16[528,256]{1,0:T(8,128)(2,1)S(1)}, u32[]{:S(2)}, u32[]{:S(2)}) collective-permute-start(s16[528,256]{1,0:T(8,128)(2,1)S(1)} %get-tuple-element.22), channel_id=1, source_target_pairs={{0,96},{8,104},{16,112},{24,120},{32,0},{40,8},{48,16},{56,24},{64... | collective-permute-start | bytes 811016 | tf_op jit(solution)/shard_map/ppermute | solution.py:257
  135.7 11.4 %collective-permute-start.18 = (s16[528,256]{1,0:T(8,128)(2,1)S(1)}, s16[528,256]{1,0:T(8,128)(2,1)S(1)}, u32[]{:S(2)}, u32[]{:S(2)}) collective-permute-start(s16[528,256]{1,0:T(8,128)(2,1)S(1)} %get-tuple-element.27), channel_id=1, source_target_pairs={{0,24},{8,0},{16,8},{24,16},{32,56},{40,32},{48,40},{56,48},{64,88... | collective-permute-start | bytes 811016 | tf_op jit(solution)/shard_map/ppermute | solution.py:257
  138.5 11.9 %collective-permute-start.22 = (s16[528,256]{1,0:T(8,128)(2,1)S(1)}, s16[528,256]{1,0:T(8,128)(2,1)S(1)}, u32[]{:S(2)}, u32[]{:S(2)}) collective-permute-start(s16[528,256]{1,0:T(8,128)(2,1)S(1)} %get-tuple-element.31), channel_id=1, source_target_pairs={{0,8},{8,16},{16,24},{24,0},{32,40},{40,48},{48,56},{56,32},{64,72... | collective-permute-start | bytes 811016 | tf_op jit(solution)/shard_map/ppermute | solution.py:257
  140.1 11.2 %collective-permute-start.21 = (s16[528,256]{1,0:T(8,128)(2,1)S(1)}, s16[528,256]{1,0:T(8,128)(2,1)S(1)}, u32[]{:S(2)}, u32[]{:S(2)}) collective-permute-start(s16[528,256]{1,0:T(8,128)(2,1)S(1)} %get-tuple-element.30), channel_id=1, source_target_pairs={{0,8},{8,16},{16,24},{24,0},{32,40},{40,48},{48,56},{56,32},{64,72... | collective-permute-start | bytes 811016 | tf_op jit(solution)/shard_map/ppermute | solution.py:257
  141.9 14.3 %collective-permute-start.10 = (s16[528,256]{1,0:T(8,128)(2,1)S(1)}, s16[528,256]{1,0:T(8,128)(2,1)S(1)}, u32[]{:S(2)}, u32[]{:S(2)}) collective-permute-start(s16[528,256]{1,0:T(8,128)(2,1)S(1)} %get-tuple-element.24), channel_id=1, source_target_pairs={{0,32},{8,40},{16,48},{24,56},{32,64},{40,72},{48,80},{56,88},{64,... | collective-permute-start | bytes 811016 | tf_op jit(solution)/shard_map/ppermute | solution.py:257
  141.9 14.3 %collective-permute-start.6 = (s16[528,256]{1,0:T(8,128)(2,1)S(1)}, s16[528,256]{1,0:T(8,128)(2,1)S(1)}, u32[]{:S(2)}, u32[]{:S(2)}) collective-permute-start(s16[528,256]{1,0:T(8,128)(2,1)S(1)} %get-tuple-element.20), channel_id=1, source_target_pairs={{0,96},{8,104},{16,112},{24,120},{32,0},{40,8},{48,16},{56,24},{64... | collective-permute-start | bytes 811016 | tf_op jit(solution)/shard_map/ppermute | solution.py:257
  147.1 7.3 %collective-permute-start.23 = (s16[528,256]{1,0:T(8,128)(2,1)S(1)}, s16[528,256]{1,0:T(8,128)(2,1)S(1)}, u32[]{:S(2)}, u32[]{:S(2)}) collective-permute-start(s16[528,256]{1,0:T(8,128)(2,1)S(1)} %get-tuple-element.32), channel_id=1, source_target_pairs={{0,24},{8,0},{16,8},{24,16},{32,56},{40,32},{48,40},{56,48},{64,88... | collective-permute-start | bytes 811016 | tf_op jit(solution)/shard_map/ppermute | solution.py:257
  150.4 6.5 %collective-permute-start.11 = (s16[528,256]{1,0:T(8,128)(2,1)S(1)}, s16[528,256]{1,0:T(8,128)(2,1)S(1)}, u32[]{:S(2)}, u32[]{:S(2)}) collective-permute-start(s16[528,256]{1,0:T(8,128)(2,1)S(1)} %get-tuple-element.25), channel_id=1, source_target_pairs={{0,96},{8,104},{16,112},{24,120},{32,0},{40,8},{48,16},{56,24},{64... | collective-permute-start | bytes 811016 | tf_op jit(solution)/shard_map/ppermute | solution.py:257
  151.3 7.7 %collective-permute-start.9 = (s16[528,256]{1,0:T(8,128)(2,1)S(1)}, s16[528,256]{1,0:T(8,128)(2,1)S(1)}, u32[]{:S(2)}, u32[]{:S(2)}) collective-permute-start(s16[528,256]{1,0:T(8,128)(2,1)S(1)} %get-tuple-element.23), channel_id=1, source_target_pairs={{0,32},{8,40},{16,48},{24,56},{32,64},{40,72},{48,80},{56,88},{64,... | collective-permute-start | bytes 811016 | tf_op jit(solution)/shard_map/ppermute | solution.py:257

commit v4 on v3

--- a/solution.py
+++ b/solution.py
@@ -16,6 +16,7 @@
 TILES = 3
 TAIL = 16
 SIDE = 4
+WAVENUMS = 4
 PAIR = 2
 GROUPS = 4
 TOP = 32766.0
@@ -87,7 +88,7 @@
 def block_at(at, axis, ahead, b):
     chunk = chunk_at(at, axis, ahead)
     other = at[1 - axis] if b is None else b
-    return chunk * SIDE + other if axis == 0 else other * SIDE + chunk
+    return chunk * at[2 + axis] + other * at[3 - axis]
 
 
 def tile_specs(slots, rows, width, group, blocks):
@@ -108,7 +109,7 @@
 
     def value(slot, b):
         first = block_at(at_ref, axis, ahead, b) * width
-        mval = at_ref[2 + group * PAIR + slot]
+        mval = at_ref[WAVENUMS + group * PAIR + slot]
         total = own_part(four_ref, slot, tiles[b * TILES : (b + 1) * TILES], slot, first, mval)
         at = slot * SIDE + b
         for state in states:
@@ -141,7 +142,7 @@
 
         def value(slot, b):
             at = pair * PAIR + slot
-            mval = at_ref[2 + (1 - axis) * 2 * PAIR + at]
+            mval = at_ref[WAVENUMS + (1 - axis) * 2 * PAIR + at]
             return summed(at_ref, four_ref, at, slot, mval, refs, axis, ahead, width)
 
         store_coded(rest[job - len(jobs)], 1, value, False)
@@ -157,7 +158,7 @@
         for slot in range(PAIR):
             at = pair * PAIR + slot
             k = start * PAIR + at
-            total = summed(at_ref, four_ref, at, slot, at_ref[2 + k], refs, 1 - start // 2, 0, width)
+            total = summed(at_ref, four_ref, at, slot, at_ref[WAVENUMS + k], refs, 1 - start // 2, 0, width)
             out_ref[:, k, :] = total.T[:width]
 
 
@@ -233,8 +234,9 @@
     pairs = []
     for x in range(SIDE):
         for z in range(SIDE):
-            to = ((x + sign) % SIDE, z) if axis == 0 else (x, (z + sign) % SIDE)
-            pairs.append((x * SIDE + z, to[0] * SIDE + to[1]))
+            for wave in range(8):
+                to = ((x + sign) % SIDE, z) if axis == wave % 2 else (x, (z + sign) % SIDE)
+                pairs.append(((x * SIDE + z) * 8 + wave, (to[0] * SIDE + to[1]) * 8 + wave))
     return pairs
 
 
@@ -247,14 +249,18 @@
     split = fourier.transpose(2, 0, 3, 1)
     split = split.reshape(8, slots, 2, split.shape[2], rows)
     four = lax.all_to_all(split, "wave", split_axis=0, concat_axis=0, tiled=True)
-    at = jnp.concatenate([jnp.stack([me // SIDE, me % SIDE]).astype(jnp.int32), wavenums])
+    swapped = lax.axis_index("wave") % 2 == 1
+    x, z = me // SIDE, me % SIDE
+    places = [jnp.where(swapped, z, x), jnp.where(swapped, x, z)]
+    strides = [jnp.where(swapped, 1, SIDE), jnp.where(swapped, SIDE, 1)]
+    at = jnp.concatenate([jnp.stack(places + strides).astype(jnp.int32), wavenums])
     table = lax.optimization_barrier(with_layout_constraint(table, Layout((0, 1, 2))))
     half = table[: 2 * PAIR]
     table, half = lax.optimization_barrier((table, half))
     table = (half, table[2 * PAIR :])
 
     def send(array, axis, sign):
-        return lax.ppermute(array, "lat", ring(axis, sign))
+        return lax.ppermute(array, ("lat", "wave"), ring(axis, sign))
 
     def first(group, ahead, states):
         return first_hop(group, ahead, at, four, table, states, width)

time: 163 us -> 137 us (0.84)
  waiting for transfers between devices: 61.5 us -> 34.8 us
    ppermute x24, waiting for transfers between devices: 61.5 us -> 34.7 us  [send(): return lax.ppermute(array, ('lat', 'wave'), ring(axis, sign))]
  transfers between devices with their start and end apart: 25 -> 25, of which waited for: 12 -> 9; matrix products, arithmetic and copies ran while one was open for 10% -> 12% of each run, Pallas kernels for 19% -> 22%
where the time goes in v4:
time: 137 us
  starting transfers between devices  44.9 us (33%)
  Pallas kernels  35.5 us (26%)
  waiting for transfers between devices  34.8 us (25%)
  local copies, waits for them, and re-layouts  21.2 us (15%)
    ppermute x24, starting transfers between devices, send(): return lax.ppermute(array, ('lat', 'wave'), ring(axis, sign))  40 us
    pallas_call x18, Pallas kernels, call(): pl.pallas_call(body, grid_spec=pltpu.PrefetchScalarGridSpec(num_scalar_pr...  35.5 us
    ppermute x24, waiting for transfers between devices, send(): return lax.ppermute(array, ('lat', 'wave'), ring(axis, sign))  34.7 us
    unnamed x11, local copies, waits for them, and re-layouts  13.6 us
    all_to_all x1, starting transfers between devices, per_device(): lax.all_to_all(split, 'wave', split_axis=0, concat_axis=0, tiled=True)  4.92 us
    slice x1, local copies, waits for them, and re-layouts, per_device(): half = table[:2 * PAIR]  4.7 us
  transfers between devices with their start and end apart: 25, of which 9 were waited for; matrix products, arithmetic and copies ran while one was open for 12% of the time, Pallas kernels for 22%

profile of v4, /device:TPU:8, one launch (start us, length us, event | category | flops | bytes accessed | tf_op | source)
XLA Modules:
  0.0 136.6 jit_solution(3300668306057269516)
XLA Ops:
  0.0 2.3 %copy.4 = bf16[64,2,32,125]{3,2,1,0:T(8,128)(2,1)} copy(bf16[64,2,32,125]{3,2,0,1:T(8,128)(2,1)} %bitcast.8) | data formatting | bytes 2048000 | tf_op jit(solution)/shard_map/transpose | solution.py:249
  2.3 4.9 %all-to-all-start = ((bf16[8,8,2,32,125]{4,3,2,1,0:T(8,128)(2,1)}), bf16[8,8,2,32,125]{4,3,2,1,0:T(8,128)(2,1)S(1)}, u32[]{:S(2)}, u32[]{:S(2)}) async-start(bf16[8,8,2,32,125]{4,3,2,1,0:T(8,128)(2,1)} %bitcast.5), calls=%async_computation | async-start | bytes 2097152 | tf_op jit(solution)/shard_map/all_to_all | solution.py:251
  7.3 11.1 %copy.5 = bf16[8,125,4000]{2,1,0:T(8,128)(2,1)} copy(bf16[8,125,4000]{2,0,1:T(8,128)(2,1)} %param.4) | data formatting | bytes 16000000 | tf_op args[1]
  18.4 4.7 %slice.8.rest_0_.rest_1_.rest_2_.rest_3_.rest_4_.rest_5_.rest_6_.rest_7_.rest_8_.rest_9_.rest_10_.rest_11_.rest_18_.rest_19_.rest_20_.rest_27_.rest_28_.rest_29_.rest_12_.rest_13_ = bf16[4,125,4000]{2,1,0:T(8,128)(2,1)} slice(bf16[8,125,4000]{2,1,0:T(8,128)(2,1)} %copy.5), slice={[0:4], [0:125], [0:4000]} | slice | bytes 8000000 | tf_op jit(solution)/shard_map/slice | solution.py:258
  23.2 2.2 %copy-done = bf16[4,125,4000]{2,1,0:T(8,128)(2,1)S(1)} copy-done((bf16[4,125,4000]{2,1,0:T(8,128)(2,1)S(1)}, bf16[4,125,4000]{2,1,0:T(8,128)(2,1)}, u32[]{:S(2)}) %copy-start) | copy-done | bytes 4000024
  25.4 1.6 %shard_map.46 = s16[2064,256]{1,0:T(8,128)(2,1)S(1)} custom-call(s32[12]{0:T(128)S(1)} %concatenate.3.at_ref, bf16[8,8,2,32,125]{4,3,2,1,0:T(8,128)(2,1)S(1)} %all-to-all-done.four_ref, bf16[4,125,4000]{2,1,0:T(8,128)(2,1)S(1)} %copy-done, bf16[4,125,4000]{2,1,0:T(8,128)(2,1)S(1)} %copy-done, bf16[4,125,4000]{2,1,0:T(8,128)(2,1)S(1)} %copy-done, ...), custom_call_target="tpu_custom_call" | custom-call | tf_op jit(solution)/shard_map/pallas_call | solution.py:188
  27.0 1.6 %collective-permute-start.13 = (s16[2064,256]{1,0:T(8,128)(2,1)S(1)}, s16[2064,256]{1,0:T(8,128)(2,1)S(1)}, u32[]{:S(2)}, u32[]{:S(2)}) collective-permute-start(s16[2064,256]{1,0:T(8,128)(2,1)S(1)} %shard_map.46), channel_id=1, source_target_pairs={{0,32},{1,9},{2,34},{3,11},{4,36},{5,13},{6,38},{7,15},{8,40},{9,1... | collective-permute-start | bytes 3170312 | tf_op jit(solution)/shard_map/ppermute | solution.py:263
  28.5 1.6 %shard_map.49 = s16[2064,256]{1,0:T(8,128)(2,1)S(1)} custom-call(s32[12]{0:T(128)S(1)} %concatenate.3.at_ref, bf16[8,8,2,32,125]{4,3,2,1,0:T(8,128)(2,1)S(1)} %all-to-all-done.four_ref, bf16[4,125,4000]{2,1,0:T(8,128)(2,1)S(1)} %copy-done, bf16[4,125,4000]{2,1,0:T(8,128)(2,1)S(1)} %copy-done, bf16[4,125,4000]{2,1,0:T(8,128)(2,1)S(1)} %copy-done, ...), custom_call_target="tpu_custom_call" | custom-call | tf_op jit(solution)/shard_map/pallas_call | solution.py:188
  30.1 1.8 %collective-permute-start.16 = (s16[2064,256]{1,0:T(8,128)(2,1)S(1)}, s16[2064,256]{1,0:T(8,128)(2,1)S(1)}, u32[]{:S(2)}, u32[]{:S(2)}) collective-permute-start(s16[2064,256]{1,0:T(8,128)(2,1)S(1)} %shard_map.49), channel_id=1, source_target_pairs={{0,96},{1,25},{2,98},{3,27},{4,100},{5,29},{6,102},{7,31},{8,104},... | collective-permute-start | bytes 3170312 | tf_op jit(solution)/shard_map/ppermute | solution.py:263
  32.4 1.6 %shard_map.41 = s16[2064,256]{1,0:T(8,128)(2,1)S(1)} custom-call(s32[12]{0:T(128)S(1)} %concatenate.3.at_ref, bf16[8,8,2,32,125]{4,3,2,1,0:T(8,128)(2,1)S(1)} %all-to-all-done.four_ref, ...), custom_call_target="tpu_custom_call" | custom-call | tf_op jit(solution)/shard_map/pallas_call | solution.py:188
  34.1 4.1 %collective-permute-start.4 = (s16[2064,256]{1,0:T(8,128)(2,1)S(1)}, s16[2064,256]{1,0:T(8,128)(2,1)S(1)}, u32[]{:S(2)}, u32[]{:S(2)}) collective-permute-start(s16[2064,256]{1,0:T(8,128)(2,1)S(1)} %shard_map.41), channel_id=1, source_target_pairs={{0,24},{1,97},{2,26},{3,99},{4,28},{5,101},{6,30},{7,103},{8,0},{9... | collective-permute-start | bytes 3170312 | tf_op jit(solution)/shard_map/ppermute | solution.py:263
  38.2 1.6 %shard_map.38 = s16[2064,256]{1,0:T(8,128)(2,1)S(1)} custom-call(s32[12]{0:T(128)S(1)} %concatenate.3.at_ref, bf16[8,8,2,32,125]{4,3,2,1,0:T(8,128)(2,1)S(1)} %all-to-all-done.four_ref, ...), custom_call_target="tpu_custom_call" | custom-call | tf_op jit(solution)/shard_map/pallas_call | solution.py:188
  40.4 2.0 %shard_map.45 = s16[2064,256]{1,0:T(8,128)(2,1)S(1)} custom-call(s32[12]{0:T(128)S(1)} %concatenate.3.at_ref, bf16[8,8,2,32,125]{4,3,2,1,0:T(8,128)(2,1)S(1)} %all-to-all-done.four_ref, bf16[4,125,4000]{2,1,0:T(8,128)(2,1)S(1)} %copy-done.1, bf16[4,125,4000]{2,1,0:T(8,128)(2,1)S(1)} %copy-done.1, bf16[4,125,4000]{2,1,0:T(8,128)(2,1)S(1)} %copy-done.1, ...), custom_call_target="tpu_custom_call" | custom-call | tf_op jit(solution)/shard_map/pallas_call | solution.py:188
  42.3 1.6 %collective-permute-start.12 = (s16[2064,256]{1,0:T(8,128)(2,1)S(1)}, s16[2064,256]{1,0:T(8,128)(2,1)S(1)}, u32[]{:S(2)}, u32[]{:S(2)}) collective-permute-start(s16[2064,256]{1,0:T(8,128)(2,1)S(1)} %shard_map.45), channel_id=1, source_target_pairs={{0,96},{1,25},{2,98},{3,27},{4,100},{5,29},{6,102},{7,31},{8,104},... | collective-permute-start | bytes 3170312 | tf_op jit(solution)/shard_map/ppermute | solution.py:263
  44.0 2.0 %shard_map.48 = s16[2064,256]{1,0:T(8,128)(2,1)S(1)} custom-call(s32[12]{0:T(128)S(1)} %concatenate.3.at_ref, bf16[8,8,2,32,125]{4,3,2,1,0:T(8,128)(2,1)S(1)} %all-to-all-done.four_ref, bf16[4,125,4000]{2,1,0:T(8,128)(2,1)S(1)} %copy-done.1, bf16[4,125,4000]{2,1,0:T(8,128)(2,1)S(1)} %copy-done.1, bf16[4,125,4000]{2,1,0:T(8,128)(2,1)S(1)} %copy-done.1, ...), custom_call_target="tpu_custom_call" | custom-call | tf_op jit(solution)/shard_map/pallas_call | solution.py:188
  46.5 2.1 %shard_map.47 = s16[2064,256]{1,0:T(8,128)(2,1)S(1)} custom-call(s32[12]{0:T(128)S(1)} %concatenate.3.at_ref, bf16[8,8,2,32,125]{4,3,2,1,0:T(8,128)(2,1)S(1)} %all-to-all-done.four_ref, bf16[4,125,4000]{2,1,0:T(8,128)(2,1)S(1)} %copy-done.1, bf16[4,125,4000]{2,1,0:T(8,128)(2,1)S(1)} %copy-done.1, bf16[4,125,4000]{2,1,0:T(8,128)(2,1)S(1)} %copy-done.1, ...), custom_call_target="tpu_custom_call" | custom-call | tf_op jit(solution)/shard_map/pallas_call | solution.py:188
  48.6 4.2 %collective-permute-done.16.rest_12_ = s16[2064,256]{1,0:T(8,128)(2,1)S(1)} collective-permute-done((s16[2064,256]{1,0:T(8,128)(2,1)S(1)}, s16[2064,256]{1,0:T(8,128)(2,1)S(1)}, u32[]{:S(2)}, u32[]{:S(2)}) %collective-permute-start.16) | collective-permute-done | bytes 1056800 | tf_op jit(solution)/shard_map/ppermute | solution.py:263
  52.8 1.5 %collective-permute-start.14 = (s16[2064,256]{1,0:T(8,128)(2,1)S(1)}, s16[2064,256]{1,0:T(8,128)(2,1)S(1)}, u32[]{:S(2)}, u32[]{:S(2)}) collective-permute-start(s16[2064,256]{1,0:T(8,128)(2,1)S(1)} %shard_map.47), channel_id=1, source_target_pairs={{0,32},{1,9},{2,34},{3,11},{4,36},{5,13},{6,38},{7,15},{8,40},{9,1... | collective-permute-start | bytes 3170312 | tf_op jit(solution)/shard_map/ppermute | solution.py:263
  54.3 2.1 %shard_map.50 = s16[2064,256]{1,0:T(8,128)(2,1)S(1)} custom-call(s32[12]{0:T(128)S(1)} %concatenate.3.at_ref, bf16[8,8,2,32,125]{4,3,2,1,0:T(8,128)(2,1)S(1)} %all-to-all-done.four_ref, bf16[4,125,4000]{2,1,0:T(8,128)(2,1)S(1)} %copy-done.1, bf16[4,125,4000]{2,1,0:T(8,128)(2,1)S(1)} %copy-done.1, bf16[4,125,4000]{2,1,0:T(8,128)(2,1)S(1)} %copy-done.1, ...), custom_call_target="tpu_custom_call" | custom-call | tf_op jit(solution)/shard_map/pallas_call | solution.py:188
  56.4 5.5 %collective-permute-done.4.rest_12_ = s16[2064,256]{1,0:T(8,128)(2,1)S(1)} collective-permute-done((s16[2064,256]{1,0:T(8,128)(2,1)S(1)}, s16[2064,256]{1,0:T(8,128)(2,1)S(1)}, u32[]{:S(2)}, u32[]{:S(2)}) %collective-permute-start.4) | collective-permute-done | bytes 1056800 | tf_op jit(solution)/shard_map/ppermute | solution.py:263
  61.9 1.6 %collective-permute-start.17 = (s16[2064,256]{1,0:T(8,128)(2,1)S(1)}, s16[2064,256]{1,0:T(8,128)(2,1)S(1)}, u32[]{:S(2)}, u32[]{:S(2)}) collective-permute-start(s16[2064,256]{1,0:T(8,128)(2,1)S(1)} %shard_map.50), channel_id=1, source_target_pairs={{0,96},{1,25},{2,98},{3,27},{4,100},{5,29},{6,102},{7,31},{8,104},... | collective-permute-start | bytes 3170312 | tf_op jit(solution)/shard_map/ppermute | solution.py:263
  63.4 2.0 %shard_map.40 = s16[2064,256]{1,0:T(8,128)(2,1)S(1)} custom-call(s32[12]{0:T(128)S(1)} %concatenate.3.at_ref, bf16[8,8,2,32,125]{4,3,2,1,0:T(8,128)(2,1)S(1)} %all-to-all-done.four_ref, ...), custom_call_target="tpu_custom_call" | custom-call | tf_op jit(solution)/shard_map/pallas_call | solution.py:188
  65.9 2.0 %shard_map.37 = s16[2064,256]{1,0:T(8,128)(2,1)S(1)} custom-call(s32[12]{0:T(128)S(1)} %concatenate.3.at_ref, bf16[8,8,2,32,125]{4,3,2,1,0:T(8,128)(2,1)S(1)} %all-to-all-done.four_ref, ...), custom_call_target="tpu_custom_call" | custom-call | tf_op jit(solution)/shard_map/pallas_call | solution.py:188
  67.8 2.1 %shard_map.42 = s16[2064,256]{1,0:T(8,128)(2,1)S(1)} custom-call(s32[12]{0:T(128)S(1)} %concatenate.3.at_ref, bf16[8,8,2,32,125]{4,3,2,1,0:T(8,128)(2,1)S(1)} %all-to-all-done.four_ref, ...), custom_call_target="tpu_custom_call" | custom-call | tf_op jit(solution)/shard_map/pallas_call | solution.py:188
  69.9 2.1 %shard_map.39 = s16[2064,256]{1,0:T(8,128)(2,1)S(1)} custom-call(s32[12]{0:T(128)S(1)} %concatenate.3.at_ref, bf16[8,8,2,32,125]{4,3,2,1,0:T(8,128)(2,1)S(1)} %all-to-all-done.four_ref, ...), custom_call_target="tpu_custom_call" | custom-call | tf_op jit(solution)/shard_map/pallas_call | solution.py:188
  72.0 3.4 %collective-permute-start = (s16[2064,256]{1,0:T(8,128)(2,1)S(1)}, s16[2064,256]{1,0:T(8,128)(2,1)S(1)}, u32[]{:S(2)}, u32[]{:S(2)}) collective-permute-start(s16[2064,256]{1,0:T(8,128)(2,1)S(1)} %shard_map.37), channel_id=1, source_target_pairs={{0,24},{1,97},{2,26},{3,99},{4,28},{5,101},{6,30},{7,103},{8,0},{9... | collective-permute-start | bytes 3170312 | tf_op jit(solution)/shard_map/ppermute | solution.py:263
  75.4 2.0 %collective-permute-start.5 = (s16[2064,256]{1,0:T(8,128)(2,1)S(1)}, s16[2064,256]{1,0:T(8,128)(2,1)S(1)}, u32[]{:S(2)}, u32[]{:S(2)}) collective-permute-start(s16[2064,256]{1,0:T(8,128)(2,1)S(1)} %shard_map.42), channel_id=1, source_target_pairs={{0,24},{1,97},{2,26},{3,99},{4,28},{5,101},{6,30},{7,103},{8,0},{9... | collective-permute-start | bytes 3170312 | tf_op jit(solution)/shard_map/ppermute | solution.py:263
  77.4 8.3 %collective-permute-done.14.rest_6_.rest_7_.rest_8_.rest_24_.rest_25_.rest_26_ = s16[2064,256]{1,0:T(8,128)(2,1)S(1)} collective-permute-done((s16[2064,256]{1,0:T(8,128)(2,1)S(1)}, s16[2064,256]{1,0:T(8,128)(2,1)S(1)}, u32[]{:S(2)}, u32[]{:S(2)}) %collective-permute-start.14) | collective-permute-done | bytes 1056800 | tf_op jit(solution)/shard_map/ppermute | solution.py:263
  85.7 3.5 %collective-permute-start.2 = (s16[2064,256]{1,0:T(8,128)(2,1)S(1)}, s16[2064,256]{1,0:T(8,128)(2,1)S(1)}, u32[]{:S(2)}, u32[]{:S(2)}) collective-permute-start(s16[2064,256]{1,0:T(8,128)(2,1)S(1)} %shard_map.39), channel_id=1, source_target_pairs={{0,8},{1,33},{2,10},{3,35},{4,12},{5,37},{6,14},{7,39},{8,16},{9,4... | collective-permute-start | bytes 3170312 | tf_op jit(solution)/shard_map/ppermute | solution.py:263
  89.2 2.2 %shard_map.51 = (s16[528,256]{1,0:T(8,128)(2,1)S(1)}, s16[528,256]{1,0:T(8,128)(2,1)S(1)}, s16[528,256]{1,0:T(8,128)(2,1)S(1)}, s16[528,256]{1,0:T(8,128)(2,1)S(1)}) custom-call(s32[12]{0:T(128)S(1)} %concatenate.3.at_ref, bf16[8,8,2,32,125]{4,3,2,1,0:T(8,128)(2,1)S(1)} %all-to-all-done.four_ref, bf16[4,125,4000]{2,1,0:T(8,128)(2,1)S(1)} %copy-done.1, ...), custom_call_target="tpu_custom_call" | custom-call | tf_op jit(solution)/shard_map/pallas_call | solution.py:188
  91.5 3.3 %collective-permute-start.19 = (s16[528,256]{1,0:T(8,128)(2,1)S(1)}, s16[528,256]{1,0:T(8,128)(2,1)S(1)}, u32[]{:S(2)}, u32[]{:S(2)}) collective-permute-start(s16[528,256]{1,0:T(8,128)(2,1)S(1)} %get-tuple-element.28), channel_id=1, source_target_pairs={{0,8},{1,33},{2,10},{3,35},{4,12},{5,37},{6,14},{7,39},{8,16},{9,4... | collective-permute-start | bytes 811016 | tf_op jit(solution)/shard_map/ppermute | solution.py:263
  94.8 1.2 collective-permute-start.20
  96.0 5.2 %collective-permute-done.5.rest_15_.rest_16_.rest_17_.rest_33_.rest_34_.rest_35_.rest_18_.rest_19_ = s16[2064,256]{1,0:T(8,128)(2,1)S(1)} collective-permute-done((s16[2064,256]{1,0:T(8,128)(2,1)S(1)}, s16[2064,256]{1,0:T(8,128)(2,1)S(1)}, u32[]{:S(2)}, u32[]{:S(2)}) %collective-permute-start.5) | collective-permute-done | bytes 1056800 | tf_op jit(solution)/shard_map/ppermute | solution.py:263
  101.2 5.1 %collective-permute-done.2.rest_6_.rest_7_.rest_8_.rest_24_.rest_25_.rest_26_ = s16[2064,256]{1,0:T(8,128)(2,1)S(1)} collective-permute-done((s16[2064,256]{1,0:T(8,128)(2,1)S(1)}, s16[2064,256]{1,0:T(8,128)(2,1)S(1)}, u32[]{:S(2)}, u32[]{:S(2)}) %collective-permute-start.2) | collective-permute-done | bytes 1056800 | tf_op jit(solution)/shard_map/ppermute | solution.py:263
  106.3 2.2 %shard_map.43 = (s16[528,256]{1,0:T(8,128)(2,1)S(1)}, s16[528,256]{1,0:T(8,128)(2,1)S(1)}, s16[528,256]{1,0:T(8,128)(2,1)S(1)}, s16[528,256]{1,0:T(8,128)(2,1)S(1)}) custom-call(s32[12]{0:T(128)S(1)} %concatenate.3.at_ref, bf16[8,8,2,32,125]{4,3,2,1,0:T(8,128)(2,1)S(1)} %all-to-all-done.four_ref, ...), custom_call_target="tpu_custom_call" | custom-call | tf_op jit(solution)/shard_map/pallas_call | solution.py:188
  108.5 1.4 %collective-permute-start.7 = (s16[528,256]{1,0:T(8,128)(2,1)S(1)}, s16[528,256]{1,0:T(8,128)(2,1)S(1)}, u32[]{:S(2)}, u32[]{:S(2)}) collective-permute-start(s16[528,256]{1,0:T(8,128)(2,1)S(1)} %get-tuple-element.21), channel_id=1, source_target_pairs={{0,32},{1,9},{2,34},{3,11},{4,36},{5,13},{6,38},{7,15},{8,40},{9,1... | collective-permute-start | bytes 811016 | tf_op jit(solution)/shard_map/ppermute | solution.py:263
  109.9 1.9 %collective-permute-start.8 = (s16[528,256]{1,0:T(8,128)(2,1)S(1)}, s16[528,256]{1,0:T(8,128)(2,1)S(1)}, u32[]{:S(2)}, u32[]{:S(2)}) collective-permute-start(s16[528,256]{1,0:T(8,128)(2,1)S(1)} %get-tuple-element.22), channel_id=1, source_target_pairs={{0,96},{1,25},{2,98},{3,27},{4,100},{5,29},{6,102},{7,31},{8,104},... | collective-permute-start | bytes 811016 | tf_op jit(solution)/shard_map/ppermute | solution.py:263
  111.8 2.0 %collective-permute-start.18 = (s16[528,256]{1,0:T(8,128)(2,1)S(1)}, s16[528,256]{1,0:T(8,128)(2,1)S(1)}, u32[]{:S(2)}, u32[]{:S(2)}) collective-permute-start(s16[528,256]{1,0:T(8,128)(2,1)S(1)} %get-tuple-element.27), channel_id=1, source_target_pairs={{0,24},{1,97},{2,26},{3,99},{4,28},{5,101},{6,30},{7,103},{8,0},{9... | collective-permute-start | bytes 811016 | tf_op jit(solution)/shard_map/ppermute | solution.py:263
  113.8 1.6 %shard_map.52 = (s16[528,256]{1,0:T(8,128)(2,1)S(1)}, s16[528,256]{1,0:T(8,128)(2,1)S(1)}) custom-call(s32[12]{0:T(128)S(1)} %concatenate.3.at_ref, bf16[8,8,2,32,125]{4,3,2,1,0:T(8,128)(2,1)S(1)} %all-to-all-done.four_ref, bf16[4,125,4000]{2,1,0:T(8,128)(2,1)S(1)} %copy-done.1, bf16[4,125,4000]{2,1,0:T(8,128)(2,1)S(1)} %copy-done.1, ...), custom_call_target="tpu_custom_call" | custom-call | tf_op jit(solution)/shard_map/pallas_call | solution.py:188
  115.5 2.5 %collective-permute-done.7.rest_9_ = s16[528,256]{1,0:T(8,128)(2,1)S(1)} collective-permute-done((s16[528,256]{1,0:T(8,128)(2,1)S(1)}, s16[528,256]{1,0:T(8,128)(2,1)S(1)}, u32[]{:S(2)}, u32[]{:S(2)}) %collective-permute-start.7) | collective-permute-done | bytes 270368 | tf_op jit(solution)/shard_map/ppermute | solution.py:263
  119.1 2.1 %collective-permute-start.6 = (s16[528,256]{1,0:T(8,128)(2,1)S(1)}, s16[528,256]{1,0:T(8,128)(2,1)S(1)}, u32[]{:S(2)}, u32[]{:S(2)}) collective-permute-start(s16[528,256]{1,0:T(8,128)(2,1)S(1)} %get-tuple-element.20), channel_id=1, source_target_pairs={{0,96},{1,25},{2,98},{3,27},{4,100},{5,29},{6,102},{7,31},{8,104},... | collective-permute-start | bytes 811016 | tf_op jit(solution)/shard_map/ppermute | solution.py:263
  121.2 1.6 %shard_map.44 = (s16[528,256]{1,0:T(8,128)(2,1)S(1)}, s16[528,256]{1,0:T(8,128)(2,1)S(1)}) custom-call(s32[12]{0:T(128)S(1)} %concatenate.3.at_ref, bf16[8,8,2,32,125]{4,3,2,1,0:T(8,128)(2,1)S(1)} %all-to-all-done.four_ref, ...), custom_call_target="tpu_custom_call" | custom-call | tf_op jit(solution)/shard_map/pallas_call | solution.py:188
  122.9 2.4 %collective-permute-start.23 = (s16[528,256]{1,0:T(8,128)(2,1)S(1)}, s16[528,256]{1,0:T(8,128)(2,1)S(1)}, u32[]{:S(2)}, u32[]{:S(2)}) collective-permute-start(s16[528,256]{1,0:T(8,128)(2,1)S(1)} %get-tuple-element.32), channel_id=1, source_target_pairs={{0,24},{1,97},{2,26},{3,99},{4,28},{5,101},{6,30},{7,103},{8,0},{9... | collective-permute-start | bytes 811016 | tf_op jit(solution)/shard_map/ppermute | solution.py:263
  125.3 2.0 %collective-permute-start.9 = (s16[528,256]{1,0:T(8,128)(2,1)S(1)}, s16[528,256]{1,0:T(8,128)(2,1)S(1)}, u32[]{:S(2)}, u32[]{:S(2)}) collective-permute-start(s16[528,256]{1,0:T(8,128)(2,1)S(1)} %get-tuple-element.23), channel_id=1, source_target_pairs={{0,32},{1,9},{2,34},{3,11},{4,36},{5,13},{6,38},{7,15},{8,40},{9,1... | collective-permute-start | bytes 811016 | tf_op jit(solution)/shard_map/ppermute | solution.py:263
  127.3 2.1 %collective-permute-done.23.rest_21_ = s16[528,256]{1,0:T(8,128)(2,1)S(1)} collective-permute-done((s16[528,256]{1,0:T(8,128)(2,1)S(1)}, s16[528,256]{1,0:T(8,128)(2,1)S(1)}, u32[]{:S(2)}, u32[]{:S(2)}) %collective-permute-start.23) | collective-permute-done | bytes 270368 | tf_op jit(solution)/shard_map/ppermute | solution.py:263
  129.4 1.9 %shard_map.53.rest_22_ = f32[250,4,256]{2,1,0:T(4,128)S(1)} custom-call(s32[12]{0:T(128)S(1)} %concatenate.3.at_ref, bf16[8,8,2,32,125]{4,3,2,1,0:T(8,128)(2,1)S(1)} %all-to-all-done.four_ref, bf16[4,125,4000]{2,1,0:T(8,128)(2,1)S(1)} %copy-done.1, bf16[4,125,4000]{2,1,0:T(8,128)(2,1)S(1)} %copy-done.1, bf16[4,125,4000]{2,1,0:T(8,128)(2,1)S(1)} %copy-done.1, ...), custom_call_target="tpu_custom_call" | custom-call | tf_op jit(solution)/shard_map/pallas_call | solution.py:188
  131.8 1.4 %collective-permute-done.9.rest_10_ = s16[528,256]{1,0:T(8,128)(2,1)S(1)} collective-permute-done((s16[528,256]{1,0:T(8,128)(2,1)S(1)}, s16[528,256]{1,0:T(8,128)(2,1)S(1)}, u32[]{:S(2)}, u32[]{:S(2)}) %collective-permute-start.9) | collective-permute-done | bytes 270368 | tf_op jit(solution)/shard_map/ppermute | solution.py:263
  133.2 3.4 %shard_map.54 = f32[250,8,256]{2,1,0:T(8,128)} custom-call(s32[12]{0:T(128)S(1)} %concatenate.3.at_ref, bf16[8,8,2,32,125]{4,3,2,1,0:T(8,128)(2,1)S(1)} %all-to-all-done.four_ref, ...), custom_call_target="tpu_custom_call" | custom-call | tf_op jit(solution)/shard_map/pallas_call | solution.py:188
  (36 shorter events, 3.9 us)
Async XLA Ops:
  2.3 20.8 %all-to-all-start = ((bf16[8,8,2,32,125]{4,3,2,1,0:T(8,128)(2,1)}), bf16[8,8,2,32,125]{4,3,2,1,0:T(8,128)(2,1)S(1)}, u32[]{:S(2)}, u32[]{:S(2)}) async-start(bf16[8,8,2,32,125]{4,3,2,1,0:T(8,128)(2,1)} %bitcast.5), calls=%async_computation | async-start | bytes 2097152 | tf_op jit(solution)/shard_map/all_to_all | solution.py:251
  18.4 4.7 %copy-start.2 = (s32[8]{0:T(128)S(1)}, s32[8]{0:T(128)}, u32[]{:S(2)}) copy-start(s32[8]{0:T(128)} %param.5) | copy-start | bytes 100
  23.2 2.2 %copy-start = (bf16[4,125,4000]{2,1,0:T(8,128)(2,1)S(1)}, bf16[4,125,4000]{2,1,0:T(8,128)(2,1)}, u32[]{:S(2)}) copy-start(bf16[4,125,4000]{2,1,0:T(8,128)(2,1)} %slice.8.rest_0_.rest_1_.rest_2_.rest_3_.rest_4_.rest_5_.rest_6_.rest_7_.rest_8_.rest_9_.rest_10_.rest_11_.rest_18_.rest_19_.rest_20_.rest_27_.rest_28_.rest_29_.rest_12_.rest_13_) | copy-start | bytes 12000004
  25.4 6.6 %slice-start = ((s8[8388608]{0:T(1024)(128)(4,1)}), s8[4194304]{0:T(1024)(128)(4,1)S(1)}, s32[]{:S(2)}) async-start(s8[8388608]{0:T(1024)(128)(4,1)} %bitcast.6), calls=%async_computation.1 | async-start | bytes 8388608
  27.0 5.0 %slice-start.1 = ((s8[8388608]{0:T(1024)(128)(4,1)}), s8[4194304]{0:T(1024)(128)(4,1)S(1)}, s32[]{:S(2)}) async-start(s8[8388608]{0:T(1024)(128)(4,1)} %bitcast.6), calls=%async_computation.2 | async-start | bytes 8388608
  27.0 19.0 %collective-permute-start.13 = (s16[2064,256]{1,0:T(8,128)(2,1)S(1)}, s16[2064,256]{1,0:T(8,128)(2,1)S(1)}, u32[]{:S(2)}, u32[]{:S(2)}) collective-permute-start(s16[2064,256]{1,0:T(8,128)(2,1)S(1)} %shard_map.46), channel_id=1, source_target_pairs={{0,32},{1,9},{2,34},{3,11},{4,36},{5,13},{6,38},{7,15},{8,40},{9,1... | collective-permute-start | bytes 3170312 | tf_op jit(solution)/shard_map/ppermute | solution.py:263
  30.1 22.6 %collective-permute-start.16 = (s16[2064,256]{1,0:T(8,128)(2,1)S(1)}, s16[2064,256]{1,0:T(8,128)(2,1)S(1)}, u32[]{:S(2)}, u32[]{:S(2)}) collective-permute-start(s16[2064,256]{1,0:T(8,128)(2,1)S(1)} %shard_map.49), channel_id=1, source_target_pairs={{0,96},{1,25},{2,98},{3,27},{4,100},{5,29},{6,102},{7,31},{8,104},... | collective-permute-start | bytes 3170312 | tf_op jit(solution)/shard_map/ppermute | solution.py:263
  34.1 27.8 %collective-permute-start.4 = (s16[2064,256]{1,0:T(8,128)(2,1)S(1)}, s16[2064,256]{1,0:T(8,128)(2,1)S(1)}, u32[]{:S(2)}, u32[]{:S(2)}) collective-permute-start(s16[2064,256]{1,0:T(8,128)(2,1)S(1)} %shard_map.41), channel_id=1, source_target_pairs={{0,24},{1,97},{2,26},{3,99},{4,28},{5,101},{6,30},{7,103},{8,0},{9... | collective-permute-start | bytes 3170312 | tf_op jit(solution)/shard_map/ppermute | solution.py:263
  38.2 2.2 %copy-start.1 = (bf16[4,125,4000]{2,1,0:T(8,128)(2,1)S(1)}, bf16[4,125,4000]{2,1,0:T(8,128)(2,1)}, u32[]{:S(2)}) copy-start(bf16[4,125,4000]{2,1,0:T(8,128)(2,1)} %slice.8.rest_0_.rest_1_.rest_2_.rest_3_.rest_4_.rest_5_.rest_6_.rest_7_.rest_8_.rest_9_.rest_10_.rest_11_.rest_18_.rest_19_.rest_20_.rest_27_.rest_28_.rest_29_.rest_12_.rest_13_) | copy-start | bytes 12000004
  39.8 25.7 %collective-permute-start.1 = (s16[2064,256]{1,0:T(8,128)(2,1)S(1)}, s16[2064,256]{1,0:T(8,128)(2,1)S(1)}, u32[]{:S(2)}, u32[]{:S(2)}) collective-permute-start(s16[2064,256]{1,0:T(8,128)(2,1)S(1)} %shard_map.38), channel_id=1, source_target_pairs={{0,8},{1,33},{2,10},{3,35},{4,12},{5,37},{6,14},{7,39},{8,16},{9,4... | collective-permute-start | bytes 3170312 | tf_op jit(solution)/shard_map/ppermute | solution.py:263
  42.3 29.7 %collective-permute-start.12 = (s16[2064,256]{1,0:T(8,128)(2,1)S(1)}, s16[2064,256]{1,0:T(8,128)(2,1)S(1)}, u32[]{:S(2)}, u32[]{:S(2)}) collective-permute-start(s16[2064,256]{1,0:T(8,128)(2,1)S(1)} %shard_map.45), channel_id=1, source_target_pairs={{0,96},{1,25},{2,98},{3,27},{4,100},{5,29},{6,102},{7,31},{8,104},... | collective-permute-start | bytes 3170312 | tf_op jit(solution)/shard_map/ppermute | solution.py:263
  46.0 29.5 %collective-permute-start.15 = (s16[2064,256]{1,0:T(8,128)(2,1)S(1)}, s16[2064,256]{1,0:T(8,128)(2,1)S(1)}, u32[]{:S(2)}, u32[]{:S(2)}) collective-permute-start(s16[2064,256]{1,0:T(8,128)(2,1)S(1)} %shard_map.48), channel_id=1, source_target_pairs={{0,32},{1,9},{2,34},{3,11},{4,36},{5,13},{6,38},{7,15},{8,40},{9,1... | collective-permute-start | bytes 3170312 | tf_op jit(solution)/shard_map/ppermute | solution.py:263
  52.8 32.9 %collective-permute-start.14 = (s16[2064,256]{1,0:T(8,128)(2,1)S(1)}, s16[2064,256]{1,0:T(8,128)(2,1)S(1)}, u32[]{:S(2)}, u32[]{:S(2)}) collective-permute-start(s16[2064,256]{1,0:T(8,128)(2,1)S(1)} %shard_map.47), channel_id=1, source_target_pairs={{0,32},{1,9},{2,34},{3,11},{4,36},{5,13},{6,38},{7,15},{8,40},{9,1... | collective-permute-start | bytes 3170312 | tf_op jit(solution)/shard_map/ppermute | solution.py:263
  61.9 27.4 %collective-permute-start.17 = (s16[2064,256]{1,0:T(8,128)(2,1)S(1)}, s16[2064,256]{1,0:T(8,128)(2,1)S(1)}, u32[]{:S(2)}, u32[]{:S(2)}) collective-permute-start(s16[2064,256]{1,0:T(8,128)(2,1)S(1)} %shard_map.50), channel_id=1, source_target_pairs={{0,96},{1,25},{2,98},{3,27},{4,100},{5,29},{6,102},{7,31},{8,104},... | collective-permute-start | bytes 3170312 | tf_op jit(solution)/shard_map/ppermute | solution.py:263
  65.4 29.3 %collective-permute-start.3 = (s16[2064,256]{1,0:T(8,128)(2,1)S(1)}, s16[2064,256]{1,0:T(8,128)(2,1)S(1)}, u32[]{:S(2)}, u32[]{:S(2)}) collective-permute-start(s16[2064,256]{1,0:T(8,128)(2,1)S(1)} %shard_map.40), channel_id=1, source_target_pairs={{0,8},{1,33},{2,10},{3,35},{4,12},{5,37},{6,14},{7,39},{8,16},{9,4... | collective-permute-start | bytes 3170312 | tf_op jit(solution)/shard_map/ppermute | solution.py:263
  72.0 24.0 %collective-permute-start = (s16[2064,256]{1,0:T(8,128)(2,1)S(1)}, s16[2064,256]{1,0:T(8,128)(2,1)S(1)}, u32[]{:S(2)}, u32[]{:S(2)}) collective-permute-start(s16[2064,256]{1,0:T(8,128)(2,1)S(1)} %shard_map.37), channel_id=1, source_target_pairs={{0,24},{1,97},{2,26},{3,99},{4,28},{5,101},{6,30},{7,103},{8,0},{9... | collective-permute-start | bytes 3170312 | tf_op jit(solution)/shard_map/ppermute | solution.py:263
  75.4 25.7 %collective-permute-start.5 = (s16[2064,256]{1,0:T(8,128)(2,1)S(1)}, s16[2064,256]{1,0:T(8,128)(2,1)S(1)}, u32[]{:S(2)}, u32[]{:S(2)}) collective-permute-start(s16[2064,256]{1,0:T(8,128)(2,1)S(1)} %shard_map.42), channel_id=1, source_target_pairs={{0,24},{1,97},{2,26},{3,99},{4,28},{5,101},{6,30},{7,103},{8,0},{9... | collective-permute-start | bytes 3170312 | tf_op jit(solution)/shard_map/ppermute | solution.py:263
  85.7 20.6 %collective-permute-start.2 = (s16[2064,256]{1,0:T(8,128)(2,1)S(1)}, s16[2064,256]{1,0:T(8,128)(2,1)S(1)}, u32[]{:S(2)}, u32[]{:S(2)}) collective-permute-start(s16[2064,256]{1,0:T(8,128)(2,1)S(1)} %shard_map.39), channel_id=1, source_target_pairs={{0,8},{1,33},{2,10},{3,35},{4,12},{5,37},{6,14},{7,39},{8,16},{9,4... | collective-permute-start | bytes 3170312 | tf_op jit(solution)/shard_map/ppermute | solution.py:263
  91.5 22.4 %collective-permute-start.19 = (s16[528,256]{1,0:T(8,128)(2,1)S(1)}, s16[528,256]{1,0:T(8,128)(2,1)S(1)}, u32[]{:S(2)}, u32[]{:S(2)}) collective-permute-start(s16[528,256]{1,0:T(8,128)(2,1)S(1)} %get-tuple-element.28), channel_id=1, source_target_pairs={{0,8},{1,33},{2,10},{3,35},{4,12},{5,37},{6,14},{7,39},{8,16},{9,4... | collective-permute-start | bytes 811016 | tf_op jit(solution)/shard_map/ppermute | solution.py:263
  94.8 19.1 %collective-permute-start.20 = (s16[528,256]{1,0:T(8,128)(2,1)S(1)}, s16[528,256]{1,0:T(8,128)(2,1)S(1)}, u32[]{:S(2)}, u32[]{:S(2)}) collective-permute-start(s16[528,256]{1,0:T(8,128)(2,1)S(1)} %get-tuple-element.29), channel_id=1, source_target_pairs={{0,24},{1,97},{2,26},{3,99},{4,28},{5,101},{6,30},{7,103},{8,0},{9... | collective-permute-start | bytes 811016 | tf_op jit(solution)/shard_map/ppermute | solution.py:263
  108.5 9.5 %collective-permute-start.7 = (s16[528,256]{1,0:T(8,128)(2,1)S(1)}, s16[528,256]{1,0:T(8,128)(2,1)S(1)}, u32[]{:S(2)}, u32[]{:S(2)}) collective-permute-start(s16[528,256]{1,0:T(8,128)(2,1)S(1)} %get-tuple-element.21), channel_id=1, source_target_pairs={{0,32},{1,9},{2,34},{3,11},{4,36},{5,13},{6,38},{7,15},{8,40},{9,1... | collective-permute-start | bytes 811016 | tf_op jit(solution)/shard_map/ppermute | solution.py:263
  109.9 9.3 %collective-permute-start.8 = (s16[528,256]{1,0:T(8,128)(2,1)S(1)}, s16[528,256]{1,0:T(8,128)(2,1)S(1)}, u32[]{:S(2)}, u32[]{:S(2)}) collective-permute-start(s16[528,256]{1,0:T(8,128)(2,1)S(1)} %get-tuple-element.22), channel_id=1, source_target_pairs={{0,96},{1,25},{2,98},{3,27},{4,100},{5,29},{6,102},{7,31},{8,104},... | collective-permute-start | bytes 811016 | tf_op jit(solution)/shard_map/ppermute | solution.py:263
  111.8 11.1 %collective-permute-start.18 = (s16[528,256]{1,0:T(8,128)(2,1)S(1)}, s16[528,256]{1,0:T(8,128)(2,1)S(1)}, u32[]{:S(2)}, u32[]{:S(2)}) collective-permute-start(s16[528,256]{1,0:T(8,128)(2,1)S(1)} %get-tuple-element.27), channel_id=1, source_target_pairs={{0,24},{1,97},{2,26},{3,99},{4,28},{5,101},{6,30},{7,103},{8,0},{9... | collective-permute-start | bytes 811016 | tf_op jit(solution)/shard_map/ppermute | solution.py:263
  113.8 11.5 %collective-permute-start.22 = (s16[528,256]{1,0:T(8,128)(2,1)S(1)}, s16[528,256]{1,0:T(8,128)(2,1)S(1)}, u32[]{:S(2)}, u32[]{:S(2)}) collective-permute-start(s16[528,256]{1,0:T(8,128)(2,1)S(1)} %get-tuple-element.31), channel_id=1, source_target_pairs={{0,8},{1,33},{2,10},{3,35},{4,12},{5,37},{6,14},{7,39},{8,16},{9,4... | collective-permute-start | bytes 811016 | tf_op jit(solution)/shard_map/ppermute | solution.py:263
  115.4 9.9 %collective-permute-start.21 = (s16[528,256]{1,0:T(8,128)(2,1)S(1)}, s16[528,256]{1,0:T(8,128)(2,1)S(1)}, u32[]{:S(2)}, u32[]{:S(2)}) collective-permute-start(s16[528,256]{1,0:T(8,128)(2,1)S(1)} %get-tuple-element.30), channel_id=1, source_target_pairs={{0,8},{1,33},{2,10},{3,35},{4,12},{5,37},{6,14},{7,39},{8,16},{9,4... | collective-permute-start | bytes 811016 | tf_op jit(solution)/shard_map/ppermute | solution.py:263
  118.0 13.3 %collective-permute-start.10 = (s16[528,256]{1,0:T(8,128)(2,1)S(1)}, s16[528,256]{1,0:T(8,128)(2,1)S(1)}, u32[]{:S(2)}, u32[]{:S(2)}) collective-permute-start(s16[528,256]{1,0:T(8,128)(2,1)S(1)} %get-tuple-element.24), channel_id=1, source_target_pairs={{0,32},{1,9},{2,34},{3,11},{4,36},{5,13},{6,38},{7,15},{8,40},{9,1... | collective-permute-start | bytes 811016 | tf_op jit(solution)/shard_map/ppermute | solution.py:263
  119.1 12.2 %collective-permute-start.6 = (s16[528,256]{1,0:T(8,128)(2,1)S(1)}, s16[528,256]{1,0:T(8,128)(2,1)S(1)}, u32[]{:S(2)}, u32[]{:S(2)}) collective-permute-start(s16[528,256]{1,0:T(8,128)(2,1)S(1)} %get-tuple-element.20), channel_id=1, source_target_pairs={{0,96},{1,25},{2,98},{3,27},{4,100},{5,29},{6,102},{7,31},{8,104},... | collective-permute-start | bytes 811016 | tf_op jit(solution)/shard_map/ppermute | solution.py:263
  122.9 6.5 %collective-permute-start.23 = (s16[528,256]{1,0:T(8,128)(2,1)S(1)}, s16[528,256]{1,0:T(8,128)(2,1)S(1)}, u32[]{:S(2)}, u32[]{:S(2)}) collective-permute-start(s16[528,256]{1,0:T(8,128)(2,1)S(1)} %get-tuple-element.32), channel_id=1, source_target_pairs={{0,24},{1,97},{2,26},{3,99},{4,28},{5,101},{6,30},{7,103},{8,0},{9... | collective-permute-start | bytes 811016 | tf_op jit(solution)/shard_map/ppermute | solution.py:263
  125.3 6.5 %collective-permute-start.11 = (s16[528,256]{1,0:T(8,128)(2,1)S(1)}, s16[528,256]{1,0:T(8,128)(2,1)S(1)}, u32[]{:S(2)}, u32[]{:S(2)}) collective-permute-start(s16[528,256]{1,0:T(8,128)(2,1)S(1)} %get-tuple-element.25), channel_id=1, source_target_pairs={{0,96},{1,25},{2,98},{3,27},{4,100},{5,29},{6,102},{7,31},{8,104},... | collective-permute-start | bytes 811016 | tf_op jit(solution)/shard_map/ppermute | solution.py:263
  125.3 7.9 %collective-permute-start.9 = (s16[528,256]{1,0:T(8,128)(2,1)S(1)}, s16[528,256]{1,0:T(8,128)(2,1)S(1)}, u32[]{:S(2)}, u32[]{:S(2)}) collective-permute-start(s16[528,256]{1,0:T(8,128)(2,1)S(1)} %get-tuple-element.23), channel_id=1, source_target_pairs={{0,32},{1,9},{2,34},{3,11},{4,36},{5,13},{6,38},{7,15},{8,40},{9,1... | collective-permute-start | bytes 811016 | tf_op jit(solution)/shard_map/ppermute | solution.py:263
